TPU v7x, 256 devices: a whole 4x4x8 slice. The times are simulated.
256 devices in a mesh: gx: 8 (over x, y_hi), gy: 32 (over y_lo, z, core).
Axes of the slice: x: 4, y: 4 (y_hi: 2, y_lo: 2; y = y_hi * 2 + y_lo), z: 8, core: 2. Of those that a mesh axis runs over, the one named last changes fastest.
Arguments:
- noise: float32 [16, 64, 4, 128], P('gx', 'gy'), may hold values from -4 to 4
- w_first: bfloat16 [16, 1, 3, 3, 3, 3], replicated, may hold values from -0.625 to 0.625
- b_first: float32 [16], replicated, may hold values from -2 to 2
- w_middle: bfloat16 [16, 16, 3, 3, 3, 3], replicated, may hold values from -0.15625 to 0.15625
- b_middle: float32 [16], replicated, may hold values from -2 to 2
- w_last: bfloat16 [2, 16, 3, 3, 3, 3], replicated, may hold values from -0.15625 to 0.15625
- b_last: float32 [2], replicated, may hold values from -2 to 2
Outputs:
- field: float32 [16, 64, 4, 128], P('gx', 'gy')
- noise_grad: float32 [16, 64, 4, 128], P('gx', 'gy')
- loss: float32 [], replicated
- w_first_grad: float32 [16, 1, 3, 3, 3, 3], replicated
- b_first_grad: float32 [16], replicated
- w_middle_grad: float32 [16, 16, 3, 3, 3, 3], replicated
- b_middle_grad: float32 [16], replicated
- w_last_grad: float32 [2, 16, 3, 3, 3, 3], replicated
- b_last_grad: float32 [2], replicated
All inputs are finite; a program needn't handle non-finite values.
Results may differ from a plain program's by a relative error of at most 0.0074.
Values may be sent and summed in bfloat16 or wider, within the bound.
No kernel may reach another device: no remote copies, remote signals or barrier semaphores. Data moves between devices by JAX's collectives and lax.ppermute only.
A program may use at most 128 MiB of HBM per device.

v0:
```python
import jax
import jax.numpy as jnp
from jax import lax
from jax.sharding import PartitionSpec as P

HOPPING = 0.15
QUARTIC = 0.1


def padded_2(array, sides, width):
    for axis, dim in sides:
        devices, length = (lax.axis_size(axis), array.shape[dim])
        up = [(i, (i + 1) % devices) for i in range(devices)]
        down = [(j, i) for i, j in up]
        last = lax.slice_in_dim(array, length - width, length, axis=dim)
        leading = lax.slice_in_dim(array, 0, width, axis=dim)
        before = lax.ppermute(last, axis, up)
        after = lax.ppermute(leading, axis, down)
        array = jnp.concatenate([before, array, after], axis=dim)
    return array


def parity_mask(shape, offset_x, offset_y):
    index_x = jnp.arange(shape[0], dtype=jnp.int32) + offset_x
    index_y = jnp.arange(shape[1], dtype=jnp.int32) + offset_y
    index_t = jnp.arange(shape[2], dtype=jnp.int32)
    index_z = jnp.arange(shape[3], dtype=jnp.int32)
    summed = (
        index_x[:, None, None, None]
        + index_y[None, :, None, None]
        + index_t[None, None, :, None]
        + index_z[None, None, None, :]
    )
    return jnp.where(summed % 2 == 0, 1.0, 0.0).astype(jnp.float32)


def shifted_stack(padded):
    width_z = padded.shape[4] - 2
    return jnp.concatenate([padded[:, :, :, :, d : d + width_z] for d in range(3)], axis=0)


def conv_block(padded, kernel):
    width_x = padded.shape[1] - 2
    width_y = padded.shape[2] - 2
    width_t = padded.shape[3] - 2
    out_ch = kernel.shape[0]
    in_ch = kernel.shape[1]
    stacked = shifted_stack(padded)
    tap_weights = jnp.transpose(kernel, (2, 3, 4, 0, 5, 1)).reshape((3, 3, 3, out_ch, 3 * in_ch))
    summed = None
    for a in range(3):
        for b in range(3):
            for c in range(3):
                window = stacked[:, a : a + width_x, b : b + width_y, c : c + width_t]
                partial_out = jnp.einsum(
                    "ok,kxytz->oxytz",
                    tap_weights[a, b, c],
                    window,
                    preferred_element_type=jnp.float32,
                )
                summed = partial_out if summed is None else summed + partial_out
    return summed


def kernel_grad(padded, cotangent):
    width_x = cotangent.shape[1]
    width_y = cotangent.shape[2]
    width_t = cotangent.shape[3]
    out_ch = cotangent.shape[0]
    in_ch = padded.shape[0]
    stacked = shifted_stack(padded)
    pieces = []
    for a in range(3):
        for b in range(3):
            for c in range(3):
                window = stacked[:, a : a + width_x, b : b + width_y, c : c + width_t]
                pieces.append(
                    jnp.einsum(
                        "oxytz,kxytz->ok", cotangent, window, preferred_element_type=jnp.float32
                    )
                )
    gathered = jnp.stack(pieces).reshape((3, 3, 3, out_ch, 3, in_ch))
    return jnp.transpose(gathered, (3, 5, 0, 1, 2, 4))


def flip_kernel(kernel):
    return jnp.transpose(kernel[:, :, ::-1, ::-1, ::-1, ::-1], (1, 0, 2, 3, 4, 5))


def wrap_planes(field, depth):
    return jnp.pad(field, ((0, 0), (0, 0), (0, 0), (depth, depth), (depth, depth)), mode="wrap")


def channel_bias(bias):
    return bias[:, None, None, None, None]


def hidden_rims(field):
    return wrap_planes(padded_2(field, (("gx", 1), ("gy", 2)), 1), 1)


def channel_sum(cotangent):
    return jnp.sum(cotangent.astype(jnp.float32), axis=(1, 2, 3, 4))


def local(noise, w_first, b_first, w_middle, b_middle, w_last, b_last):
    sites = float(noise.size * lax.axis_size("gx") * lax.axis_size("gy"))
    frozen = parity_mask(
        noise.shape, lax.axis_index("gx") * noise.shape[0], lax.axis_index("gy") * noise.shape[1]
    )
    active = 1.0 - frozen
    inputs = (frozen * noise).astype(jnp.bfloat16)[None]
    padded_in = wrap_planes(padded_2(inputs, (("gx", 1), ("gy", 2)), 1), 1)
    hidden_one = jnp.tanh(conv_block(padded_in, w_first) + channel_bias(b_first)).astype(
        jnp.bfloat16
    )
    padded_one = hidden_rims(hidden_one)
    hidden_two = jnp.tanh(conv_block(padded_one, w_middle) + channel_bias(b_middle)).astype(
        jnp.bfloat16
    )
    padded_two = hidden_rims(hidden_two)
    head_out = conv_block(padded_two, w_last) + channel_bias(b_last)
    log_scale = jnp.tanh(head_out[0])
    offset_field = head_out[1]
    growth = jnp.exp(log_scale)
    field = frozen * noise + active * (noise * growth + offset_field)
    extended = padded_2(field, (("gx", 0), ("gy", 1)), 1)
    upward = (
        extended[2:, 1:-1] + extended[1:-1, 2:] + jnp.roll(field, -1, 2) + jnp.roll(field, -1, 3)
    )
    downward = (
        extended[:-2, 1:-1] + extended[1:-1, :-2] + jnp.roll(field, 1, 2) + jnp.roll(field, 1, 3)
    )
    squared = field * field
    density = (
        -2.0 * HOPPING * field * upward + squared + QUARTIC * (squared - 1.0) * (squared - 1.0)
    )
    local_loss = jnp.sum(-0.5 * noise * noise - active * log_scale + density)
    force_field = (
        -2.0 * HOPPING * (upward + downward) + 2.0 * field + 4.0 * QUARTIC * field * (squared - 1.0)
    )
    d_scale = active * (force_field * noise * growth - 1.0) * (1.0 - log_scale * log_scale)
    d_offset = active * force_field
    cot_last = jnp.stack([d_scale, d_offset], axis=0).astype(jnp.bfloat16)
    grad_last = kernel_grad(padded_two, cot_last)
    bias_last = channel_sum(cot_last)
    two_float = hidden_two.astype(jnp.float32)
    cot_middle = (
        conv_block(hidden_rims(cot_last), flip_kernel(w_last)) * (1.0 - two_float * two_float)
    ).astype(jnp.bfloat16)
    grad_middle = kernel_grad(padded_one, cot_middle)
    bias_middle = channel_sum(cot_middle)
    one_float = hidden_one.astype(jnp.float32)
    cot_first = (
        conv_block(hidden_rims(cot_middle), flip_kernel(w_middle)) * (1.0 - one_float * one_float)
    ).astype(jnp.bfloat16)
    grad_first = kernel_grad(padded_in, cot_first)
    bias_first = channel_sum(cot_first)
    grad_first, bias_first, grad_middle, bias_middle, grad_last, bias_last, local_loss = lax.psum(
        (grad_first, bias_first, grad_middle, bias_middle, grad_last, bias_last, local_loss),
        ("gx", "gy"),
    )
    d_inputs = conv_block(hidden_rims(cot_first), flip_kernel(w_first))
    noise_grad = frozen * d_inputs[0] + force_field * (frozen + active * growth) - noise
    return (
        field,
        noise_grad,
        local_loss / sites,
        grad_first / sites,
        bias_first / sites,
        grad_middle / sites,
        bias_middle / sites,
        grad_last / sites,
        bias_last / sites,
    )


def solution(mesh):
    placed = (P("gx", "gy", None, None), P(), P(), P(), P(), P(), P())
    return jax.shard_map(
        local,
        mesh=mesh,
        in_specs=placed,
        out_specs=(
            P("gx", "gy", None, None),
            P("gx", "gy", None, None),
            P(),
            P(),
            P(),
            P(),
            P(),
            P(),
            P(),
        ),
        check_vma=False,
    )
```

profile of v0, /device:TPU:1, one launch (start us, length us, event | category | flops | bytes accessed | tf_op | source)
XLA Modules:
  0.0 499.7 jit_solution(6943930336084102894)
XLA Ops:
  7.4 0.8 fusion.432
  8.2 3.8 collective-permute-start
  12.0 2.3 collective-permute-start.1
  14.3 0.9 collective-permute-done
  15.2 0.8 collective-permute-done.1
  16.0 3.7 collective-permute-start.2
  19.8 0.8 reverse_bitcast_fusion
  20.6 1.0 rev.10
  21.6 1.2 copy.1000
  29.8 2.0 collective-permute-start.4
  31.8 3.2 collective-permute-start.5
  35.0 0.7 fusion.621
  35.7 0.7 collective-permute-done.4
  36.4 3.2 collective-permute-start.6
  39.6 2.1 collective-permute-start.7
  41.7 0.7 fusion.622
  42.4 0.9 collective-permute-done.7
  48.5 2.9 collective-permute-start.8
  51.4 2.5 collective-permute-start.9
  53.9 1.6 fusion.607
  55.7 1.5 collective-permute-start.10
  57.2 3.7 collective-permute-start.11
  67.2 0.6 fusion.609
  67.8 5.2 %collective-permute-start.12 = (f32[1,2,4,128]{3,2,1,0:T(4,128)S(1)}, f32[1,2,4,128]{3,2,1,0:T(4,128)S(1)}, u32[]{:S(2)}, u32[]{:S(2)}) collective-permute-start(f32[1,2,4,128]{3,2,1,0:T(4,128)S(1)} %get-tuple-element.236), channel_id=1, source_target_pairs={{32,0},{64,32},{96,64},{128,96},{160,128},{192,160},{224,192},{0,2... | collective-permute-start | bytes 12296 | tf_op jit(solution)/shard_map/ppermute | solution.py:18
  73.1 0.7 collective-permute-done.12
  73.8 5.3 %collective-permute-done.13 = f32[1,2,4,128]{3,2,1,0:T(4,128)S(1)} collective-permute-done((f32[1,2,4,128]{3,2,1,0:T(4,128)S(1)}, f32[1,2,4,128]{3,2,1,0:T(4,128)S(1)}, u32[]{:S(2)}, u32[]{:S(2)}) %collective-permute-start.13) | collective-permute-done | bytes 4128 | tf_op jit(solution)/shard_map/ppermute | solution.py:17
  79.1 6.3 %collective-permute-start.14 = (f32[4,1,4,128]{3,2,1,0:T(4,128)S(1)}, f32[4,1,4,128]{3,2,1,0:T(4,128)S(1)}, u32[]{:S(2)}, u32[]{:S(2)}) collective-permute-start(f32[4,1,4,128]{3,2,1,0:T(4,128)S(1)} %get-tuple-element.218), channel_id=1, source_target_pairs={{1,0},{2,1},{3,2},{4,3},{5,4},{6,5},{7,6},{8,7},{9,8},{10,9},{11,1... | collective-permute-start | bytes 24584 | tf_op jit(solution)/shard_map/ppermute | solution.py:18
  85.4 0.8 collective-permute-done.14
  86.2 0.7 fusion.411
  86.9 1.0 collective-permute-done.15
  88.2 5.1 %collective-permute-start.17 = (bf16[2,1,2,4,128]{4,3,2,1,0:T(4,128)(2,1)S(1)}, bf16[2,1,2,4,128]{4,3,2,1,0:T(4,128)(2,1)S(1)}, u32[]{:S(2)}, u32[]{:S(2)}) collective-permute-start(bf16[2,1,2,4,128]{4,3,2,1,0:T(4,128)(2,1)S(1)} %get-tuple-element.226), channel_id=1, source_target_pairs={{32,0},{64,32},{96,64},{128,96},{160,128},{192,160},{224,192},{0,2... | collective-permute-start | bytes 12296 | tf_op jit(solution)/shard_map/ppermute | solution.py:18
  98.2 10.1 %collective-permute-start.18 = (bf16[2,4,1,4,128]{4,3,2,1,0:T(4,128)(2,1)S(1)}, bf16[2,4,1,4,128]{4,3,2,1,0:T(4,128)(2,1)S(1)}, u32[]{:S(2)}, u32[]{:S(2)}) collective-permute-start(bf16[2,4,1,4,128]{4,3,2,1,0:T(4,128)(2,1)S(1)} %get-tuple-element.215), channel_id=1, source_target_pairs={{0,1},{1,2},{2,3},{3,4},{4,5},{5,6},{6,7},{7,8},{8,9},{9,10},{10,1... | collective-permute-start | bytes 24584 | tf_op jit(solution)/shard_map/ppermute | solution.py:17
  108.3 4.0 collective-permute-start.19
  119.9 5.1 %collective-permute-start.21 = (bf16[16,1,2,4,128]{4,0,3,2,1:T(8,128)(2,1)S(1)}, bf16[16,1,2,4,128]{4,0,3,2,1:T(8,128)(2,1)S(1)}, u32[]{:S(2)}, u32[]{:S(2)}) collective-permute-start(bf16[16,1,2,4,128]{4,0,3,2,1:T(8,128)(2,1)S(1)} %get-tuple-element.199), channel_id=1, source_target_pairs={{32,0},{64,32},{96,64},{128,96},{160,128},{192,160},{224,192},{0,2... | collective-permute-start | bytes 98312 | tf_op jit(solution)/shard_map/ppermute | solution.py:18
  129.6 1.3 reshape.292
  131.1 4.9 collective-permute-start.23
  136.0 246.7 %all-reduce.3.cloned.1.call-done = f32[16,16,3,3,3,3]{1,5,0,4,3,2:T(4,128)} async-done(((f32[16,16,3,3,3,3]{1,5,0,4,3,2:T(4,128)}), f32[16,16,3,3,3,3]{1,5,0,4,3,2:T(4,128)}) %all-reduce.3.cloned.1.call-update) | async-done | bytes 82960 | tf_op jit(solution)/shard_map/psum | solution.py:159
  382.7 1.4 broadcast_multiply_fusion
  384.1 0.9 copy.1222
  395.6 78.0 %all-reduce = (f32[]{:T(128)}, f32[16,1,3,3,3,3]{0,4,3,2,5,1:T(4,128)S(1)}, f32[16]{0:T(128)S(1)}, f32[16]{0:T(128)S(1)}, f32[2,16,3,3,3,3]{1,5,0,4,3,2:T(4,128)S(1)}, /*index=5*/f32[2]{0:T(128)S(1)}) all-reduce(f32[]{:T(128)} %get-tuple-element.53, ...), channel_id=1, replica_groups=mesh['gx'=8,'gy'=32] {'gx','gy'}, use_global_device_ids=true, to_apply=%region_1.2 | all-reduce | flops 3923 | bytes 31384 | tf_op jit(solution)/shard_map/psum | solution.py:159
  474.2 1.3 collective-permute-start.24
  475.5 4.0 collective-permute-start.25
  480.0 0.8 collective-permute-done.24
  480.8 1.7 collective-permute-start.26
  483.4 0.7 copy.1223
  484.1 0.7 copy.1221
  485.4 0.8 collective-permute-done.27
  490.8 0.7 fusion.418
  (435 shorter events, 53.1 us)
Async XLA Ops:
  7.2 15.8 %copy-start.17 = (bf16[2,16,3,3,3,3]{1,0,5,4,3,2:T(2,128)(2,1)S(1)}, bf16[2,16,3,3,3,3]{1,0,5,4,3,2:T(2,128)(2,1)}, u32[]{:S(2)}) copy-start(bf16[2,16,3,3,3,3]{1,0,5,4,3,2:T(2,128)(2,1)} %param.12) | copy-start | bytes 15556
  7.2 375.5 %all-reduce.3.cloned.1.call-start = ((), (), s32[]{:S(2)}) async-start(), calls=%async_computation | async-start | bytes 1769472 | tf_op jit(solution)/shard_map/psum | solution.py:159
  8.2 7.0 %collective-permute-start = (bf16[1,1,2,4,128]{4,0,3,2,1:T(2,128)(2,1)S(1)}, bf16[1,1,2,4,128]{4,0,3,2,1:T(2,128)(2,1)S(1)}, u32[]{:S(2)}, u32[]{:S(2)}) collective-permute-start(bf16[1,1,2,4,128]{4,0,3,2,1:T(2,128)(2,1)S(1)} %copy.1904), channel_id=1, source_target_pairs={{0,32},{32,64},{64,96},{96,128},{128,160},{160,192},{192,224},{224... | collective-permute-start | bytes 6152 | tf_op jit(solution)/shard_map/ppermute | solution.py:17
  12.0 4.0 collective-permute-start.1
  16.0 7.2 %copy-start.18 = (bf16[16,1,3,3,3,3]{0,5,4,3,2,1:T(4,128)(2,1)S(1)}, bf16[16,1,3,3,3,3]{0,5,4,3,2,1:T(4,128)(2,1)}, u32[]{:S(2)}) copy-start(bf16[16,1,3,3,3,3]{0,5,4,3,2,1:T(4,128)(2,1)} %param.8) | copy-start | bytes 7780
  16.0 7.3 %collective-permute-start.2 = (bf16[1,4,1,4,128]{4,0,3,2,1:T(2,128)(2,1)S(1)}, bf16[1,4,1,4,128]{4,0,3,2,1:T(2,128)(2,1)S(1)}, u32[]{:S(2)}, u32[]{:S(2)}) collective-permute-start(bf16[1,4,1,4,128]{4,0,3,2,1:T(2,128)(2,1)S(1)} %get-tuple-element.221), channel_id=1, source_target_pairs={{0,1},{1,2},{2,3},{3,4},{4,5},{5,6},{6,7},{7,8},{8,9},{9,10},{10,1... | collective-permute-start | bytes 12296 | tf_op jit(solution)/shard_map/ppermute | solution.py:17
  19.7 3.6 collective-permute-start.3
  29.8 6.6 %collective-permute-start.4 = (bf16[16,1,2,4,128]{4,0,3,2,1:T(8,128)(2,1)S(1)}, bf16[16,1,2,4,128]{4,0,3,2,1:T(8,128)(2,1)S(1)}, u32[]{:S(2)}, u32[]{:S(2)}) collective-permute-start(bf16[16,1,2,4,128]{4,0,3,2,1:T(8,128)(2,1)S(1)} %get-tuple-element.206), channel_id=1, source_target_pairs={{0,32},{32,64},{64,96},{96,128},{128,160},{160,192},{192,224},{224... | collective-permute-start | bytes 98312 | tf_op jit(solution)/shard_map/ppermute | solution.py:17
  31.8 4.6 collective-permute-start.5
  36.4 6.0 %collective-permute-start.6 = (bf16[16,4,1,4,128]{4,0,3,2,1:T(8,128)(2,1)S(1)}, bf16[16,4,1,4,128]{4,0,3,2,1:T(8,128)(2,1)S(1)}, u32[]{:S(2)}, u32[]{:S(2)}) collective-permute-start(bf16[16,4,1,4,128]{4,0,3,2,1:T(8,128)(2,1)S(1)} %get-tuple-element.168), channel_id=1, source_target_pairs={{0,1},{1,2},{2,3},{3,4},{4,5},{5,6},{6,7},{7,8},{8,9},{9,10},{10,1... | collective-permute-start | bytes 196616 | tf_op jit(solution)/shard_map/ppermute | solution.py:17
  39.6 3.7 collective-permute-start.7
  48.5 7.0 %collective-permute-start.8 = (bf16[16,1,2,4,128]{4,0,3,2,1:T(8,128)(2,1)S(1)}, bf16[16,1,2,4,128]{4,0,3,2,1:T(8,128)(2,1)S(1)}, u32[]{:S(2)}, u32[]{:S(2)}) collective-permute-start(bf16[16,1,2,4,128]{4,0,3,2,1:T(8,128)(2,1)S(1)} %get-tuple-element.204), channel_id=1, source_target_pairs={{0,32},{32,64},{64,96},{96,128},{128,160},{160,192},{192,224},{224... | collective-permute-start | bytes 98312 | tf_op jit(solution)/shard_map/ppermute | solution.py:17
  51.4 4.3 collective-permute-start.9
  55.7 5.8 %collective-permute-start.10 = (bf16[16,4,1,4,128]{4,0,3,2,1:T(8,128)(2,1)S(1)}, bf16[16,4,1,4,128]{4,0,3,2,1:T(8,128)(2,1)S(1)}, u32[]{:S(2)}, u32[]{:S(2)}) collective-permute-start(bf16[16,4,1,4,128]{4,0,3,2,1:T(8,128)(2,1)S(1)} %get-tuple-element.166), channel_id=1, source_target_pairs={{0,1},{1,2},{2,3},{3,4},{4,5},{5,6},{6,7},{7,8},{8,9},{9,10},{10,1... | collective-permute-start | bytes 196616 | tf_op jit(solution)/shard_map/ppermute | solution.py:17
  57.2 4.6 collective-permute-start.11
  66.8 21.1 %copy-start = (f32[2,2,4,128]{3,2,1,0:T(4,128)}, f32[2,2,4,128]{3,2,1,0:T(4,128)S(1)}, u32[]{:S(2)}) copy-start(f32[2,2,4,128]{3,2,1,0:T(4,128)S(1)} %fusion.413) | copy-start | bytes 24580
  67.8 6.0 %collective-permute-start.12 = (f32[1,2,4,128]{3,2,1,0:T(4,128)S(1)}, f32[1,2,4,128]{3,2,1,0:T(4,128)S(1)}, u32[]{:S(2)}, u32[]{:S(2)}) collective-permute-start(f32[1,2,4,128]{3,2,1,0:T(4,128)S(1)} %get-tuple-element.236), channel_id=1, source_target_pairs={{32,0},{64,32},{96,64},{128,96},{160,128},{192,160},{224,192},{0,2... | collective-permute-start | bytes 12296 | tf_op jit(solution)/shard_map/ppermute | solution.py:18
  73.0 6.1 %collective-permute-start.13 = (f32[1,2,4,128]{3,2,1,0:T(4,128)S(1)}, f32[1,2,4,128]{3,2,1,0:T(4,128)S(1)}, u32[]{:S(2)}, u32[]{:S(2)}) collective-permute-start(f32[1,2,4,128]{3,2,1,0:T(4,128)S(1)} %get-tuple-element.235), channel_id=1, source_target_pairs={{0,32},{32,64},{64,96},{96,128},{128,160},{160,192},{192,224},{224... | collective-permute-start | bytes 12296 | tf_op jit(solution)/shard_map/ppermute | solution.py:17
  79.1 7.1 %collective-permute-start.14 = (f32[4,1,4,128]{3,2,1,0:T(4,128)S(1)}, f32[4,1,4,128]{3,2,1,0:T(4,128)S(1)}, u32[]{:S(2)}, u32[]{:S(2)}) collective-permute-start(f32[4,1,4,128]{3,2,1,0:T(4,128)S(1)} %get-tuple-element.218), channel_id=1, source_target_pairs={{1,0},{2,1},{3,2},{4,3},{5,4},{6,5},{7,6},{8,7},{9,8},{10,9},{11,1... | collective-permute-start | bytes 24584 | tf_op jit(solution)/shard_map/ppermute | solution.py:18
  85.4 2.5 collective-permute-start.15
  88.2 9.9 %collective-permute-start.16 = (bf16[2,1,2,4,128]{4,3,2,1,0:T(4,128)(2,1)S(1)}, bf16[2,1,2,4,128]{4,3,2,1,0:T(4,128)(2,1)S(1)}, u32[]{:S(2)}, u32[]{:S(2)}) collective-permute-start(bf16[2,1,2,4,128]{4,3,2,1,0:T(4,128)(2,1)S(1)} %get-tuple-element.225), channel_id=1, source_target_pairs={{0,32},{32,64},{64,96},{96,128},{128,160},{160,192},{192,224},{224... | collective-permute-start | bytes 12296 | tf_op jit(solution)/shard_map/ppermute | solution.py:17
  88.2 9.9 %collective-permute-start.17 = (bf16[2,1,2,4,128]{4,3,2,1,0:T(4,128)(2,1)S(1)}, bf16[2,1,2,4,128]{4,3,2,1,0:T(4,128)(2,1)S(1)}, u32[]{:S(2)}, u32[]{:S(2)}) collective-permute-start(bf16[2,1,2,4,128]{4,3,2,1,0:T(4,128)(2,1)S(1)} %get-tuple-element.226), channel_id=1, source_target_pairs={{32,0},{64,32},{96,64},{128,96},{160,128},{192,160},{224,192},{0,2... | collective-permute-start | bytes 12296 | tf_op jit(solution)/shard_map/ppermute | solution.py:18
  98.2 14.7 %collective-permute-start.18 = (bf16[2,4,1,4,128]{4,3,2,1,0:T(4,128)(2,1)S(1)}, bf16[2,4,1,4,128]{4,3,2,1,0:T(4,128)(2,1)S(1)}, u32[]{:S(2)}, u32[]{:S(2)}) collective-permute-start(bf16[2,4,1,4,128]{4,3,2,1,0:T(4,128)(2,1)S(1)} %get-tuple-element.215), channel_id=1, source_target_pairs={{0,1},{1,2},{2,3},{3,4},{4,5},{5,6},{6,7},{7,8},{8,9},{9,10},{10,1... | collective-permute-start | bytes 24584 | tf_op jit(solution)/shard_map/ppermute | solution.py:17
  108.3 4.8 collective-permute-start.19
  119.8 6.5 %copy-start.16 = (bf16[48,2,2,4,128]{4,0,3,2,1:T(8,128)(2,1)S(1)}, bf16[48,2,2,4,128]{4,0,3,2,1:T(8,128)(2,1)}, u32[]{:S(2)}) copy-start(bf16[48,2,2,4,128]{4,0,3,2,1:T(8,128)(2,1)} %get-tuple-element.75) | copy-start | bytes 589828
  119.9 11.0 %collective-permute-start.20 = (bf16[16,1,2,4,128]{4,0,3,2,1:T(8,128)(2,1)S(1)}, bf16[16,1,2,4,128]{4,0,3,2,1:T(8,128)(2,1)S(1)}, u32[]{:S(2)}, u32[]{:S(2)}) collective-permute-start(bf16[16,1,2,4,128]{4,0,3,2,1:T(8,128)(2,1)S(1)} %get-tuple-element.200), channel_id=1, source_target_pairs={{0,32},{32,64},{64,96},{96,128},{128,160},{160,192},{192,224},{224... | collective-permute-start | bytes 98312 | tf_op jit(solution)/shard_map/ppermute | solution.py:17
  119.9 11.0 %collective-permute-start.21 = (bf16[16,1,2,4,128]{4,0,3,2,1:T(8,128)(2,1)S(1)}, bf16[16,1,2,4,128]{4,0,3,2,1:T(8,128)(2,1)S(1)}, u32[]{:S(2)}, u32[]{:S(2)}) collective-permute-start(bf16[16,1,2,4,128]{4,0,3,2,1:T(8,128)(2,1)S(1)} %get-tuple-element.199), channel_id=1, source_target_pairs={{32,0},{64,32},{96,64},{128,96},{160,128},{192,160},{224,192},{0,2... | collective-permute-start | bytes 98312 | tf_op jit(solution)/shard_map/ppermute | solution.py:18
  125.7 1.4 copy-start.11
  125.9 1.4 copy-start.10
  126.1 1.4 copy-start.9
  131.0 254.0 %collective-permute-start.22 = (bf16[16,4,1,4,128]{4,0,3,2,1:T(8,128)(2,1)S(1)}, bf16[16,4,1,4,128]{4,0,3,2,1:T(8,128)(2,1)S(1)}, u32[]{:S(2)}, u32[]{:S(2)}) collective-permute-start(bf16[16,4,1,4,128]{4,0,3,2,1:T(8,128)(2,1)S(1)} %get-tuple-element.164), channel_id=1, source_target_pairs={{0,1},{1,2},{2,3},{3,4},{4,5},{5,6},{6,7},{7,8},{8,9},{9,10},{10,1... | collective-permute-start | bytes 196616 | tf_op jit(solution)/shard_map/ppermute | solution.py:17
  131.1 253.9 %collective-permute-start.23 = (bf16[16,4,1,4,128]{4,0,3,2,1:T(8,128)(2,1)S(1)}, bf16[16,4,1,4,128]{4,0,3,2,1:T(8,128)(2,1)S(1)}, u32[]{:S(2)}, u32[]{:S(2)}) collective-permute-start(bf16[16,4,1,4,128]{4,0,3,2,1:T(8,128)(2,1)S(1)} %get-tuple-element.165), channel_id=1, source_target_pairs={{1,0},{2,1},{3,2},{4,3},{5,4},{6,5},{7,6},{8,7},{9,8},{10,9},{11,1... | collective-permute-start | bytes 196616 | tf_op jit(solution)/shard_map/ppermute | solution.py:18
  391.1 1.5 copy-start.30
  391.1 1.7 copy-start.29
  391.1 1.8 copy-start.28
  391.6 1.4 copy-start.27
  391.6 1.6 copy-start.26
  391.6 1.7 copy-start.25
  391.6 1.9 copy-start.24
  391.6 2.0 copy-start.23
  391.6 2.1 copy-start.22
  391.6 2.3 copy-start.21
  391.6 2.4 copy-start.20
  391.7 2.5 copy-start.19
  474.2 6.6 %collective-permute-start.24 = (bf16[16,1,2,4,128]{4,0,3,2,1:T(8,128)(2,1)S(1)}, bf16[16,1,2,4,128]{4,0,3,2,1:T(8,128)(2,1)S(1)}, u32[]{:S(2)}, u32[]{:S(2)}) collective-permute-start(bf16[16,1,2,4,128]{4,0,3,2,1:T(8,128)(2,1)S(1)} %get-tuple-element.198), channel_id=1, source_target_pairs={{0,32},{32,64},{64,96},{96,128},{128,160},{160,192},{192,224},{224... | collective-permute-start | bytes 98312 | tf_op jit(solution)/shard_map/ppermute | solution.py:17
  475.5 5.3 %collective-permute-start.25 = (bf16[16,1,2,4,128]{4,0,3,2,1:T(8,128)(2,1)S(1)}, bf16[16,1,2,4,128]{4,0,3,2,1:T(8,128)(2,1)S(1)}, u32[]{:S(2)}, u32[]{:S(2)}) collective-permute-start(bf16[16,1,2,4,128]{4,0,3,2,1:T(8,128)(2,1)S(1)} %get-tuple-element.197), channel_id=1, source_target_pairs={{32,0},{64,32},{96,64},{128,96},{160,128},{192,160},{224,192},{0,2... | collective-permute-start | bytes 98312 | tf_op jit(solution)/shard_map/ppermute | solution.py:18
  480.8 4.6 collective-permute-start.26
  482.5 3.7 collective-permute-start.27
  (21 other events, 25.6 us)
Sparse Core Ops, SparseCore 0:
  131.0 251.6 all-reduce.2
where the time goes:
time: 506 us; the launch traced here: 500 us
  waiting for transfers between devices  261 us (52%)
  starting transfers between devices  79.1 us (16%)
  blocking collectives  78 us (15%)
  matrix products  42 us (8%)
  between operations  17.1 us (3%)
  local copies, waits for them, and re-layouts  13.3 us (3%)
  other arithmetic  9.33 us (2%)
    psum x1, waiting for transfers between devices, local(): lax.psum((grad_first, bias_first, grad_middle, bias_middle, grad_last, bi...  247 us
    psum x1, blocking collectives, local(): lax.psum((grad_first, bias_first, grad_middle, bias_middle, grad_last, bi...  78 us
    ppermute x14, starting transfers between devices, padded_2(): after = lax.ppermute(leading, axis, down)  48.8 us
    ppermute x14, starting transfers between devices, padded_2(): before = lax.ppermute(last, axis, up)  30.3 us
    dot_general x162, matrix products, conv_block(): jnp.einsum('ok,kxytz->oxytz', tap_weights[a, b, c], window, preferred_ele...  28.9 us
    dot_general x81, matrix products, kernel_grad(): jnp.einsum('oxytz,kxytz->ok', cotangent, window, preferred_element_type=j...  13.1 us
  transfers between devices with their start and end apart: 29, of which 16 were waited for; matrix products, arithmetic and copies ran while one was open for 5% of the time, Pallas kernels for 0%

commit v1 on v0

v1 whole, which is shorter than its diff:
```python
import functools

import jax
import jax.numpy as jnp
import numpy as np
from jax import lax
from jax.experimental import pallas as pl
from jax.experimental.pallas import tpu as pltpu
from jax.sharding import PartitionSpec as P

HOPPING = 0.15
QUARTIC = 0.1
F32 = jnp.float32
BF16 = jnp.bfloat16

HALO = 6
ROWS = 2 + 2 * HALO
XP = 10
PACK_ROWS = 344


def tap_selector():
    table = np.zeros((32, 16, 64), np.float32)
    for x in range(2):
        for y in range(2):
            for t in range(4):
                for a in range(3):
                    for b in range(3):
                        for c in range(3):
                            column = (x + a) * 16 + (y + b) * 4 + (t + c - 1) % 4
                            table[a * 9 + b * 3 + c, (x * 2 + y) * 4 + t, column] = 1.0
    return table.reshape(32, 1024)


def roll_z(v, shift):
    shift = shift % 128
    if shift == 0:
        return v
    last = v.ndim - 1
    return jnp.concatenate(
        [pltpu.roll(v[..., :128], shift, last), pltpu.roll(v[..., 128:], shift, last)], axis=last
    )


def swap_halves(v):
    return jnp.concatenate([v[..., 128:], v[..., :128]], axis=v.ndim - 1)


def iota(shape, dim):
    return lax.broadcasted_iota(jnp.int32, shape, dim)


def band_tile(taps, first, rows):
    zero = jnp.zeros((rows, 128), F32)
    left = taps[first] if 0 <= first <= 2 else zero
    right = taps[first + 1] if 0 <= first + 1 <= 2 else zero
    return jnp.where(iota((rows, 128), 1) < 64, left, right)


def build_hidden_band(taps_ref, band_ref):
    zero = jnp.zeros((16, 128), BF16)
    for d in range(3):
        for t in range(4):
            for a in range(3):
                taps = []
                for b in range(3):
                    tap = taps_ref[d * 9 + a * 3 + b].astype(F32)
                    taps.append(pltpu.roll(tap, (16 * (t - 1)) % 128, 1))
                for y in range(2):
                    for pair in range(2):
                        tile = band_tile(taps, 2 * pair - y, 16).astype(BF16)
                        for x in range(2):
                            row = d * 256 + ((x * 2 + y) * 4 + t) * 16
                            lane = ((x + a) * 2 + pair) * 128
                            band_ref[row : row + 16, lane : lane + 128] = tile
            for y in range(2):
                for pair in range(2):
                    for x, far in ((0, 3), (1, 0)):
                        row = d * 256 + ((x * 2 + y) * 4 + t) * 16
                        lane = (far * 2 + pair) * 128
                        band_ref[row : row + 16, lane : lane + 128] = zero


def build_head_band(taps_ref, band_ref):
    for d in range(3):
        for x in range(2):
            for window in range(4):
                a = window - x
                for pair in range(3):
                    for half in range(2):
                        row = d * 64 + x * 32 + half * 16
                        lane = (window * 3 + pair) * 128
                        if 0 <= a <= 2:
                            taps = [taps_ref[d * 9 + a * 3 + b].astype(F32) for b in range(3)]
                            tile = jnp.concatenate(
                                [band_tile(taps, 2 * pair - 2 * half - y, 8) for y in range(2)], axis=0
                            )
                        else:
                            tile = jnp.zeros((16, 128), F32)
                        band_ref[row : row + 16, lane : lane + 128] = tile.astype(BF16)


def combine_z(parts, rows):
    return (
        roll_z(parts[:rows], 1) + parts[rows : 2 * rows] + roll_z(parts[2 * rows :], -1)
    )


def rotate_groups(v, step, lanes):
    if step == 0:
        return v
    group = (iota(v.shape, 1) // lanes) % 4
    ahead = pltpu.roll(v, (128 - lanes * step) % 128, 1)
    behind = pltpu.roll(v, lanes * (4 - step), 1)
    return jnp.where(group + step < 4, ahead, behind)


def rotate_rows(v, step):
    if step == 0:
        return v
    ahead = pltpu.roll(v, v.shape[0] - step, 0)
    behind = pltpu.roll(v, 4 - step, 0)
    return jnp.where(iota(v.shape, 0) % 4 + step < 4, ahead, behind)


def main_kernel(
    place_ref,
    noise_ref,
    small_ref,
    selector_ref,
    taps2_ref,
    taps2t_ref,
    taps3_ref,
    b1_ref,
    b2_ref,
    b3_ref,
    field_out,
    rest_out,
    window_out,
    pack_out,
    nz,
    inp,
    h1,
    h2,
    cm,
    cmr,
    cf,
    cl,
    head,
    phi,
    own_field,
    own_rest,
    w1,
    wl,
    w2,
    w2t,
    w3,
    gm,
    gl,
    gf,
):
    spread = jnp.dot(small_ref[...], selector_ref[...], preferred_element_type=F32)
    for g in range(16):
        piece = spread[:, g * 64 : (g + 1) * 64]
        w1[g * 16 : (g + 1) * 16, :] = jnp.concatenate(
            [piece[16 * k : 16 * k + 16] for k in range(3)], axis=1
        ).astype(BF16)
        wl[g * 16 : (g + 1) * 16, :] = jnp.concatenate(
            [piece[48 + 16 * k : 64 + 16 * k] for k in range(6)], axis=1
        ).astype(BF16)
    build_hidden_band(taps2_ref, w2)
    build_hidden_band(taps2t_ref, w2t)
    build_head_band(taps3_ref, w3)

    rows_in = 4 * ROWS
    shape = (rows_in, 256)
    site = iota(shape, 0) // 4 + iota(shape, 0) % 4 + iota(shape, 1) % 128
    even = site % 2
    for xl in range(8):
        v = jnp.concatenate([noise_ref[xl], noise_ref[xl + 8]], axis=1)
        nz[xl + 1] = v
        if xl == 7:
            nz[0] = swap_halves(v)
        if xl == 0:
            nz[9] = swap_halves(v)
    for xl in range(XP):
        v = jnp.where(even == (xl + 1) % 2, nz[xl], 0.0)
        inp[0, xl] = roll_z(v, 1)
        inp[1, xl] = v
        inp[2, xl] = roll_z(v, -1)

    def wrap(ref):
        ref[0] = swap_halves(ref[8])
        ref[9] = swap_halves(ref[1])

    def first_body(step, _):
        xp = step // 6
        yp = step % 6
        window = inp[:, pl.ds(2 * xp, 4), pl.ds(pl.multiple_of(8 * yp, 8), 16), :]
        window = window.reshape(192, 256).astype(BF16)
        out = jnp.dot(w1[...], window, preferred_element_type=F32)
        out = jnp.tanh(out.reshape(16, 16, 256) + b1_ref[...][None]).reshape(256, 256).astype(BF16)
        row = pl.ds(pl.multiple_of(yp * 128, 128), 128)
        h1[2 * xp + 1, row, :] = out[:128]
        h1[2 * xp + 2, row, :] = out[128:]
        return 0

    lax.fori_loop(0, 24, first_body, 0)
    wrap(h1)

    def second_body(step, _):
        xp = step // 5
        yp = step % 5
        window = h1[pl.ds(2 * xp, 4), pl.ds(pl.multiple_of(yp * 128, 128), 256), :].reshape(1024, 256)
        parts = jnp.dot(w2[...], window, preferred_element_type=F32)
        out = combine_z(parts, 256)
        out = jnp.tanh(out.reshape(16, 16, 256) + b2_ref[...][None]).reshape(256, 256).astype(BF16)
        row = pl.ds(pl.multiple_of(yp * 128, 128), 128)
        h2[2 * xp + 1, row, :] = out[:128]
        h2[2 * xp + 2, row, :] = out[128:]
        return 0

    lax.fori_loop(0, 20, second_body, 0)
    wrap(h2)

    top = iota((8, 256), 0) < 4

    def head_body(step, _):
        xp = step // 2
        yq = step % 2
        window = h2[pl.ds(2 * xp, 4), pl.ds(pl.multiple_of(yq * 256, 256), 384), :].reshape(1536, 256)
        parts = jnp.dot(w3[...], window, preferred_element_type=F32)
        out = combine_z(parts, 64)
        out = (out.reshape(8, 8, 256) + b3_ref[...][None]).reshape(64, 256)
        for x in range(2):
            for pair in range(2):
                base = x * 32 + pair * 16
                lower = out[base : base + 8]
                upper = out[base + 8 : base + 16]
                row = pl.ds(pl.multiple_of(yq * 16, 16) + pair * 8, 8)
                head[0, 2 * xp + x, row, :] = jnp.where(top, lower, pltpu.roll(upper, 4, 0))
                head[1, 2 * xp + x, row, :] = jnp.where(top, pltpu.roll(lower, 4, 0), upper)
        return 0

    lax.fori_loop(0, 8, head_body, 0)

    shape = (32, 256)
    row32 = iota(shape, 0)
    site = row32 // 4 + 1 + row32 % 4 + iota(shape, 1) % 128
    even = site % 2
    for xl in range(8):
        frozen = even == xl % 2
        noise = nz[xl + 1, 12:44, :]
        log_scale = jnp.tanh(head[0, xl])
        head[0, xl] = log_scale
        moved = noise * jnp.exp(log_scale) + head[1, xl]
        phi[xl + 1] = jnp.where(frozen, noise, moved)
    wrap(phi)

    own = (row32 >= 12) & (row32 < 20)
    inner_t = row32 % 4
    loss = jnp.zeros(shape, F32)
    cot_sum = [jnp.zeros((8, 256), F32), jnp.zeros((8, 256), F32)]
    for xl in range(8):
        frozen = even == xl % 2
        noise = nz[xl + 1, 12:44, :]
        log_scale = head[0, xl]
        growth = jnp.exp(log_scale)
        here = phi[xl + 1]
        upward = (
            phi[xl + 2]
            + pltpu.roll(here, 28, 0)
            + jnp.where(inner_t == 3, pltpu.roll(here, 3, 0), pltpu.roll(here, 31, 0))
            + roll_z(here, -1)
        )
        downward = (
            phi[xl]
            + pltpu.roll(here, 4, 0)
            + jnp.where(inner_t == 0, pltpu.roll(here, 29, 0), pltpu.roll(here, 1, 0))
            + roll_z(here, 1)
        )
        squared = here * here
        density = (
            -2.0 * HOPPING * here * upward + squared + QUARTIC * (squared - 1.0) * (squared - 1.0)
        )
        local = -0.5 * noise * noise - jnp.where(frozen, 0.0, log_scale) + density
        loss = loss + jnp.where(own, local, 0.0)
        force = (
            -2.0 * HOPPING * (upward + downward)
            + 2.0 * here
            + 4.0 * QUARTIC * here * (squared - 1.0)
        )
        d_scale = (force * noise * growth - 1.0) * (1.0 - log_scale * log_scale)
        pair = (jnp.where(frozen, 0.0, d_scale), jnp.where(frozen, 0.0, force))
        rest = force * jnp.where(frozen, 1.0, growth) - noise
        own_field[xl] = here[12:20]
        own_rest[xl] = rest[12:20]
        for ch in range(2):
            v = pltpu.roll(pair[ch], 28, 0)[:24].astype(BF16).astype(F32)
            cot_sum[ch] = cot_sum[ch] + v[8:16]
            for d, shift in ((0, 1), (1, 0), (2, -1)):
                moved = roll_z(v, shift)
                cl[d, ch, xl + 1] = moved
                if xl == 7:
                    cl[d, ch, 0] = swap_halves(moved)
                if xl == 0:
                    cl[d, ch, 9] = swap_halves(moved)

    def middle_body(step, _):
        xp = step // 2
        yp = step % 2
        window = cl[:, :, pl.ds(2 * xp, 4), pl.ds(pl.multiple_of(8 * yp, 8), 16), :]
        window = window.reshape(384, 256).astype(BF16)
        out = jnp.dot(wl[...], window, preferred_element_type=F32)
        for x in range(2):
            hidden = h2[2 * xp + 1 + x, pl.ds(pl.multiple_of((3 + 2 * yp) * 64, 64), 128), :].astype(F32)
            v = out[128 * x : 128 * x + 128] * (1.0 - hidden * hidden)
            cm[2 * xp + 1 + x, pl.ds(pl.multiple_of(yp * 128, 128), 128), :] = v.astype(BF16)
        return 0

    lax.fori_loop(0, 8, middle_body, 0)
    wrap(cm)

    def shift_body(xl, _):
        v = cm[xl, 64:192, :].astype(F32)
        cmr[0, xl] = roll_z(v, -1).astype(BF16)
        cmr[1, xl] = v.astype(BF16)
        cmr[2, xl] = roll_z(v, 1).astype(BF16)
        return 0

    lax.fori_loop(0, XP, shift_body, 0)

    def first_cot_body(xp, _):
        window = cm[pl.ds(2 * xp, 4)].reshape(1024, 256)
        parts = jnp.dot(w2t[...], window, preferred_element_type=F32)
        out = combine_z(parts, 256)
        for x in range(2):
            hidden = h1[2 * xp + 1 + x, 320:448, :].astype(F32)
            v = out[128 * x : 128 * x + 128] * (1.0 - hidden * hidden)
            cf[2 * xp + 1 + x] = v.astype(BF16)
        return 0

    lax.fori_loop(0, 4, first_cot_body, 0)
    wrap(cf)

    gm[...] = jnp.zeros_like(gm)
    gl[...] = jnp.zeros_like(gl)
    gf[...] = jnp.zeros_like(gf)
    over_lanes = (((1,), (1,)), ((), ()))

    def grad_body(xl, _):
        left = cmr[:, pl.ds(xl - 1, 3)].reshape(1152, 256)
        gm[...] += lax.dot_general(left, h1[xl, 256:512, :], over_lanes, preferred_element_type=F32)
        left = cl[:, :, pl.ds(xl - 1, 3), 8:16, :].reshape(144, 256).astype(BF16)
        gl[...] += lax.dot_general(left, h2[xl, 192:448, :], over_lanes, preferred_element_type=F32)
        left = inp[:, pl.ds(xl - 1, 3), 20:36, :].reshape(144, 256).astype(BF16)
        gf[...] += lax.dot_general(left, cf[xl], over_lanes, preferred_element_type=F32)
        return 0

    lax.fori_loop(1, 9, grad_body, 0)

    low = iota((16, 128), 1) < 64
    third = []
    for g in range(9):
        sums = []
        for y in range(2):
            for side in range(2):
                total = None
                for t in range(4):
                    row = g * 128 + y * 64 + t * 16
                    block = gm[row : row + 16, side * 128 : side * 128 + 128]
                    block = rotate_groups(block, (t - 1) % 4, 16)
                    total = block if total is None else total + block
                sums.append(total)
        u0, u1, v0, v1 = sums
        v0 = pltpu.roll(v0, 64, 1)
        v1 = pltpu.roll(v1, 64, 1)
        pack_out[g * 16 : g * 16 + 16, :] = u0 + jnp.where(low, v0, v1)
        third.append(u1 + v1)
    third.append(third[8])
    for g in range(5):
        packed = jnp.where(low, third[2 * g], pltpu.roll(third[2 * g + 1], 64, 1))
        pack_out[144 + g * 16 : 160 + g * 16, :] = packed

    shape = (144, 128)
    row144 = iota(shape, 0)
    sides = []
    for side in range(2):
        v = gl[:, side * 128 : side * 128 + 128]
        total = jnp.zeros(shape, F32)
        for t in range(4):
            total = total + jnp.where(row144 % 4 == t, rotate_groups(v, (t - 1) % 4, 16), 0.0)
        sides.append(total)
    lower_y = (row144 // 4) % 2 == 0
    r0, r1 = sides
    s0 = pltpu.roll(r0, 64, 1)
    s1 = pltpu.roll(r1, 64, 1)
    low = iota(shape, 1) < 64
    both = jnp.where(lower_y, r0, jnp.where(low, s0, s1))
    last = jnp.where(lower_y, r1, s1)
    pack_out[256:304, :] = jnp.zeros((48, 128), F32)
    pack_out[256:274, :] = both.reshape(18, 8, 128).sum(axis=1)
    pack_out[280:298, :] = last.reshape(18, 8, 128).sum(axis=1)

    v = gf[...]
    total = jnp.zeros(shape, F32)
    for y in range(2):
        for t in range(4):
            moved = v if y + t == 0 else pltpu.roll(v, 128 - (y * 64 + t * 16), 1)
            if y:
                moved = pltpu.roll(moved, 140, 0)
            total = total + rotate_rows(moved, (t - 1) % 4)
    total = jnp.where(iota(shape, 1) < 16, total, 0.0)
    packed = total[:16]
    for g in range(1, 8):
        packed = packed + pltpu.roll(total[g * 16 : g * 16 + 16], 16 * g, 1)
    pack_out[224:240, :] = packed
    pack_out[240:256, :] = total[128:144]

    def channel_sum(read, base):
        acc = None
        for xl in range(1, 9):
            v = read(xl).astype(F32)
            v = v[:, :128] + v[:, 128:]
            acc = v if acc is None else acc + v
        acc = acc.reshape(8, 16, 128).sum(axis=0)
        pack_out[base : base + 16, :] = jnp.broadcast_to(jnp.sum(acc, axis=1, keepdims=True), (16, 128))

    channel_sum(lambda xl: cm[xl, 64:192, :], 304)
    channel_sum(lambda xl: cf[xl], 320)
    row8 = iota((8, 128), 0)
    tile = jnp.where(row8 == 0, jnp.sum(cot_sum[0]), 0.0)
    tile = jnp.where(row8 == 1, jnp.sum(cot_sum[1]), tile)
    pack_out[336:344, :] = jnp.where(row8 == 2, jnp.sum(loss), tile)

    place = place_ref[0]
    start = 2 * (place % 4)
    high = place >= 4

    def pick(v):
        return jnp.where(high, v[:, 128:], v[:, :128])

    for x in range(2):
        field_out[x] = pick(own_field[start + x])
        rest_out[x] = pick(own_rest[start + x])
    for x in range(4):
        window_out[x] = pick(cf[start + x])


def input_kernel(left_ref, own_ref, right_ref, taps_ref, rest_ref, out_ref, band):
    shape = (8, 128)
    upper = iota(shape, 0) < 4
    zero = jnp.zeros(shape, F32)
    for d in range(3):
        for window in range(4):
            for pair in range(2):
                tiles = []
                for x in range(2):
                    a = window - x
                    if 0 <= a <= 2:
                        taps = [taps_ref[d * 9 + a * 3 + b].astype(F32) for b in range(3)]
                        tiles.append(
                            jnp.where(
                                upper, band_tile(taps, 2 * pair, 8), band_tile(taps, 2 * pair - 1, 8)
                            )
                        )
                    else:
                        tiles.append(zero)
                lane = (window * 2 + pair) * 128
                band[d * 16 : d * 16 + 16, lane : lane + 128] = jnp.concatenate(tiles, axis=0).astype(BF16)
    window = jnp.concatenate([left_ref[...], own_ref[...], right_ref[...]], axis=1).reshape(1024, 128)
    parts = jnp.dot(band[...], window, preferred_element_type=F32)
    out = pltpu.roll(parts[:16], 1, 1) + parts[16:32] + pltpu.roll(parts[32:], 127, 1)
    site = iota(shape, 0) // 4 + iota(shape, 0) % 4 + iota(shape, 1)
    for x in range(2):
        out_ref[x] = jnp.where((site + x) % 2 == 0, out[8 * x : 8 * x + 8], 0.0) + rest_ref[x]


def vmem():
    return pl.BlockSpec(memory_space=pltpu.VMEM)


def run_main(place, noise, small, selector, taps2, taps2t, taps3, b1, b2, b3):
    scratch = [
        ((XP, 4 * ROWS, 256), F32),
        ((3, XP, 4 * ROWS, 256), F32),
        ((XP, 768, 256), BF16),
        ((XP, 640, 256), BF16),
        ((XP, 256, 256), BF16),
        ((3, XP, 128, 256), BF16),
        ((XP, 128, 256), BF16),
        ((3, 2, XP, 24, 256), F32),
        ((2, 8, 32, 256), F32),
        ((XP, 32, 256), F32),
        ((8, 8, 256), F32),
        ((8, 8, 256), F32),
        ((256, 192), BF16),
        ((256, 384), BF16),
        ((768, 1024), BF16),
        ((768, 1024), BF16),
        ((192, 1536), BF16),
        ((1152, 256), F32),
        ((144, 256), F32),
        ((144, 128), F32),
    ]
    return pl.pallas_call(
        main_kernel,
        out_shape=(
            jax.ShapeDtypeStruct((2, 8, 128), F32),
            jax.ShapeDtypeStruct((2, 8, 128), F32),
            jax.ShapeDtypeStruct((4, 128, 128), BF16),
            jax.ShapeDtypeStruct((PACK_ROWS, 128), F32),
        ),
        in_specs=[pl.BlockSpec(memory_space=pltpu.SMEM)] + [vmem()] * 9,
        out_specs=(vmem(), vmem(), vmem(), vmem()),
        scratch_shapes=[pltpu.VMEM(s, t) for s, t in scratch],
        compiler_params=pltpu.CompilerParams(vmem_limit_bytes=56 * 1024 * 1024),
    )(place, noise, small, selector, taps2, taps2t, taps3, b1, b2, b3)


def run_input(left, own, right, taps, rest):
    return pl.pallas_call(
        input_kernel,
        out_shape=jax.ShapeDtypeStruct((2, 8, 128), F32),
        in_specs=[vmem()] * 5,
        out_specs=vmem(),
        scratch_shapes=[pltpu.VMEM((48, 1024), BF16)],
        compiler_params=pltpu.CompilerParams(vmem_limit_bytes=16 * 1024 * 1024),
    )(left, own, right, taps, rest)


def pad_taps(v):
    return jnp.pad(v, [(0, 0)] * (v.ndim - 2) + [(0, 1), (0, 0)])


def hidden_taps(kernel):
    v = pad_taps(jnp.transpose(kernel, (5, 2, 3, 0, 4, 1))).reshape(27, 16, 64)
    return jnp.concatenate([v, v], axis=2)


def banded_taps(v):
    v = pad_taps(v)
    v = jnp.stack([jnp.roll(v, t - 1, axis=2) for t in range(4)], axis=2)
    v = v.reshape(27, -1, 64)
    return jnp.concatenate([v, v], axis=2)


def swapped(v, axis_size, partner):
    return lax.ppermute(v, "gy", [(i, partner(i)) for i in range(axis_size)])


def gather_noise(noise):
    size_y = lax.axis_size("gy")
    size_x = lax.axis_size("gx")
    even = lax.axis_index("gy") % 2 == 0
    chips = size_y // 2

    def far(i):
        return (i - 3) % size_y if i % 2 == 0 else (i + 3) % size_y

    def chip_after(i):
        return ((((i >> 1) + 1) ^ 1) - 1) % chips * 2 + (i & 1)

    distant = swapped(noise, size_y, far)
    beside = swapped(noise, size_y, lambda i: i ^ 1)
    block = jnp.concatenate(
        [jnp.where(even, noise, beside), jnp.where(even, beside, noise)], axis=1
    )
    paired = swapped(block, size_y, lambda i: i ^ 2)
    across = swapped(block, size_y, chip_after)
    even_chip = (lax.axis_index("gy") // 2) % 2 == 0
    before = jnp.where(even_chip, across, paired)
    after = jnp.where(even_chip, paired, across)
    middle = jnp.concatenate([before, block, after], axis=1)
    window = jnp.where(
        even,
        jnp.concatenate([distant, middle], axis=1),
        jnp.concatenate([middle, distant], axis=1),
    )
    window = window.reshape(2, 4 * ROWS, 128)
    sent = jnp.broadcast_to(window[None], (size_x,) + window.shape)
    return lax.all_to_all(sent, "gx", 0, 0, tiled=True).reshape(16, 4 * ROWS, 128)


def sum_over_y(v):
    size_y = lax.axis_size("gy")

    def along_z(partner):
        def f(i):
            return ((i >> 4) * 8 + partner((i >> 1) & 7)) * 2 + (i & 1)

        return f

    crossing = (3, 6, 5, 0, 7, 2, 1, 4)
    for partner in (
        lambda i: i ^ 1,
        lambda i: i ^ 16,
        along_z(lambda z: z ^ 1),
        along_z(lambda z: (((z + 1) ^ 1) - 1) % 8),
        along_z(lambda z: crossing[z]),
    ):
        v = v + swapped(v, size_y, partner)
    return v


def local(noise, w_first, b_first, w_middle, b_middle, w_last, b_last):
    size_y = lax.axis_size("gy")
    sites = float(noise.size * lax.axis_size("gx") * size_y)
    flip = (slice(None), slice(None)) + (slice(None, None, -1),) * 4
    small = jnp.concatenate(
        [
            jnp.transpose(w_first[:, 0], (4, 0, 1, 2, 3)).reshape(48, 27),
            jnp.transpose(w_last[flip], (5, 0, 1, 2, 3, 4)).reshape(96, 27),
        ],
        axis=0,
    )
    small = jnp.pad(small, ((0, 0), (0, 5)))
    taps2 = hidden_taps(w_middle)
    taps2t = hidden_taps(jnp.transpose(w_middle[flip], (1, 0, 2, 3, 4, 5)))
    taps3 = banded_taps(jnp.transpose(w_last, (5, 2, 3, 0, 4, 1)).reshape(27, 2, 3, 16))
    tapsd = banded_taps(jnp.transpose(w_first[flip], (5, 2, 3, 1, 4, 0)).reshape(27, 1, 3, 16))
    tapsd = jnp.concatenate([tapsd, tapsd], axis=1)

    gathered = gather_noise(noise)
    place = lax.axis_index("gx").astype(jnp.int32).reshape(1)
    field, rest, window, pack = run_main(
        place,
        gathered,
        small,
        jnp.asarray(tap_selector(), BF16),
        taps2,
        taps2t,
        taps3,
        b_first.reshape(16, 1),
        b_middle.reshape(16, 1),
        jnp.repeat(b_last, 4).reshape(8, 1),
    )
    left = swapped(window[:, 64:], size_y, lambda i: (i + 1) % size_y)
    right = swapped(window[:, :64], size_y, lambda i: (i - 1) % size_y)
    noise_grad = run_input(left, window, right, tapsd, rest)

    total = sum_over_y(pack) * (1.0 / sites)
    most = total[:144].reshape(3, 3, 16, 2, 4, 16)
    third = total[144:224].reshape(5, 16, 2, 4, 16)
    third = jnp.transpose(third, (0, 2, 1, 3, 4)).reshape(10, 16, 4, 16)[:9].reshape(3, 3, 16, 1, 4, 16)
    middle = jnp.concatenate([most, third], axis=3)[:, ::-1, :, :, :3]
    grad_middle = jnp.transpose(middle, (2, 5, 1, 3, 4, 0))
    first = jnp.concatenate([total[224:240], total[240:256, :16]], axis=1).reshape(4, 4, 3, 3, 16)
    grad_first = jnp.transpose(first[:3, :3], (4, 3, 0, 1, 2))[:, None]
    last = jnp.concatenate([total[256:274], total[280:298, :64]], axis=1)
    last = last.reshape(3, 2, 3, 3, 4, 16)[::-1, :, ::-1, :, :3]
    grad_last = jnp.transpose(last, (1, 5, 2, 3, 4, 0))
    return (
        field.reshape(noise.shape),
        noise_grad.reshape(noise.shape),
        total[338, 0],
        grad_first,
        total[320:336, 0],
        grad_middle,
        total[304:320, 0],
        grad_last,
        total[336:338, 0],
    )


def solution(mesh):
    placed = (P("gx", "gy", None, None), P(), P(), P(), P(), P(), P())
    return jax.shard_map(
        local,
        mesh=mesh,
        in_specs=placed,
        out_specs=(P("gx", "gy", None, None), P("gx", "gy", None, None)) + (P(),) * 7,
        check_vma=False,
    )
```

time: 506 us -> 111 us (0.22); the launches traced: 500 us -> 110 us
  waiting for transfers between devices: 261 us -> 28.2 us
  blocking collectives: 78 us -> 0 us
  starting transfers between devices: 79.1 us -> 24 us
  matrix products: 42 us -> 0 us
  Pallas kernels: 0 us -> 37.5 us
  between operations: 17.1 us -> 1.11 us
  other arithmetic: 9.33 us -> 2.92 us
    psum x1 -> x0, waiting for transfers between devices: 247 us -> none  [local(): lax.psum((grad_first, bias_first, grad_middle, bias_middle, grad_last, bi...]
    psum x1 -> x0, blocking collectives: 78 us -> none  [local(): lax.psum((grad_first, bias_first, grad_middle, bias_middle, grad_last, bi...]
    ppermute x28 -> x11, starting transfers between devices: 79.1 us -> 17.6 us  [swapped(): return lax.ppermute(v, 'gy', [(i, partner(i)) for i in range(axis_size)])]
    dot_general x243 -> x0, matrix products: 42 us -> none  [the longest x162 28.9 us: conv_block(): jnp.einsum('ok,kxytz->oxytz', tap_weights[a, b, c], window, preferred_ele...]
    pallas_call x0 -> x2, Pallas kernels: none -> 37.5 us  [the longest x1 36.6 us: run_main(): pl.pallas_call(main_kernel, out_shape=(jax.ShapeDtypeStruct((2, 8, 128),...]
    ppermute x28 -> x11, waiting for transfers between devices: 14.2 us -> 26.5 us  [swapped(): return lax.ppermute(v, 'gy', [(i, partner(i)) for i in range(axis_size)])]
    all_to_all x0 -> x1, starting transfers between devices: none -> 6.49 us  [gather_noise(): lax.all_to_all(sent, 'gx', 0, 0, tiled=True).reshape(16, 4 * ROWS, 128)]
  transfers between devices with their start and end apart: 29 -> 12, of which waited for: 16 -> 8; matrix products, arithmetic and copies ran while one was open for 5% -> 9% of each run, Pallas kernels for 0% -> 1%
where the time goes in v1:
time: 111 us; the launch traced here: 110 us
  Pallas kernels  37.5 us (34%)
  waiting for transfers between devices  28.2 us (25%)
  starting transfers between devices  24 us (22%)
  local copies, waits for them, and re-layouts  16.3 us (15%)
  other arithmetic  2.92 us (3%)
  between operations  1.11 us (1%)
    pallas_call x1, Pallas kernels, run_main(): pl.pallas_call(main_kernel, out_shape=(jax.ShapeDtypeStruct((2, 8, 128),...  36.6 us
    ppermute x11, waiting for transfers between devices, swapped(): return lax.ppermute(v, 'gy', [(i, partner(i)) for i in range(axis_size)])  26.5 us
    ppermute x11, starting transfers between devices, swapped(): return lax.ppermute(v, 'gy', [(i, partner(i)) for i in range(axis_size)])  17.6 us
    all_to_all x1, starting transfers between devices, gather_noise(): lax.all_to_all(sent, 'gx', 0, 0, tiled=True).reshape(16, 4 * ROWS, 128)  6.49 us
    unnamed x34, local copies, waits for them, and re-layouts  3.7 us
  transfers between devices with their start and end apart: 12, of which 8 were waited for; matrix products, arithmetic and copies ran while one was open for 9% of the time, Pallas kernels for 1%

profile of v1, /device:TPU:1, one launch (start us, length us, event | category | flops | bytes accessed | tf_op | source)
XLA Modules:
  0.0 110.0 jit_solution(4345735788528787003)
XLA Ops:
  0.6 4.5 %collective-permute-start = (f32[2,2,4,128]{3,2,1,0:T(4,128)}, f32[2,2,4,128]{3,2,1,0:T(4,128)S(1)}, u32[]{:S(2)}, u32[]{:S(2)}) collective-permute-start(f32[2,2,4,128]{3,2,1,0:T(4,128)} %param.8), channel_id=1, source_target_pairs={{0,29},{1,4},{2,31},{3,6},{4,1},{5,8},{6,3},{7,10},{8,5},{9,12},{1... | collective-permute-start | bytes 24584 | tf_op jit(solution)/shard_map/ppermute | solution.py:549
  5.1 3.9 %collective-permute-start.1 = (f32[2,2,4,128]{3,2,1,0:T(4,128)}, f32[2,2,4,128]{3,2,1,0:T(4,128)S(1)}, u32[]{:S(2)}, u32[]{:S(2)}) collective-permute-start(f32[2,2,4,128]{3,2,1,0:T(4,128)} %param.8), channel_id=1, source_target_pairs={{0,1},{1,0},{2,3},{3,2},{4,5},{5,4},{6,7},{7,6},{8,9},{9,8},{10,11... | collective-permute-start | bytes 24584 | tf_op jit(solution)/shard_map/ppermute | solution.py:549
  9.0 0.8 copy.58
  10.2 0.5 pad_maximum_fusion.1
  10.7 0.3 copy-done.7
  11.0 0.7 copy-done.8
  12.0 0.6 copy-done.9
  12.6 0.8 collective-permute-start.3
  13.4 0.7 collective-permute-start.2
  14.1 1.1 %collective-permute-done.3 = f32[2,4,4,128]{3,2,1,0:T(4,128)S(1)} collective-permute-done((f32[2,4,4,128]{3,2,1,0:T(4,128)S(1)}, f32[2,4,4,128]{3,2,1,0:T(4,128)S(1)}, u32[]{:S(2)}, u32[]{:S(2)}) %collective-permute-start.3) | collective-permute-done | bytes 16416 | tf_op jit(solution)/shard_map/ppermute | solution.py:549
  15.2 2.8 %collective-permute-done.2 = f32[2,4,4,128]{3,2,1,0:T(4,128)S(1)} collective-permute-done((f32[2,4,4,128]{3,2,1,0:T(4,128)S(1)}, f32[2,4,4,128]{3,2,1,0:T(4,128)S(1)}, u32[]{:S(2)}, u32[]{:S(2)}) %collective-permute-start.2) | collective-permute-done | bytes 16416 | tf_op jit(solution)/shard_map/ppermute | solution.py:549
  18.2 0.8 broadcast_in_dim.11
  19.0 6.5 %all-to-all-start = ((f32[8,2,56,128]{3,2,1,0:T(8,128)}), f32[8,2,56,128]{3,2,1,0:T(8,128)S(1)}, u32[]{:S(2)}, u32[]{:S(2)}) async-start(f32[8,2,56,128]{3,2,1,0:T(8,128)} %broadcast_in_dim.11), calls=%async_computation | async-start | bytes 917504 | tf_op jit(solution)/shard_map/all_to_all | solution.py:582
  25.6 0.7 reshape_reshape.4.b3_ref
  26.3 0.7 copy.62.b1_ref
  27.0 0.7 copy.63.b2_ref
  27.8 0.3 copy.59
  28.3 0.3 copy.81
  28.5 0.6 pad.21.small_ref
  29.2 0.3 pad.23.clone
  29.4 0.2 reshape.100
  29.9 0.3 pad.22.clone
  30.2 0.2 reshape.99
  30.4 0.7 pad_maximum_fusion.4.taps3_ref
  31.1 0.8 pad_maximum_fusion.2
  32.0 1.7 %all-to-all-done = f32[8,2,56,128]{3,2,1,0:T(8,128)S(1)} async-done(((f32[8,2,56,128]{3,2,1,0:T(8,128)}), f32[8,2,56,128]{3,2,1,0:T(8,128)S(1)}, u32[]{:S(2)}, u32[]{:S(2)}) %all-to-all-start) | async-done | bytes 458784 | tf_op jit(solution)/shard_map/all_to_all | solution.py:582
  33.7 0.8 copy-done.2
  34.4 36.6 %shard_map.151 = (f32[2,8,128]{2,1,0:T(8,128)}, f32[2,8,128]{2,1,0:T(8,128)}, bf16[4,128,128]{2,1,0:T(8,128)(2,1)}, f32[344,128]{1,0:T(8,128)}) custom-call(s32[1]{0:T(128)} %bitcast.place_ref, f32[16,56,128]{2,1,0:T(8,128)} %bitcast.58, bf16[144,32]{1,0:T(8,128)(2,1)} %pad.21.small_ref, bf16[32,1024]{1,0:T(8,128)(2,1)} %constant.44.clone.selector_ref, ...), custom_call_target="tpu_custom_call" | custom-call | tf_op jit(solution)/shard_map/pallas_call | solution.py:506
  71.1 3.3 %collective-permute-start.6 = (f32[344,128]{1,0:T(8,128)}, f32[344,128]{1,0:T(8,128)S(1)}, u32[]{:S(2)}, u32[]{:S(2)}) collective-permute-start(f32[344,128]{1,0:T(8,128)} %get-tuple-element.16), channel_id=1, source_target_pairs={{0,1},{1,0},{2,3},{3,2},{4,5},{5,4},{6,7},{7,6},{8,9},{9,8},{10,11... | collective-permute-start | bytes 528392 | tf_op jit(solution)/shard_map/ppermute | solution.py:549
  74.6 1.0 collective-permute-done.6
  75.7 0.3 collective-permute-start.7
  76.2 5.4 %collective-permute-done.7 = f32[344,128]{1,0:T(8,128)S(1)} collective-permute-done((f32[344,128]{1,0:T(8,128)S(1)}, f32[344,128]{1,0:T(8,128)S(1)}, u32[]{:S(2)}, u32[]{:S(2)}) %collective-permute-start.7) | collective-permute-done | bytes 176160 | tf_op jit(solution)/shard_map/ppermute | solution.py:549
  81.8 4.7 %collective-permute-done.8 = f32[344,128]{1,0:T(8,128)S(1)} collective-permute-done((f32[344,128]{1,0:T(8,128)S(1)}, f32[344,128]{1,0:T(8,128)S(1)}, u32[]{:S(2)}, u32[]{:S(2)}) %collective-permute-start.8) | collective-permute-done | bytes 176160 | tf_op jit(solution)/shard_map/ppermute | solution.py:549
  87.1 5.0 %collective-permute-done.9 = f32[344,128]{1,0:T(8,128)S(1)} collective-permute-done((f32[344,128]{1,0:T(8,128)S(1)}, f32[344,128]{1,0:T(8,128)S(1)}, u32[]{:S(2)}, u32[]{:S(2)}) %collective-permute-start.9) | collective-permute-done | bytes 176160 | tf_op jit(solution)/shard_map/ppermute | solution.py:549
  92.1 0.3 collective-permute-start.10
  92.4 3.6 %collective-permute-start.5 = (bf16[4,64,128]{2,1,0:T(8,128)(2,1)S(1)}, bf16[4,64,128]{2,1,0:T(8,128)(2,1)S(1)}, u32[]{:S(2)}, u32[]{:S(2)}) collective-permute-start(bf16[4,64,128]{2,1,0:T(8,128)(2,1)S(1)} %get-tuple-element.37), channel_id=1, source_target_pairs={{0,31},{1,0},{2,1},{3,2},{4,3},{5,4},{6,5},{7,6},{8,7},{9,8},{10,9... | collective-permute-start | bytes 196616 | tf_op jit(solution)/shard_map/ppermute | solution.py:549
  96.1 0.4 maximum_maximum_fusion.taps_ref
  96.5 6.3 %collective-permute-done.5.right_ref = bf16[4,64,128]{2,1,0:T(8,128)(2,1)S(1)} collective-permute-done((bf16[4,64,128]{2,1,0:T(8,128)(2,1)S(1)}, bf16[4,64,128]{2,1,0:T(8,128)(2,1)S(1)}, u32[]{:S(2)}, u32[]{:S(2)}) %collective-permute-start.5) | collective-permute-done | bytes 65568 | tf_op jit(solution)/shard_map/ppermute | solution.py:549
  102.8 0.9 shard_map.152
  103.7 0.6 slice.120
  104.2 0.6 slice_reduce_fusion.2
  104.9 0.6 slice_reduce_fusion
  105.7 0.7 copy.78
  106.5 0.7 reverse_bitcast_fusion.2
  107.3 0.3 reshape.110
  107.7 0.8 slice-done.2
  108.5 0.4 reshape.109
  109.1 0.9 reverse_bitcast_fusion
  (93 shorter events, 3.3 us)
Async XLA Ops:
  0.6 13.5 %collective-permute-start = (f32[2,2,4,128]{3,2,1,0:T(4,128)}, f32[2,2,4,128]{3,2,1,0:T(4,128)S(1)}, u32[]{:S(2)}, u32[]{:S(2)}) collective-permute-start(f32[2,2,4,128]{3,2,1,0:T(4,128)} %param.8), channel_id=1, source_target_pairs={{0,29},{1,4},{2,31},{3,6},{4,1},{5,8},{6,3},{7,10},{8,5},{9,12},{1... | collective-permute-start | bytes 24584 | tf_op jit(solution)/shard_map/ppermute | solution.py:549
  5.1 6.9 %collective-permute-start.1 = (f32[2,2,4,128]{3,2,1,0:T(4,128)}, f32[2,2,4,128]{3,2,1,0:T(4,128)S(1)}, u32[]{:S(2)}, u32[]{:S(2)}) collective-permute-start(f32[2,2,4,128]{3,2,1,0:T(4,128)} %param.8), channel_id=1, source_target_pairs={{0,1},{1,0},{2,3},{3,2},{4,5},{5,4},{6,7},{7,6},{8,9},{9,8},{10,11... | collective-permute-start | bytes 24584 | tf_op jit(solution)/shard_map/ppermute | solution.py:549
  10.2 0.8 copy-start.7
  11.0 0.7 copy-start.8
  11.8 0.7 copy-start.9
  12.6 2.7 %collective-permute-start.3 = (f32[2,4,4,128]{3,2,1,0:T(4,128)S(1)}, f32[2,4,4,128]{3,2,1,0:T(4,128)S(1)}, u32[]{:S(2)}, u32[]{:S(2)}) collective-permute-start(f32[2,4,4,128]{3,2,1,0:T(4,128)S(1)} %pad_maximum_fusion.8), channel_id=1, source_target_pairs={{0,2},{1,3},{2,0},{3,1},{4,6},{5,7},{6,4},{7,5},{8,10},{9,11},{10,... | collective-permute-start | bytes 49160 | tf_op jit(solution)/shard_map/ppermute | solution.py:549
  13.4 4.7 %collective-permute-start.2 = (f32[2,4,4,128]{3,2,1,0:T(4,128)S(1)}, f32[2,4,4,128]{3,2,1,0:T(4,128)S(1)}, u32[]{:S(2)}, u32[]{:S(2)}) collective-permute-start(f32[2,4,4,128]{3,2,1,0:T(4,128)S(1)} %pad_maximum_fusion.8), channel_id=1, source_target_pairs={{0,30},{1,31},{2,4},{3,5},{4,2},{5,3},{6,8},{7,9},{8,6},{9,7},{10,... | collective-permute-start | bytes 49160 | tf_op jit(solution)/shard_map/ppermute | solution.py:549
  19.0 6.6 %copy-start.12 = (f32[2]{0:T(128)S(1)}, f32[2]{0:T(128)}, u32[]{:S(2)}) copy-start(f32[2]{0:T(128)} %param.14) | copy-start | bytes 28
  19.0 7.3 %copy-start.10 = (f32[16]{0:T(128)S(1)}, f32[16]{0:T(128)}, u32[]{:S(2)}) copy-start(f32[16]{0:T(128)} %param.10) | copy-start | bytes 196
  19.0 8.0 %copy-start.11 = (f32[16]{0:T(128)S(1)}, f32[16]{0:T(128)}, u32[]{:S(2)}) copy-start(f32[16]{0:T(128)} %param.12) | copy-start | bytes 196
  19.0 14.7 %all-to-all-start = ((f32[8,2,56,128]{3,2,1,0:T(8,128)}), f32[8,2,56,128]{3,2,1,0:T(8,128)S(1)}, u32[]{:S(2)}, u32[]{:S(2)}) async-start(f32[8,2,56,128]{3,2,1,0:T(8,128)} %broadcast_in_dim.11), calls=%async_computation | async-start | bytes 917504 | tf_op jit(solution)/shard_map/all_to_all | solution.py:582
  25.5 2.8 %copy-start.3 = (bf16[16,16,3,3,3,3]{1,0,5,4,3,2:T(8,128)(2,1)S(1)}, bf16[16,16,3,3,3,3]{1,0,5,4,3,2:T(8,128)(2,1)}, u32[]{:S(2)}) copy-start(bf16[16,16,3,3,3,3]{1,0,5,4,3,2:T(8,128)(2,1)} %param.11) | copy-start | bytes 124420
  33.7 0.8 copy-start.2
  71.1 4.6 %copy-start.6 = (f32[344,128]{1,0:T(8,128)S(1)}, f32[344,128]{1,0:T(8,128)}, u32[]{:S(2)}) copy-start(f32[344,128]{1,0:T(8,128)} %get-tuple-element.16) | copy-start | bytes 528388
  71.1 4.6 %collective-permute-start.6 = (f32[344,128]{1,0:T(8,128)}, f32[344,128]{1,0:T(8,128)S(1)}, u32[]{:S(2)}, u32[]{:S(2)}) collective-permute-start(f32[344,128]{1,0:T(8,128)} %get-tuple-element.16), channel_id=1, source_target_pairs={{0,1},{1,0},{2,3},{3,2},{4,5},{5,4},{6,7},{7,6},{8,9},{9,8},{10,11... | collective-permute-start | bytes 528392 | tf_op jit(solution)/shard_map/ppermute | solution.py:549
  74.5 7.2 %copy-start.5 = (bf16[27,1,3,16]{3,0,2,1:T(8,128)(2,1)}, bf16[27,1,3,16]{3,0,2,1:T(8,128)(2,1)S(1)}, u32[]{:S(2)}) copy-start(bf16[27,1,3,16]{3,0,2,1:T(8,128)(2,1)S(1)} %reshape.106) | copy-start | bytes 7780
  75.7 5.9 %collective-permute-start.7 = (f32[344,128]{1,0:T(8,128)S(1)}, f32[344,128]{1,0:T(8,128)S(1)}, u32[]{:S(2)}, u32[]{:S(2)}) collective-permute-start(f32[344,128]{1,0:T(8,128)S(1)} %add.39), channel_id=1, source_target_pairs={{0,16},{1,17},{2,18},{3,19},{4,20},{5,21},{6,22},{7,23},{8,24},{9,... | collective-permute-start | bytes 528392 | tf_op jit(solution)/shard_map/ppermute | solution.py:549
  81.6 4.8 %collective-permute-start.8 = (f32[344,128]{1,0:T(8,128)S(1)}, f32[344,128]{1,0:T(8,128)S(1)}, u32[]{:S(2)}, u32[]{:S(2)}) collective-permute-start(f32[344,128]{1,0:T(8,128)S(1)} %add.40), channel_id=1, source_target_pairs={{0,2},{1,3},{2,0},{3,1},{4,6},{5,7},{6,4},{7,5},{8,10},{9,11},{10,... | collective-permute-start | bytes 528392 | tf_op jit(solution)/shard_map/ppermute | solution.py:549
  81.8 4.8 %slice-start.3 = ((bf16[27,1,3,16]{3,0,2,1:T(8,128)(2,1)}), bf16[27,1,1,16]{3,0,2,1:T(8,128)(2,1)S(1)}, s32[]{:S(2)}) async-start(bf16[27,1,3,16]{3,0,2,1:T(8,128)(2,1)} %copy-done.5), calls=%async_computation.4 | async-start | bytes 16384 | tf_op jit(solution)/shard_map/jit(_roll_static)/slice | solution.py:543
  86.5 5.6 %collective-permute-start.9 = (f32[344,128]{1,0:T(8,128)S(1)}, f32[344,128]{1,0:T(8,128)S(1)}, u32[]{:S(2)}, u32[]{:S(2)}) collective-permute-start(f32[344,128]{1,0:T(8,128)S(1)} %add.41), channel_id=1, source_target_pairs={{0,14},{1,15},{2,4},{3,5},{4,2},{5,3},{6,8},{7,9},{8,6},{9,7},{10,... | collective-permute-start | bytes 528392 | tf_op jit(solution)/shard_map/ppermute | solution.py:549
  87.1 5.3 %copy-start = (bf16[4,128,128]{2,1,0:T(8,128)(2,1)S(1)}, bf16[4,128,128]{2,1,0:T(8,128)(2,1)}, u32[]{:S(2)}) copy-start(bf16[4,128,128]{2,1,0:T(8,128)(2,1)} %get-tuple-element.14.own_ref) | copy-start | bytes 393220
  92.1 11.5 %collective-permute-start.10 = (f32[344,128]{1,0:T(8,128)S(1)}, f32[344,128]{1,0:T(8,128)S(1)}, u32[]{:S(2)}, u32[]{:S(2)}) collective-permute-start(f32[344,128]{1,0:T(8,128)S(1)} %add.42), channel_id=1, source_target_pairs={{0,6},{1,7},{2,12},{3,13},{4,10},{5,11},{6,0},{7,1},{8,14},{9,15},... | collective-permute-start | bytes 528392 | tf_op jit(solution)/shard_map/ppermute | solution.py:549
  92.4 10.4 %collective-permute-start.5 = (bf16[4,64,128]{2,1,0:T(8,128)(2,1)S(1)}, bf16[4,64,128]{2,1,0:T(8,128)(2,1)S(1)}, u32[]{:S(2)}, u32[]{:S(2)}) collective-permute-start(bf16[4,64,128]{2,1,0:T(8,128)(2,1)S(1)} %get-tuple-element.37), channel_id=1, source_target_pairs={{0,31},{1,0},{2,1},{3,2},{4,3},{5,4},{6,5},{7,6},{8,7},{9,8},{10,9... | collective-permute-start | bytes 196616 | tf_op jit(solution)/shard_map/ppermute | solution.py:549
  96.0 6.7 %copy-start.1 = (f32[2,8,128]{2,1,0:T(8,128)S(1)}, f32[2,8,128]{2,1,0:T(8,128)}, u32[]{:S(2)}) copy-start(f32[2,8,128]{2,1,0:T(8,128)} %get-tuple-element.15.rest_ref) | copy-start | bytes 24580
  96.0 6.7 %collective-permute-start.4 = (bf16[4,64,128]{2,1,0:T(8,128)(2,1)S(1)}, bf16[4,64,128]{2,1,0:T(8,128)(2,1)S(1)}, u32[]{:S(2)}, u32[]{:S(2)}) collective-permute-start(bf16[4,64,128]{2,1,0:T(8,128)(2,1)S(1)} %get-tuple-element.38), channel_id=1, source_target_pairs={{0,1},{1,2},{2,3},{3,4},{4,5},{5,6},{6,7},{7,8},{8,9},{9,10},{10,1... | collective-permute-start | bytes 196616 | tf_op jit(solution)/shard_map/ppermute | solution.py:549
  103.7 1.8 %copy-start.4 = (f32[344,128]{1,0:T(8,128)}, f32[344,128]{1,0:T(8,128)S(1)}, u32[]{:S(2)}) copy-start(f32[344,128]{1,0:T(8,128)S(1)} %add_multiply_fusion) | copy-start | bytes 528388
  105.6 0.7 slice-start
  106.5 0.8 slice-start.1
  107.7 0.9 slice-start.2

commit v2 on v1

--- a/solution.py
+++ b/solution.py
@@ -16,7 +16,8 @@
 HALO = 6
 ROWS = 2 + 2 * HALO
 XP = 10
-PACK_ROWS = 344
+PACK_ROWS = 288
+GROUP = 8
 
 
 def tap_selector():
@@ -58,7 +59,6 @@
 
 
 def build_hidden_band(taps_ref, band_ref):
-    zero = jnp.zeros((16, 128), BF16)
     for d in range(3):
         for t in range(4):
             for a in range(3):
@@ -68,17 +68,10 @@
                     taps.append(pltpu.roll(tap, (16 * (t - 1)) % 128, 1))
                 for y in range(2):
                     for pair in range(2):
-                        tile = band_tile(taps, 2 * pair - y, 16).astype(BF16)
-                        for x in range(2):
-                            row = d * 256 + ((x * 2 + y) * 4 + t) * 16
-                            lane = ((x + a) * 2 + pair) * 128
-                            band_ref[row : row + 16, lane : lane + 128] = tile
-            for y in range(2):
-                for pair in range(2):
-                    for x, far in ((0, 3), (1, 0)):
-                        row = d * 256 + ((x * 2 + y) * 4 + t) * 16
-                        lane = (far * 2 + pair) * 128
-                        band_ref[row : row + 16, lane : lane + 128] = zero
+                        row = d * 128 + (y * 4 + t) * 16
+                        lane = (a * 2 + pair) * 128
+                        tile = band_tile(taps, 2 * pair - y, 16)
+                        band_ref[row : row + 16, lane : lane + 128] = tile.astype(BF16)
 
 
 def build_head_band(taps_ref, band_ref):
@@ -137,7 +130,10 @@
     field_out,
     rest_out,
     window_out,
-    pack_out,
+    partner_out,
+    beyond_out,
+    mine_out,
+    theirs_out,
     nz,
     inp,
     h1,
@@ -158,6 +154,7 @@
     gm,
     gl,
     gf,
+    pack_out,
 ):
     spread = jnp.dot(small_ref[...], selector_ref[...], preferred_element_type=F32)
     for g in range(16):
@@ -205,22 +202,20 @@
         h1[2 * xp + 2, row, :] = out[128:]
         return 0
 
-    lax.fori_loop(0, 24, first_body, 0)
+    lax.fori_loop(0, 24, first_body, 0, unroll=12)
     wrap(h1)
 
     def second_body(step, _):
-        xp = step // 5
+        xl = step // 5
         yp = step % 5
-        window = h1[pl.ds(2 * xp, 4), pl.ds(pl.multiple_of(yp * 128, 128), 256), :].reshape(1024, 256)
+        window = h1[pl.ds(xl, 3), pl.ds(pl.multiple_of(yp * 128, 128), 256), :].reshape(768, 256)
         parts = jnp.dot(w2[...], window, preferred_element_type=F32)
-        out = combine_z(parts, 256)
-        out = jnp.tanh(out.reshape(16, 16, 256) + b2_ref[...][None]).reshape(256, 256).astype(BF16)
-        row = pl.ds(pl.multiple_of(yp * 128, 128), 128)
-        h2[2 * xp + 1, row, :] = out[:128]
-        h2[2 * xp + 2, row, :] = out[128:]
+        out = combine_z(parts, 128)
+        out = jnp.tanh(out.reshape(8, 16, 256) + b2_ref[...][None]).reshape(128, 256)
+        h2[xl + 1, pl.ds(pl.multiple_of(yp * 128, 128), 128), :] = out.astype(BF16)
         return 0
 
-    lax.fori_loop(0, 20, second_body, 0)
+    lax.fori_loop(0, 40, second_body, 0, unroll=20)
     wrap(h2)
 
     top = iota((8, 256), 0) < 4
@@ -242,7 +237,7 @@
                 head[1, 2 * xp + x, row, :] = jnp.where(top, pltpu.roll(lower, 4, 0), upper)
         return 0
 
-    lax.fori_loop(0, 8, head_body, 0)
+    lax.fori_loop(0, 8, head_body, 0, unroll=8)
 
     shape = (32, 256)
     row32 = iota(shape, 0)
@@ -318,7 +313,7 @@
             cm[2 * xp + 1 + x, pl.ds(pl.multiple_of(yp * 128, 128), 128), :] = v.astype(BF16)
         return 0
 
-    lax.fori_loop(0, 8, middle_body, 0)
+    lax.fori_loop(0, 8, middle_body, 0, unroll=8)
     wrap(cm)
 
     def shift_body(xl, _):
@@ -328,19 +323,17 @@
         cmr[2, xl] = roll_z(v, 1).astype(BF16)
         return 0
 
-    lax.fori_loop(0, XP, shift_body, 0)
-
-    def first_cot_body(xp, _):
-        window = cm[pl.ds(2 * xp, 4)].reshape(1024, 256)
+    lax.fori_loop(0, XP, shift_body, 0, unroll=5)
+
+    def first_cot_body(xl, _):
+        window = cm[pl.ds(xl, 3)].reshape(768, 256)
         parts = jnp.dot(w2t[...], window, preferred_element_type=F32)
-        out = combine_z(parts, 256)
-        for x in range(2):
-            hidden = h1[2 * xp + 1 + x, 320:448, :].astype(F32)
-            v = out[128 * x : 128 * x + 128] * (1.0 - hidden * hidden)
-            cf[2 * xp + 1 + x] = v.astype(BF16)
+        out = combine_z(parts, 128)
+        hidden = h1[xl + 1, 320:448, :].astype(F32)
+        cf[xl + 1] = (out * (1.0 - hidden * hidden)).astype(BF16)
         return 0
 
-    lax.fori_loop(0, 4, first_cot_body, 0)
+    lax.fori_loop(0, 8, first_cot_body, 0, unroll=8)
     wrap(cf)
 
     gm[...] = jnp.zeros_like(gm)
@@ -348,16 +341,24 @@
     gf[...] = jnp.zeros_like(gf)
     over_lanes = (((1,), (1,)), ((), ()))
 
-    def grad_body(xl, _):
-        left = cmr[:, pl.ds(xl - 1, 3)].reshape(1152, 256)
-        gm[...] += lax.dot_general(left, h1[xl, 256:512, :], over_lanes, preferred_element_type=F32)
-        left = cl[:, :, pl.ds(xl - 1, 3), 8:16, :].reshape(144, 256).astype(BF16)
-        gl[...] += lax.dot_general(left, h2[xl, 192:448, :], over_lanes, preferred_element_type=F32)
-        left = inp[:, pl.ds(xl - 1, 3), 20:36, :].reshape(144, 256).astype(BF16)
-        gf[...] += lax.dot_general(left, cf[xl], over_lanes, preferred_element_type=F32)
+    def grad_body(step, _):
+        xs = [GROUP * step + 1 + k for k in range(GROUP)]
+
+        def along(parts):
+            return jnp.concatenate(parts, axis=1)
+
+        left = along([cmr[:, pl.ds(x - 1, 3)].reshape(1152, 256) for x in xs])
+        right = along([h1[x, 256:512, :] for x in xs])
+        gm[...] += lax.dot_general(left, right, over_lanes, preferred_element_type=F32)
+        left = along([cl[:, :, pl.ds(x - 1, 3), 8:16, :].reshape(144, 256).astype(BF16) for x in xs])
+        right = along([h2[x, 192:448, :] for x in xs])
+        gl[...] += lax.dot_general(left, right, over_lanes, preferred_element_type=F32)
+        left = along([inp[:, pl.ds(x - 1, 3), 20:36, :].reshape(144, 256).astype(BF16) for x in xs])
+        right = along([cf[x] for x in xs])
+        gf[...] += lax.dot_general(left, right, over_lanes, preferred_element_type=F32)
         return 0
 
-    lax.fori_loop(1, 9, grad_body, 0)
+    lax.fori_loop(0, 8 // GROUP, grad_body, 0)
 
     low = iota((16, 128), 1) < 64
     third = []
@@ -377,7 +378,21 @@
         v1 = pltpu.roll(v1, 64, 1)
         pack_out[g * 16 : g * 16 + 16, :] = u0 + jnp.where(low, v0, v1)
         third.append(u1 + v1)
-    third.append(third[8])
+    v = gf[...]
+    shape = (144, 128)
+    total = jnp.zeros(shape, F32)
+    for y in range(2):
+        for t in range(4):
+            moved = v if y + t == 0 else pltpu.roll(v, 128 - (y * 64 + t * 16), 1)
+            if y:
+                moved = pltpu.roll(moved, 140, 0)
+            total = total + rotate_rows(moved, (t - 1) % 4)
+    total = jnp.where(iota(shape, 1) < 16, total, 0.0)
+    packed = total[:16]
+    for g in range(1, 8):
+        packed = packed + pltpu.roll(total[g * 16 : g * 16 + 16], 16 * g, 1)
+    pack_out[224:240, :] = packed
+    third.append(total[128:144])
     for g in range(5):
         packed = jnp.where(low, third[2 * g], pltpu.roll(third[2 * g + 1], 64, 1))
         pack_out[144 + g * 16 : 160 + g * 16, :] = packed
@@ -398,40 +413,31 @@
     low = iota(shape, 1) < 64
     both = jnp.where(lower_y, r0, jnp.where(low, s0, s1))
     last = jnp.where(lower_y, r1, s1)
-    pack_out[256:304, :] = jnp.zeros((48, 128), F32)
-    pack_out[256:274, :] = both.reshape(18, 8, 128).sum(axis=1)
-    pack_out[280:298, :] = last.reshape(18, 8, 128).sum(axis=1)
-
-    v = gf[...]
-    total = jnp.zeros(shape, F32)
-    for y in range(2):
-        for t in range(4):
-            moved = v if y + t == 0 else pltpu.roll(v, 128 - (y * 64 + t * 16), 1)
-            if y:
-                moved = pltpu.roll(moved, 140, 0)
-            total = total + rotate_rows(moved, (t - 1) % 4)
-    total = jnp.where(iota(shape, 1) < 16, total, 0.0)
-    packed = total[:16]
-    for g in range(1, 8):
-        packed = packed + pltpu.roll(total[g * 16 : g * 16 + 16], 16 * g, 1)
-    pack_out[224:240, :] = packed
-    pack_out[240:256, :] = total[128:144]
-
-    def channel_sum(read, base):
+    pack_out[240:288, :] = jnp.zeros((48, 128), F32)
+    pack_out[240:258, :] = both.reshape(18, 8, 128).sum(axis=1)
+    pack_out[264:282, :] = last.reshape(18, 8, 128).sum(axis=1)
+
+    diagonal = iota((16, 128), 0) == iota((16, 128), 1)
+
+    def channel_sum(read):
         acc = None
         for xl in range(1, 9):
             v = read(xl).astype(F32)
             v = v[:, :128] + v[:, 128:]
             acc = v if acc is None else acc + v
-        acc = acc.reshape(8, 16, 128).sum(axis=0)
-        pack_out[base : base + 16, :] = jnp.broadcast_to(jnp.sum(acc, axis=1, keepdims=True), (16, 128))
-
-    channel_sum(lambda xl: cm[xl, 64:192, :], 304)
-    channel_sum(lambda xl: cf[xl], 320)
-    row8 = iota((8, 128), 0)
-    tile = jnp.where(row8 == 0, jnp.sum(cot_sum[0]), 0.0)
-    tile = jnp.where(row8 == 1, jnp.sum(cot_sum[1]), tile)
-    pack_out[336:344, :] = jnp.where(row8 == 2, jnp.sum(loss), tile)
+        acc = jnp.sum(acc.reshape(8, 16, 128).sum(axis=0), axis=1, keepdims=True)
+        return jnp.sum(jnp.where(diagonal, acc, 0.0), axis=0, keepdims=True)
+
+    pack_out[258:259, :] = channel_sum(lambda xl: cm[xl, 64:192, :])
+    pack_out[259:260, :] = channel_sum(lambda xl: cf[xl])
+    lane = iota((1, 128), 1)
+    row = jnp.where(lane == 0, jnp.sum(cot_sum[0]), 0.0)
+    row = jnp.where(lane == 1, jnp.sum(cot_sum[1]), row)
+    pack_out[260:261, :] = jnp.where(lane == 2, jnp.sum(loss), row)
+    core = place_ref[1]
+    half = PACK_ROWS // 2
+    mine_out[...] = pack_out[pl.ds(pl.multiple_of(core * half, 8), half), :]
+    theirs_out[...] = pack_out[pl.ds(pl.multiple_of((1 - core) * half, 8), half), :]
 
     place = place_ref[0]
     start = 2 * (place % 4)
@@ -445,9 +451,11 @@
         rest_out[x] = pick(own_rest[start + x])
     for x in range(4):
         window_out[x] = pick(cf[start + x])
-
-
-def input_kernel(left_ref, own_ref, right_ref, taps_ref, rest_ref, out_ref, band):
+        partner_out[x] = pick(cf[start + x, pl.ds(pl.multiple_of((1 - core) * 64, 64), 64), :])
+        beyond_out[x] = pick(cf[start + x, pl.ds(pl.multiple_of(core * 64, 64), 64), :])
+
+
+def input_kernel(place_ref, partner_ref, beyond_ref, own_ref, taps_ref, rest_ref, out_ref, band):
     shape = (8, 128)
     upper = iota(shape, 0) < 4
     zero = jnp.zeros(shape, F32)
@@ -468,7 +476,10 @@
                         tiles.append(zero)
                 lane = (window * 2 + pair) * 128
                 band[d * 16 : d * 16 + 16, lane : lane + 128] = jnp.concatenate(tiles, axis=0).astype(BF16)
-    window = jnp.concatenate([left_ref[...], own_ref[...], right_ref[...]], axis=1).reshape(1024, 128)
+    low_core = place_ref[1] == 0
+    left = jnp.where(low_core, beyond_ref[...], partner_ref[...])
+    right = jnp.where(low_core, partner_ref[...], beyond_ref[...])
+    window = jnp.concatenate([left, own_ref[...], right], axis=1).reshape(1024, 128)
     parts = jnp.dot(band[...], window, preferred_element_type=F32)
     out = pltpu.roll(parts[:16], 1, 1) + parts[16:32] + pltpu.roll(parts[32:], 127, 1)
     site = iota(shape, 0) // 4 + iota(shape, 0) % 4 + iota(shape, 1)
@@ -496,12 +507,13 @@
         ((8, 8, 256), F32),
         ((256, 192), BF16),
         ((256, 384), BF16),
-        ((768, 1024), BF16),
-        ((768, 1024), BF16),
+        ((384, 768), BF16),
+        ((384, 768), BF16),
         ((192, 1536), BF16),
         ((1152, 256), F32),
         ((144, 256), F32),
         ((144, 128), F32),
+        ((PACK_ROWS, 128), F32),
     ]
     return pl.pallas_call(
         main_kernel,
@@ -509,24 +521,90 @@
             jax.ShapeDtypeStruct((2, 8, 128), F32),
             jax.ShapeDtypeStruct((2, 8, 128), F32),
             jax.ShapeDtypeStruct((4, 128, 128), BF16),
-            jax.ShapeDtypeStruct((PACK_ROWS, 128), F32),
+            jax.ShapeDtypeStruct((4, 64, 128), BF16),
+            jax.ShapeDtypeStruct((4, 64, 128), BF16),
+            jax.ShapeDtypeStruct((PACK_ROWS // 2, 128), F32),
+            jax.ShapeDtypeStruct((PACK_ROWS // 2, 128), F32),
         ),
         in_specs=[pl.BlockSpec(memory_space=pltpu.SMEM)] + [vmem()] * 9,
-        out_specs=(vmem(), vmem(), vmem(), vmem()),
+        out_specs=(vmem(),) * 7,
         scratch_shapes=[pltpu.VMEM(s, t) for s, t in scratch],
         compiler_params=pltpu.CompilerParams(vmem_limit_bytes=56 * 1024 * 1024),
     )(place, noise, small, selector, taps2, taps2t, taps3, b1, b2, b3)
 
 
-def run_input(left, own, right, taps, rest):
+def run_input(place, partner, beyond, own, taps, rest):
     return pl.pallas_call(
         input_kernel,
         out_shape=jax.ShapeDtypeStruct((2, 8, 128), F32),
-        in_specs=[vmem()] * 5,
+        in_specs=[pl.BlockSpec(memory_space=pltpu.SMEM)] + [vmem()] * 5,
         out_specs=vmem(),
         scratch_shapes=[pltpu.VMEM((48, 1024), BF16)],
         compiler_params=pltpu.CompilerParams(vmem_limit_bytes=16 * 1024 * 1024),
-    )(left, own, right, taps, rest)
+    )(place, partner, beyond, own, taps, rest)
+
+
+def unpack_kernel(scale, place_ref, mine_ref, theirs_ref, loss, first, b1, middle, b2, last, b3, both):
+    core = place_ref[1]
+    half = PACK_ROWS // 2
+    both[pl.ds(pl.multiple_of(core * half, 8), half), :] = mine_ref[...] * scale
+    both[pl.ds(pl.multiple_of((1 - core) * half, 8), half), :] = theirs_ref[...] * scale
+
+    def lanes_from(v, start):
+        return v if start == 0 else pltpu.roll(v, 128 - start, 1)
+
+    for d in range(3):
+        for j in range(3):
+            a = 2 - j
+            g = d * 3 + j
+            most = both[g * 16 : g * 16 + 16, :]
+            third = both[144 + (g // 2) * 16 : 160 + (g // 2) * 16, :]
+            for b in range(3):
+                for c in range(3):
+                    if b < 2:
+                        v = lanes_from(most, b * 64 + c * 16)
+                    else:
+                        v = lanes_from(third, (g % 2) * 64 + c * 16)
+                    middle[a * 27 + b * 9 + c * 3 + d] = v[:, :16]
+    for d in range(3):
+        for a in range(3):
+            g = d * 3 + a
+            if g < 8:
+                v = lanes_from(both[224:240, :], 16 * g)
+            else:
+                v = lanes_from(both[208:224, :], 64)
+            for b in range(3):
+                for c in range(3):
+                    row = b * 4 + c
+                    first[a * 9 + b * 3 + c, d : d + 1, :] = v[row : row + 1, :16]
+    for b in range(3):
+        for c in range(3):
+            if b < 2:
+                v = lanes_from(both[240:264, :], b * 64 + c * 16)
+            else:
+                v = lanes_from(both[264:288, :], c * 16)
+            for d in range(3):
+                for ch in range(2):
+                    for a in range(3):
+                        row = (2 - d) * 6 + ch * 3 + 2 - a
+                        last[a * 27 + b * 9 + c * 3 + d, ch : ch + 1, :] = v[row : row + 1, :16]
+    b2[...] = both[258:259, :16]
+    b1[...] = both[259:260, :16]
+    row = both[260:261, :]
+    b3[...] = row[:, :2]
+    loss[...] = pltpu.roll(row, 126, 1)[:, :1]
+
+
+def run_unpack(scale, place, mine, theirs):
+    shapes = ((1, 1), (27, 3, 16), (1, 16), (81, 16, 16), (1, 16), (81, 2, 16), (1, 2))
+    return pl.pallas_call(
+        functools.partial(unpack_kernel, scale),
+        out_shape=tuple(jax.ShapeDtypeStruct(s, F32) for s in shapes),
+        in_specs=[pl.BlockSpec(memory_space=pltpu.SMEM), vmem(), vmem()],
+        out_specs=(vmem(),) * len(shapes),
+        scratch_shapes=[pltpu.VMEM((PACK_ROWS, 128), F32)],
+        compiler_params=pltpu.CompilerParams(vmem_limit_bytes=16 * 1024 * 1024),
+    )(place, mine, theirs)
 
 
 def pad_taps(v):
@@ -561,8 +639,9 @@
     def chip_after(i):
         return ((((i >> 1) + 1) ^ 1) - 1) % chips * 2 + (i & 1)
 
-    distant = swapped(noise, size_y, far)
     beside = swapped(noise, size_y, lambda i: i ^ 1)
+    near, beside = lax.optimization_barrier((noise, beside))
+    distant = swapped(near, size_y, far)
     block = jnp.concatenate(
         [jnp.where(even, noise, beside), jnp.where(even, beside, noise)], axis=1
     )
@@ -582,7 +661,7 @@
     return lax.all_to_all(sent, "gx", 0, 0, tiled=True).reshape(16, 4 * ROWS, 128)
 
 
-def sum_over_y(v):
+def sum_over_y(mine, theirs):
     size_y = lax.axis_size("gy")
 
     def along_z(partner):
@@ -592,15 +671,15 @@
         return f
 
     crossing = (3, 6, 5, 0, 7, 2, 1, 4)
+    v = mine + swapped(theirs, size_y, lambda i: i ^ 1)
     for partner in (
-        lambda i: i ^ 1,
         lambda i: i ^ 16,
         along_z(lambda z: z ^ 1),
         along_z(lambda z: (((z + 1) ^ 1) - 1) % 8),
         along_z(lambda z: crossing[z]),
     ):
         v = v + swapped(v, size_y, partner)
-    return v
+    return v, swapped(v, size_y, lambda i: i ^ 1)
 
 
 def local(noise, w_first, b_first, w_middle, b_middle, w_last, b_last):
@@ -622,8 +701,8 @@
     tapsd = jnp.concatenate([tapsd, tapsd], axis=1)
 
     gathered = gather_noise(noise)
-    place = lax.axis_index("gx").astype(jnp.int32).reshape(1)
-    field, rest, window, pack = run_main(
+    place = jnp.stack([lax.axis_index("gx"), lax.axis_index("gy") % 2]).astype(jnp.int32)
+    field, rest, window, to_partner, to_beyond, mine, theirs = run_main(
         place,
         gathered,
         small,
@@ -635,31 +714,22 @@
         b_middle.reshape(16, 1),
         jnp.repeat(b_last, 4).reshape(8, 1),
     )
-    left = swapped(window[:, 64:], size_y, lambda i: (i + 1) % size_y)
-    right = swapped(window[:, :64], size_y, lambda i: (i - 1) % size_y)
-    noise_grad = run_input(left, window, right, tapsd, rest)
-
-    total = sum_over_y(pack) * (1.0 / sites)
-    most = total[:144].reshape(3, 3, 16, 2, 4, 16)
-    third = total[144:224].reshape(5, 16, 2, 4, 16)
-    third = jnp.transpose(third, (0, 2, 1, 3, 4)).reshape(10, 16, 4, 16)[:9].reshape(3, 3, 16, 1, 4, 16)
-    middle = jnp.concatenate([most, third], axis=3)[:, ::-1, :, :, :3]
-    grad_middle = jnp.transpose(middle, (2, 5, 1, 3, 4, 0))
-    first = jnp.concatenate([total[224:240], total[240:256, :16]], axis=1).reshape(4, 4, 3, 3, 16)
-    grad_first = jnp.transpose(first[:3, :3], (4, 3, 0, 1, 2))[:, None]
-    last = jnp.concatenate([total[256:274], total[280:298, :64]], axis=1)
-    last = last.reshape(3, 2, 3, 3, 4, 16)[::-1, :, ::-1, :, :3]
-    grad_last = jnp.transpose(last, (1, 5, 2, 3, 4, 0))
+    partner = swapped(to_partner, size_y, lambda i: i ^ 1)
+    beyond = swapped(to_beyond, size_y, lambda i: (((i + 1) ^ 1) - 1) % size_y)
+    noise_grad = run_input(place, partner, beyond, window, tapsd, rest)
+
+    mine, theirs = sum_over_y(mine, theirs)
+    loss, first, b1, middle, b2, last, b3 = run_unpack(1.0 / sites, place, mine, theirs)
     return (
         field.reshape(noise.shape),
         noise_grad.reshape(noise.shape),
-        total[338, 0],
-        grad_first,
-        total[320:336, 0],
-        grad_middle,
-        total[304:320, 0],
-        grad_last,
-        total[336:338, 0],
+        loss.reshape(()),
+        jnp.transpose(first.reshape(3, 3, 3, 3, 16), (4, 0, 1, 2, 3))[:, None],
+        b1.reshape(16),
+        jnp.transpose(middle.reshape(3, 3, 3, 3, 16, 16), (4, 5, 0, 1, 2, 3)),
+        b2.reshape(16),
+        jnp.transpose(last.reshape(3, 3, 3, 3, 2, 16), (4, 5, 0, 1, 2, 3)),
+        b3.reshape(2),
     )
 
 

time: 111 us -> 83.1 us (0.75)
  Pallas kernels: 37.5 us -> 21 us
  waiting for transfers between devices: 28.2 us -> 12.3 us
  starting transfers between devices: 24 us -> 31.9 us
  local copies, waits for them, and re-layouts: 16.3 us -> 13 us
    pallas_call x1, Pallas kernels: 36.6 us -> 18 us  [run_main(): pl.pallas_call(main_kernel, out_shape=(jax.ShapeDtypeStruct((2, 8, 128),...]
    ppermute x11 -> x12, waiting for transfers between devices: 26.5 us -> 12.3 us  [swapped(): return lax.ppermute(v, 'gy', [(i, partner(i)) for i in range(axis_size)])]
    ppermute x11 -> x12, starting transfers between devices: 17.6 us -> 25.6 us  [swapped(): return lax.ppermute(v, 'gy', [(i, partner(i)) for i in range(axis_size)])]
    slice x14 -> x0, local copies, waits for them, and re-layouts: 2.84 us -> none  [the longest x2 0.85 us: local(): most = total[:144].reshape(3, 3, 16, 2, 4, 16)]
    all_to_all x1, waiting for transfers between devices: 1.7 us -> 0.01 us  [gather_noise(): lax.all_to_all(sent, 'gx', 0, 0, tiled=True).reshape(16, 4 * ROWS, 128)]
    pallas_call x0 -> x1, Pallas kernels: none -> 1.62 us  [run_unpack(): pl.pallas_call(functools.partial(unpack_kernel, scale), out_shape=tuple((...]
    transpose x2 -> x0, local copies, waits for them, and re-layouts: 1.55 us -> none  [the longest x1 0.88 us: local(): grad_middle = jnp.transpose(middle, (2, 5, 1, 3, 4, 0))]
    unnamed x34 -> x36, local copies, waits for them, and re-layouts: 3.7 us -> 5.25 us
  transfers between devices with their start and end apart: 12 -> 13, of which waited for: 8 -> 7; matrix products, arithmetic and copies ran while one was open for 9% -> 12% of each run, Pallas kernels for 1% -> 2%
where the time goes in v2:
time: 83.1 us; the launch traced here: 82.6 us
  starting transfers between devices  31.9 us (38%)
  Pallas kernels  21 us (25%)
  local copies, waits for them, and re-layouts  13 us (16%)
  waiting for transfers between devices  12.3 us (15%)
  other arithmetic  3.36 us (4%)
  between operations  1.01 us (1%)
    ppermute x12, starting transfers between devices, swapped(): return lax.ppermute(v, 'gy', [(i, partner(i)) for i in range(axis_size)])  25.6 us
    pallas_call x1, Pallas kernels, run_main(): pl.pallas_call(main_kernel, out_shape=(jax.ShapeDtypeStruct((2, 8, 128),...  18 us
    ppermute x12, waiting for transfers between devices, swapped(): return lax.ppermute(v, 'gy', [(i, partner(i)) for i in range(axis_size)])  12.3 us
    all_to_all x1, starting transfers between devices, gather_noise(): lax.all_to_all(sent, 'gx', 0, 0, tiled=True).reshape(16, 4 * ROWS, 128)  6.36 us
    unnamed x36, local copies, waits for them, and re-layouts  5.25 us
  transfers between devices with their start and end apart: 13, of which 7 were waited for; matrix products, arithmetic and copies ran while one was open for 12% of the time, Pallas kernels for 2%

profile of v2, /device:TPU:1, one launch (start us, length us, event | category | flops | bytes accessed | tf_op | source)
XLA Modules:
  0.0 82.6 jit_solution(2487797001800631264)
XLA Ops:
  0.7 3.3 %collective-permute-start = (f32[2,2,4,128]{3,2,1,0:T(4,128)}, f32[2,2,4,128]{3,2,1,0:T(4,128)S(1)}, u32[]{:S(2)}, u32[]{:S(2)}) collective-permute-start(f32[2,2,4,128]{3,2,1,0:T(4,128)} %param.8), channel_id=1, source_target_pairs={{0,1},{1,0},{2,3},{3,2},{4,5},{5,4},{6,7},{7,6},{8,9},{9,8},{10,11... | collective-permute-start | bytes 24584 | tf_op jit(solution)/shard_map/ppermute | solution.py:627
  4.0 0.8 copy.50
  5.2 0.5 pad_maximum_fusion
  5.7 0.3 copy-done.6
  6.2 0.6 copy-done.7
  7.0 0.6 copy-done.9
  7.6 1.2 %collective-permute-start.1 = (f32[2,2,4,128]{3,2,1,0:T(4,128)S(1)}, f32[2,2,4,128]{3,2,1,0:T(4,128)S(1)}, u32[]{:S(2)}, u32[]{:S(2)}) collective-permute-start(f32[2,2,4,128]{3,2,1,0:T(4,128)S(1)} %copy-done.9), channel_id=1, source_target_pairs={{0,29},{1,4},{2,31},{3,6},{4,1},{5,8},{6,3},{7,10},{8,5},{9,12},{1... | collective-permute-start | bytes 24584 | tf_op jit(solution)/shard_map/ppermute | solution.py:627
  8.7 3.8 %collective-permute-start.2 = (f32[2,4,4,128]{3,2,1,0:T(4,128)S(1)}, f32[2,4,4,128]{3,2,1,0:T(4,128)S(1)}, u32[]{:S(2)}, u32[]{:S(2)}) collective-permute-start(f32[2,4,4,128]{3,2,1,0:T(4,128)S(1)} %pad_maximum_fusion.6), channel_id=1, source_target_pairs={{0,30},{1,31},{2,4},{3,5},{4,2},{5,3},{6,8},{7,9},{8,6},{9,7},{10,... | collective-permute-start | bytes 49160 | tf_op jit(solution)/shard_map/ppermute | solution.py:627
  12.5 0.8 collective-permute-start.3
  13.3 0.6 collective-permute-done.2
  14.0 1.2 %collective-permute-done.3 = f32[2,4,4,128]{3,2,1,0:T(4,128)S(1)} collective-permute-done((f32[2,4,4,128]{3,2,1,0:T(4,128)S(1)}, f32[2,4,4,128]{3,2,1,0:T(4,128)S(1)}, u32[]{:S(2)}, u32[]{:S(2)}) %collective-permute-start.3) | collective-permute-done | bytes 16416 | tf_op jit(solution)/shard_map/ppermute | solution.py:627
  15.2 0.8 broadcast_in_dim.11
  16.0 6.4 %all-to-all-start = ((f32[8,2,56,128]{3,2,1,0:T(8,128)}), f32[8,2,56,128]{3,2,1,0:T(8,128)S(1)}, u32[]{:S(2)}, u32[]{:S(2)}) async-start(f32[8,2,56,128]{3,2,1,0:T(8,128)} %broadcast_in_dim.11), calls=%async_computation | async-start | bytes 917504 | tf_op jit(solution)/shard_map/all_to_all | solution.py:661
  22.6 0.2 copy.66
  22.8 0.6 pad.21.small_ref
  23.4 0.3 pad.22.clone
  23.7 0.2 reshape.98
  24.0 0.3 copy.67
  24.2 0.3 pad.23.clone
  24.5 0.2 reshape.99
  24.7 0.3 copy.51
  25.2 0.7 copy-done.10
  25.8 0.7 copy.54.b1_ref
  26.5 0.7 copy-done.11
  27.2 0.7 copy.55.b2_ref
  27.9 0.7 reshape_reshape.4.b3_ref
  28.7 0.6 pad_add_fusion.place_ref
  29.2 0.7 pad_maximum_fusion.3.taps3_ref
  29.9 0.8 pad_maximum_fusion.1
  30.8 0.8 copy-done.3
  31.5 18.0 %shard_map.151 = (f32[2,8,128]{2,1,0:T(8,128)}, f32[2,8,128]{2,1,0:T(8,128)}, bf16[4,128,128]{2,1,0:T(8,128)(2,1)}, bf16[4,64,128]{2,1,0:T(8,128)(2,1)}, bf16[4,...) custom-call(s32[2]{0:T(128)} %pad_add_fusion.place_ref, f32[16,56,128]{2,1,0:T(8,128)} %bitcast.61, ...), custom_call_target="tpu_custom_call" | custom-call | tf_op jit(solution)/shard_map/pallas_call | solution.py:518
  49.5 5.3 %collective-permute-start.6 = (f32[144,128]{1,0:T(8,128)}, f32[144,128]{1,0:T(8,128)S(1)}, u32[]{:S(2)}, u32[]{:S(2)}) collective-permute-start(f32[144,128]{1,0:T(8,128)} %get-tuple-element.33), channel_id=1, source_target_pairs={{0,1},{1,0},{2,3},{3,2},{4,5},{5,4},{6,7},{7,6},{8,9},{9,8},{10,11... | collective-permute-start | bytes 221192 | tf_op jit(solution)/shard_map/ppermute | solution.py:627
  54.9 1.0 %collective-permute-done.6 = f32[144,128]{1,0:T(8,128)S(1)} collective-permute-done((f32[144,128]{1,0:T(8,128)}, f32[144,128]{1,0:T(8,128)S(1)}, u32[]{:S(2)}, u32[]{:S(2)}) %collective-permute-start.6) | collective-permute-done | bytes 73760 | tf_op jit(solution)/shard_map/ppermute | solution.py:627
  56.3 3.0 %collective-permute-done.7 = f32[144,128]{1,0:T(8,128)S(1)} collective-permute-done((f32[144,128]{1,0:T(8,128)S(1)}, f32[144,128]{1,0:T(8,128)S(1)}, u32[]{:S(2)}, u32[]{:S(2)}) %collective-permute-start.7) | collective-permute-done | bytes 73760 | tf_op jit(solution)/shard_map/ppermute | solution.py:627
  59.6 3.0 %collective-permute-done.8 = f32[144,128]{1,0:T(8,128)S(1)} collective-permute-done((f32[144,128]{1,0:T(8,128)S(1)}, f32[144,128]{1,0:T(8,128)S(1)}, u32[]{:S(2)}, u32[]{:S(2)}) %collective-permute-start.8) | collective-permute-done | bytes 73760 | tf_op jit(solution)/shard_map/ppermute | solution.py:627
  62.5 1.1 %collective-permute-start.9 = (f32[144,128]{1,0:T(8,128)S(1)}, f32[144,128]{1,0:T(8,128)S(1)}, u32[]{:S(2)}, u32[]{:S(2)}) collective-permute-start(f32[144,128]{1,0:T(8,128)S(1)} %add.42), channel_id=1, source_target_pairs={{0,14},{1,15},{2,4},{3,5},{4,2},{5,3},{6,8},{7,9},{8,6},{9,7},{10,... | collective-permute-start | bytes 221192 | tf_op jit(solution)/shard_map/ppermute | solution.py:627
  63.7 3.4 %collective-permute-done.9 = f32[144,128]{1,0:T(8,128)S(1)} collective-permute-done((f32[144,128]{1,0:T(8,128)S(1)}, f32[144,128]{1,0:T(8,128)S(1)}, u32[]{:S(2)}, u32[]{:S(2)}) %collective-permute-start.9) | collective-permute-done | bytes 73760 | tf_op jit(solution)/shard_map/ppermute | solution.py:627
  67.1 0.2 collective-permute-start.10
  67.5 0.4 copy-done.13
  67.9 3.8 %collective-permute-start.4 = (bf16[4,64,128]{2,1,0:T(8,128)(2,1)S(1)}, bf16[4,64,128]{2,1,0:T(8,128)(2,1)S(1)}, u32[]{:S(2)}, u32[]{:S(2)}) collective-permute-start(bf16[4,64,128]{2,1,0:T(8,128)(2,1)S(1)} %copy-done.13), channel_id=1, source_target_pairs={{0,1},{1,0},{2,3},{3,2},{4,5},{5,4},{6,7},{7,6},{8,9},{9,8},{10,11... | collective-permute-start | bytes 196616 | tf_op jit(solution)/shard_map/ppermute | solution.py:627
  71.7 0.9 %collective-permute-start.5 = (bf16[4,64,128]{2,1,0:T(8,128)(2,1)S(1)}, bf16[4,64,128]{2,1,0:T(8,128)(2,1)S(1)}, u32[]{:S(2)}, u32[]{:S(2)}) collective-permute-start(bf16[4,64,128]{2,1,0:T(8,128)(2,1)S(1)} %copy-done.12), channel_id=1, source_target_pairs={{0,31},{1,2},{2,1},{3,4},{4,3},{5,6},{6,5},{7,8},{8,7},{9,10},{10,... | collective-permute-start | bytes 196616 | tf_op jit(solution)/shard_map/ppermute | solution.py:627
  72.8 5.0 %collective-permute-start.11 = (f32[144,128]{1,0:T(8,128)S(1)}, f32[144,128]{1,0:T(8,128)S(1)}, u32[]{:S(2)}, u32[]{:S(2)}) collective-permute-start(f32[144,128]{1,0:T(8,128)S(1)} %add.44.mine_ref), channel_id=1, source_target_pairs={{0,1},{1,0},{2,3},{3,2},{4,5},{5,4},{6,7},{7,6},{8,9},{9,8},{10,11... | collective-permute-start | bytes 221192 | tf_op jit(solution)/shard_map/ppermute | solution.py:627
  77.8 0.4 maximum_maximum_fusion.taps_ref
  78.3 0.2 copy-done.1
  78.5 0.4 copy-done.2
  78.9 1.4 %shard_map.152 = f32[2,8,128]{2,1,0:T(8,128)} custom-call(s32[2]{0:T(128)S(1)} %copy-done.2, bf16[4,64,128]{2,1,0:T(8,128)(2,1)S(1)} %collective-permute-done.4.partner_ref, bf16[4,64,128]{2,1,0:T(8,128)(2,1)S(1)} %collective-permute-done.5.beyond_ref, bf16[4,128,128]{2,1,0:T(8,128)(2,1)S(1)} %copy-done, ...), custom_call_target="tpu_custom_call" | custom-call | tf_op jit(solution)/shard_map/pallas_call | solution.py:537
  80.3 1.6 %shard_map.153 = (f32[1,1]{1,0:T(1,128)}, f32[27,3,16]{2,1,0:T(4,128)S(1)}, f32[1,16]{1,0:T(1,128)}, f32[81,16,16]{2,1,0:T(8,128)}, f32[1,16]{1,0:T(1,128)}, /*index=5*/f32[81,2,16]{2,1,0:T(2,128)}, f32[1,2]{1,0:T(1,128)}) custom-call(s32[2]{0:T(128)S(1)} %copy-done.2, f32[144,128]{1,0:T(8,128)S(1)} %add.44.mine_ref, ...), custom_call_target="tpu_custom_call" | custom-call | tf_op jit(solution)/shard_map/pallas_call | solution.py:600
  81.9 0.6 broadcast_in_dim.13
  (74 shorter events, 2.5 us)
Async XLA Ops:
  0.6 4.3 %copy-start.4 = (bf16[16,16,3,3,3,3]{1,0,5,4,3,2:T(8,128)(2,1)S(1)}, bf16[16,16,3,3,3,3]{1,0,5,4,3,2:T(8,128)(2,1)}, u32[]{:S(2)}) copy-start(bf16[16,16,3,3,3,3]{1,0,5,4,3,2:T(8,128)(2,1)} %param.11) | copy-start | bytes 124420
  0.7 6.3 %collective-permute-start = (f32[2,2,4,128]{3,2,1,0:T(4,128)}, f32[2,2,4,128]{3,2,1,0:T(4,128)S(1)}, u32[]{:S(2)}, u32[]{:S(2)}) collective-permute-start(f32[2,2,4,128]{3,2,1,0:T(4,128)} %param.8), channel_id=1, source_target_pairs={{0,1},{1,0},{2,3},{3,2},{4,5},{5,4},{6,7},{7,6},{8,9},{9,8},{10,11... | collective-permute-start | bytes 24584 | tf_op jit(solution)/shard_map/ppermute | solution.py:627
  5.2 0.8 copy-start.6
  6.1 0.7 copy-start.7
  6.9 0.7 copy-start.9
  7.6 5.7 %collective-permute-start.1 = (f32[2,2,4,128]{3,2,1,0:T(4,128)S(1)}, f32[2,2,4,128]{3,2,1,0:T(4,128)S(1)}, u32[]{:S(2)}, u32[]{:S(2)}) collective-permute-start(f32[2,2,4,128]{3,2,1,0:T(4,128)S(1)} %copy-done.9), channel_id=1, source_target_pairs={{0,29},{1,4},{2,31},{3,6},{4,1},{5,8},{6,3},{7,10},{8,5},{9,12},{1... | collective-permute-start | bytes 24584 | tf_op jit(solution)/shard_map/ppermute | solution.py:627
  8.7 5.2 %collective-permute-start.2 = (f32[2,4,4,128]{3,2,1,0:T(4,128)S(1)}, f32[2,4,4,128]{3,2,1,0:T(4,128)S(1)}, u32[]{:S(2)}, u32[]{:S(2)}) collective-permute-start(f32[2,4,4,128]{3,2,1,0:T(4,128)S(1)} %pad_maximum_fusion.6), channel_id=1, source_target_pairs={{0,30},{1,31},{2,4},{3,5},{4,2},{5,3},{6,8},{7,9},{8,6},{9,7},{10,... | collective-permute-start | bytes 49160 | tf_op jit(solution)/shard_map/ppermute | solution.py:627
  12.5 2.6 %collective-permute-start.3 = (f32[2,4,4,128]{3,2,1,0:T(4,128)S(1)}, f32[2,4,4,128]{3,2,1,0:T(4,128)S(1)}, u32[]{:S(2)}, u32[]{:S(2)}) collective-permute-start(f32[2,4,4,128]{3,2,1,0:T(4,128)S(1)} %pad_maximum_fusion.6), channel_id=1, source_target_pairs={{0,2},{1,3},{2,0},{3,1},{4,6},{5,7},{6,4},{7,5},{8,10},{9,11},{10,... | collective-permute-start | bytes 49160 | tf_op jit(solution)/shard_map/ppermute | solution.py:627
  16.0 14.8 %all-to-all-start = ((f32[8,2,56,128]{3,2,1,0:T(8,128)}), f32[8,2,56,128]{3,2,1,0:T(8,128)S(1)}, u32[]{:S(2)}, u32[]{:S(2)}) async-start(f32[8,2,56,128]{3,2,1,0:T(8,128)} %broadcast_in_dim.11), calls=%async_computation | async-start | bytes 917504 | tf_op jit(solution)/shard_map/all_to_all | solution.py:661
  25.2 0.7 copy-start.10
  26.5 0.7 copy-start.11
  27.2 0.7 copy-start.14
  28.6 35.0 %copy-start.5 = (bf16[27,1,3,16]{3,0,2,1:T(8,128)(2,1)}, bf16[27,1,3,16]{3,0,2,1:T(8,128)(2,1)S(1)}, u32[]{:S(2)}) copy-start(bf16[27,1,3,16]{3,0,2,1:T(8,128)(2,1)S(1)} %reshape.105) | copy-start | bytes 7780
  30.8 0.8 copy-start.3
  49.5 6.4 %copy-start.8 = (f32[144,128]{1,0:T(8,128)S(1)}, f32[144,128]{1,0:T(8,128)}, u32[]{:S(2)}) copy-start(f32[144,128]{1,0:T(8,128)} %get-tuple-element.32) | copy-start | bytes 221188
  49.5 6.4 %collective-permute-start.6 = (f32[144,128]{1,0:T(8,128)}, f32[144,128]{1,0:T(8,128)S(1)}, u32[]{:S(2)}, u32[]{:S(2)}) collective-permute-start(f32[144,128]{1,0:T(8,128)} %get-tuple-element.33), channel_id=1, source_target_pairs={{0,1},{1,0},{2,3},{3,2},{4,5},{5,4},{6,7},{7,6},{8,9},{9,8},{10,11... | collective-permute-start | bytes 221192 | tf_op jit(solution)/shard_map/ppermute | solution.py:627
  55.9 3.3 %collective-permute-start.7 = (f32[144,128]{1,0:T(8,128)S(1)}, f32[144,128]{1,0:T(8,128)S(1)}, u32[]{:S(2)}, u32[]{:S(2)}) collective-permute-start(f32[144,128]{1,0:T(8,128)S(1)} %add.40), channel_id=1, source_target_pairs={{0,16},{1,17},{2,18},{3,19},{4,20},{5,21},{6,22},{7,23},{8,24},{9,... | collective-permute-start | bytes 221192 | tf_op jit(solution)/shard_map/ppermute | solution.py:627
  59.2 3.3 %collective-permute-start.8 = (f32[144,128]{1,0:T(8,128)S(1)}, f32[144,128]{1,0:T(8,128)S(1)}, u32[]{:S(2)}, u32[]{:S(2)}) collective-permute-start(f32[144,128]{1,0:T(8,128)S(1)} %add.41), channel_id=1, source_target_pairs={{0,2},{1,3},{2,0},{3,1},{4,6},{5,7},{6,4},{7,5},{8,10},{9,11},{10,... | collective-permute-start | bytes 221192 | tf_op jit(solution)/shard_map/ppermute | solution.py:627
  62.5 4.5 %collective-permute-start.9 = (f32[144,128]{1,0:T(8,128)S(1)}, f32[144,128]{1,0:T(8,128)S(1)}, u32[]{:S(2)}, u32[]{:S(2)}) collective-permute-start(f32[144,128]{1,0:T(8,128)S(1)} %add.42), channel_id=1, source_target_pairs={{0,14},{1,15},{2,4},{3,5},{4,2},{5,3},{6,8},{7,9},{8,6},{9,7},{10,... | collective-permute-start | bytes 221192 | tf_op jit(solution)/shard_map/ppermute | solution.py:627
  63.7 3.6 %slice-start = ((bf16[27,1,3,16]{3,0,2,1:T(8,128)(2,1)}), bf16[27,1,1,16]{3,0,2,1:T(8,128)(2,1)S(1)}, s32[]{:S(2)}) async-start(bf16[27,1,3,16]{3,0,2,1:T(8,128)(2,1)} %copy-done.5), calls=%async_computation.1 | async-start | bytes 16384 | tf_op jit(solution)/shard_map/jit(_roll_static)/slice | solution.py:621
  67.1 0.8 %copy-start.13 = (bf16[4,64,128]{2,1,0:T(8,128)(2,1)S(1)}, bf16[4,64,128]{2,1,0:T(8,128)(2,1)}, u32[]{:S(2)}) copy-start(bf16[4,64,128]{2,1,0:T(8,128)(2,1)} %get-tuple-element.28) | copy-start | bytes 196612
  67.1 4.6 %copy-start.12 = (bf16[4,64,128]{2,1,0:T(8,128)(2,1)S(1)}, bf16[4,64,128]{2,1,0:T(8,128)(2,1)}, u32[]{:S(2)}) copy-start(bf16[4,64,128]{2,1,0:T(8,128)(2,1)} %get-tuple-element.29) | copy-start | bytes 196612
  67.1 5.7 %collective-permute-start.10 = (f32[144,128]{1,0:T(8,128)S(1)}, f32[144,128]{1,0:T(8,128)S(1)}, u32[]{:S(2)}, u32[]{:S(2)}) collective-permute-start(f32[144,128]{1,0:T(8,128)S(1)} %add.43), channel_id=1, source_target_pairs={{0,6},{1,7},{2,12},{3,13},{4,10},{5,11},{6,0},{7,1},{8,14},{9,15},... | collective-permute-start | bytes 221192 | tf_op jit(solution)/shard_map/ppermute | solution.py:627
  67.9 10.3 %collective-permute-start.4 = (bf16[4,64,128]{2,1,0:T(8,128)(2,1)S(1)}, bf16[4,64,128]{2,1,0:T(8,128)(2,1)S(1)}, u32[]{:S(2)}, u32[]{:S(2)}) collective-permute-start(bf16[4,64,128]{2,1,0:T(8,128)(2,1)S(1)} %copy-done.13), channel_id=1, source_target_pairs={{0,1},{1,0},{2,3},{3,2},{4,5},{5,4},{6,7},{7,6},{8,9},{9,8},{10,11... | collective-permute-start | bytes 196616 | tf_op jit(solution)/shard_map/ppermute | solution.py:627
  71.7 6.6 %copy-start = (bf16[4,128,128]{2,1,0:T(8,128)(2,1)S(1)}, bf16[4,128,128]{2,1,0:T(8,128)(2,1)}, u32[]{:S(2)}) copy-start(bf16[4,128,128]{2,1,0:T(8,128)(2,1)} %get-tuple-element.30.own_ref) | copy-start | bytes 393220
  71.7 6.5 %collective-permute-start.5 = (bf16[4,64,128]{2,1,0:T(8,128)(2,1)S(1)}, bf16[4,64,128]{2,1,0:T(8,128)(2,1)S(1)}, u32[]{:S(2)}, u32[]{:S(2)}) collective-permute-start(bf16[4,64,128]{2,1,0:T(8,128)(2,1)S(1)} %copy-done.12), channel_id=1, source_target_pairs={{0,31},{1,2},{2,1},{3,4},{4,3},{5,6},{6,5},{7,8},{8,7},{9,10},{10,... | collective-permute-start | bytes 196616 | tf_op jit(solution)/shard_map/ppermute | solution.py:627
  72.8 7.5 %collective-permute-start.11 = (f32[144,128]{1,0:T(8,128)S(1)}, f32[144,128]{1,0:T(8,128)S(1)}, u32[]{:S(2)}, u32[]{:S(2)}) collective-permute-start(f32[144,128]{1,0:T(8,128)S(1)} %add.44.mine_ref), channel_id=1, source_target_pairs={{0,1},{1,0},{2,3},{3,2},{4,5},{5,4},{6,7},{7,6},{8,9},{9,8},{10,11... | collective-permute-start | bytes 221192 | tf_op jit(solution)/shard_map/ppermute | solution.py:627
  77.8 0.7 copy-start.1
  78.3 0.7 copy-start.2

commit v3 on v2

--- a/solution.py
+++ b/solution.py
@@ -117,7 +117,6 @@
 
 
 def main_kernel(
-    place_ref,
     noise_ref,
     small_ref,
     selector_ref,
@@ -127,8 +126,7 @@
     b1_ref,
     b2_ref,
     b3_ref,
-    field_out,
-    rest_out,
+    parts_out,
     window_out,
     partner_out,
     beyond_out,
@@ -144,8 +142,7 @@
     cl,
     head,
     phi,
-    own_field,
-    own_rest,
+    own_parts,
     w1,
     wl,
     w2,
@@ -155,7 +152,21 @@
     gl,
     gf,
     pack_out,
+    raw,
+    raw_sem,
 ):
+    arriving = pltpu.make_async_copy(noise_ref, raw, raw_sem)
+    arriving.start()
+
+    def column(ref, rows, repeats):
+        shape = (rows * repeats, rows)
+        match = iota(shape, 0) // repeats == iota(shape, 1)
+        return jnp.sum(jnp.where(match, ref[...], 0.0), axis=1, keepdims=True)
+
+    b1 = column(b1_ref, 16, 1)
+    b2 = column(b2_ref, 16, 1)
+    b3 = column(b3_ref, 2, 4)
+
     spread = jnp.dot(small_ref[...], selector_ref[...], preferred_element_type=F32)
     for g in range(16):
         piece = spread[:, g * 64 : (g + 1) * 64]
@@ -169,12 +180,14 @@
     build_hidden_band(taps2t_ref, w2t)
     build_head_band(taps3_ref, w3)
 
+    arriving.wait()
+
     rows_in = 4 * ROWS
     shape = (rows_in, 256)
     site = iota(shape, 0) // 4 + iota(shape, 0) % 4 + iota(shape, 1) % 128
     even = site % 2
     for xl in range(8):
-        v = jnp.concatenate([noise_ref[xl], noise_ref[xl + 8]], axis=1)
+        v = jnp.concatenate([raw[xl], raw[xl + 8]], axis=1).astype(F32)
         nz[xl + 1] = v
         if xl == 7:
             nz[0] = swap_halves(v)
@@ -196,7 +209,7 @@
         window = inp[:, pl.ds(2 * xp, 4), pl.ds(pl.multiple_of(8 * yp, 8), 16), :]
         window = window.reshape(192, 256).astype(BF16)
         out = jnp.dot(w1[...], window, preferred_element_type=F32)
-        out = jnp.tanh(out.reshape(16, 16, 256) + b1_ref[...][None]).reshape(256, 256).astype(BF16)
+        out = jnp.tanh(out.reshape(16, 16, 256) + b1[None]).reshape(256, 256).astype(BF16)
         row = pl.ds(pl.multiple_of(yp * 128, 128), 128)
         h1[2 * xp + 1, row, :] = out[:128]
         h1[2 * xp + 2, row, :] = out[128:]
@@ -211,7 +224,7 @@
         window = h1[pl.ds(xl, 3), pl.ds(pl.multiple_of(yp * 128, 128), 256), :].reshape(768, 256)
         parts = jnp.dot(w2[...], window, preferred_element_type=F32)
         out = combine_z(parts, 128)
-        out = jnp.tanh(out.reshape(8, 16, 256) + b2_ref[...][None]).reshape(128, 256)
+        out = jnp.tanh(out.reshape(8, 16, 256) + b2[None]).reshape(128, 256)
         h2[xl + 1, pl.ds(pl.multiple_of(yp * 128, 128), 128), :] = out.astype(BF16)
         return 0
 
@@ -226,7 +239,7 @@
         window = h2[pl.ds(2 * xp, 4), pl.ds(pl.multiple_of(yq * 256, 256), 384), :].reshape(1536, 256)
         parts = jnp.dot(w3[...], window, preferred_element_type=F32)
         out = combine_z(parts, 64)
-        out = (out.reshape(8, 8, 256) + b3_ref[...][None]).reshape(64, 256)
+        out = (out.reshape(8, 8, 256) + b3[None]).reshape(64, 256)
         for x in range(2):
             for pair in range(2):
                 base = x * 32 + pair * 16
@@ -287,9 +300,9 @@
         )
         d_scale = (force * noise * growth - 1.0) * (1.0 - log_scale * log_scale)
         pair = (jnp.where(frozen, 0.0, d_scale), jnp.where(frozen, 0.0, force))
-        rest = force * jnp.where(frozen, 1.0, growth) - noise
-        own_field[xl] = here[12:20]
-        own_rest[xl] = rest[12:20]
+        own_parts[0, xl] = growth[12:20]
+        own_parts[1, xl] = head[1, xl][12:20]
+        own_parts[2, xl] = (upward + downward)[12:20]
         for ch in range(2):
             v = pltpu.roll(pair[ch], 28, 0)[:24].astype(BF16).astype(F32)
             cot_sum[ch] = cot_sum[ch] + v[8:16]
@@ -434,12 +447,12 @@
     row = jnp.where(lane == 0, jnp.sum(cot_sum[0]), 0.0)
     row = jnp.where(lane == 1, jnp.sum(cot_sum[1]), row)
     pack_out[260:261, :] = jnp.where(lane == 2, jnp.sum(loss), row)
-    core = place_ref[1]
+    core = lax.rem(lax.axis_index("gy"), 2)
     half = PACK_ROWS // 2
     mine_out[...] = pack_out[pl.ds(pl.multiple_of(core * half, 8), half), :]
     theirs_out[...] = pack_out[pl.ds(pl.multiple_of((1 - core) * half, 8), half), :]
 
-    place = place_ref[0]
+    place = lax.axis_index("gx")
     start = 2 * (place % 4)
     high = place >= 4
 
@@ -447,15 +460,17 @@
         return jnp.where(high, v[:, 128:], v[:, :128])
 
     for x in range(2):
-        field_out[x] = pick(own_field[start + x])
-        rest_out[x] = pick(own_rest[start + x])
+        for k in range(3):
+            parts_out[k, x] = pick(own_parts[k, start + x])
     for x in range(4):
         window_out[x] = pick(cf[start + x])
         partner_out[x] = pick(cf[start + x, pl.ds(pl.multiple_of((1 - core) * 64, 64), 64), :])
         beyond_out[x] = pick(cf[start + x, pl.ds(pl.multiple_of(core * 64, 64), 64), :])
 
 
-def input_kernel(place_ref, partner_ref, beyond_ref, own_ref, taps_ref, rest_ref, out_ref, band):
+def input_kernel(
+    partner_ref, beyond_ref, own_ref, taps_ref, parts_ref, noise_ref, field_ref, out_ref, band
+):
     shape = (8, 128)
     upper = iota(shape, 0) < 4
     zero = jnp.zeros(shape, F32)
@@ -476,7 +491,7 @@
                         tiles.append(zero)
                 lane = (window * 2 + pair) * 128
                 band[d * 16 : d * 16 + 16, lane : lane + 128] = jnp.concatenate(tiles, axis=0).astype(BF16)
-    low_core = place_ref[1] == 0
+    low_core = lax.rem(lax.axis_index("gy"), 2) == 0
     left = jnp.where(low_core, beyond_ref[...], partner_ref[...])
     right = jnp.where(low_core, partner_ref[...], beyond_ref[...])
     window = jnp.concatenate([left, own_ref[...], right], axis=1).reshape(1024, 128)
@@ -484,14 +499,24 @@
     out = pltpu.roll(parts[:16], 1, 1) + parts[16:32] + pltpu.roll(parts[32:], 127, 1)
     site = iota(shape, 0) // 4 + iota(shape, 0) % 4 + iota(shape, 1)
     for x in range(2):
-        out_ref[x] = jnp.where((site + x) % 2 == 0, out[8 * x : 8 * x + 8], 0.0) + rest_ref[x]
+        frozen = (site + x) % 2 == 0
+        noise = noise_ref[x]
+        growth = parts_ref[0, x]
+        here = jnp.where(frozen, noise, noise * growth + parts_ref[1, x])
+        force = (
+            -2.0 * HOPPING * parts_ref[2, x]
+            + 2.0 * here
+            + 4.0 * QUARTIC * here * (here * here - 1.0)
+        )
+        field_ref[x] = here
+        out_ref[x] = jnp.where(frozen, out[8 * x : 8 * x + 8] + force, force * growth) - noise
 
 
 def vmem():
     return pl.BlockSpec(memory_space=pltpu.VMEM)
 
 
-def run_main(place, noise, small, selector, taps2, taps2t, taps3, b1, b2, b3):
+def run_main(noise, small, selector, taps2, taps2t, taps3, b1, b2, b3):
     scratch = [
         ((XP, 4 * ROWS, 256), F32),
         ((3, XP, 4 * ROWS, 256), F32),
@@ -503,8 +528,7 @@
         ((3, 2, XP, 24, 256), F32),
         ((2, 8, 32, 256), F32),
         ((XP, 32, 256), F32),
-        ((8, 8, 256), F32),
-        ((8, 8, 256), F32),
+        ((3, 8, 8, 256), F32),
         ((256, 192), BF16),
         ((256, 384), BF16),
         ((384, 768), BF16),
@@ -514,38 +538,66 @@
         ((144, 256), F32),
         ((144, 128), F32),
         ((PACK_ROWS, 128), F32),
+        ((16, 4 * ROWS, 128), BF16),
     ]
     return pl.pallas_call(
         main_kernel,
         out_shape=(
-            jax.ShapeDtypeStruct((2, 8, 128), F32),
-            jax.ShapeDtypeStruct((2, 8, 128), F32),
+            jax.ShapeDtypeStruct((3, 2, 8, 128), F32),
             jax.ShapeDtypeStruct((4, 128, 128), BF16),
             jax.ShapeDtypeStruct((4, 64, 128), BF16),
             jax.ShapeDtypeStruct((4, 64, 128), BF16),
             jax.ShapeDtypeStruct((PACK_ROWS // 2, 128), F32),
             jax.ShapeDtypeStruct((PACK_ROWS // 2, 128), F32),
         ),
-        in_specs=[pl.BlockSpec(memory_space=pltpu.SMEM)] + [vmem()] * 9,
-        out_specs=(vmem(),) * 7,
-        scratch_shapes=[pltpu.VMEM(s, t) for s, t in scratch],
+        in_specs=[pl.BlockSpec(memory_space=pltpu.HBM)] + [vmem()] * 8,
+        out_specs=(vmem(),) * 6,
+        scratch_shapes=[pltpu.VMEM(s, t) for s, t in scratch] + [pltpu.SemaphoreType.DMA],
         compiler_params=pltpu.CompilerParams(vmem_limit_bytes=56 * 1024 * 1024),
-    )(place, noise, small, selector, taps2, taps2t, taps3, b1, b2, b3)
-
-
-def run_input(place, partner, beyond, own, taps, rest):
+    )(noise, small, selector, taps2, taps2t, taps3, b1, b2, b3)
+
+
+def window_kernel(copies, distant_ref, block_ref, paired_ref, across_ref, out_ref):
+    me = lax.axis_index("gy")
+    even = lax.rem(me, 2) == 0
+    even_chip = lax.rem(me // 2, 2) == 0
+    for x in range(2):
+        before = jnp.where(even_chip, across_ref[x], paired_ref[x])
+        after = jnp.where(even_chip, paired_ref[x], across_ref[x])
+        tiles = [before[:8], before[8:], block_ref[x, :8], block_ref[x, 8:], after[:8], after[8:]]
+        distant = distant_ref[x]
+        rows = [jnp.where(even, distant, tiles[0])]
+        rows += [jnp.where(even, tiles[k - 1], tiles[k]) for k in range(1, 6)]
+        rows += [jnp.where(even, tiles[5], distant)]
+        window = jnp.concatenate(rows, axis=0).astype(BF16)
+        for k in range(copies):
+            out_ref[k, x] = window
+
+
+def run_window(distant, block, paired, across):
+    copies = lax.axis_size("gx")
+    return pl.pallas_call(
+        functools.partial(window_kernel, copies),
+        out_shape=jax.ShapeDtypeStruct((copies, 2, 4 * ROWS, 128), BF16),
+        in_specs=[vmem()] * 4,
+        out_specs=vmem(),
+        compiler_params=pltpu.CompilerParams(vmem_limit_bytes=16 * 1024 * 1024),
+    )(distant, block, paired, across)
+
+
+def run_input(partner, beyond, own, taps, parts, noise):
     return pl.pallas_call(
         input_kernel,
-        out_shape=jax.ShapeDtypeStruct((2, 8, 128), F32),
-        in_specs=[pl.BlockSpec(memory_space=pltpu.SMEM)] + [vmem()] * 5,
-        out_specs=vmem(),
+        out_shape=(jax.ShapeDtypeStruct((2, 8, 128), F32),) * 2,
+        in_specs=[vmem()] * 6,
+        out_specs=(vmem(),) * 2,
         scratch_shapes=[pltpu.VMEM((48, 1024), BF16)],
         compiler_params=pltpu.CompilerParams(vmem_limit_bytes=16 * 1024 * 1024),
-    )(place, partner, beyond, own, taps, rest)
-
-
-def unpack_kernel(scale, place_ref, mine_ref, theirs_ref, loss, first, b1, middle, b2, last, b3, both):
-    core = place_ref[1]
+    )(partner, beyond, own, taps, parts, noise)
+
+
+def unpack_kernel(scale, mine_ref, theirs_ref, loss, first, b1, middle, b2, last, b3, both):
+    core = lax.rem(lax.axis_index("gy"), 2)
     half = PACK_ROWS // 2
     both[pl.ds(pl.multiple_of(core * half, 8), half), :] = mine_ref[...] * scale
     both[pl.ds(pl.multiple_of((1 - core) * half, 8), half), :] = theirs_ref[...] * scale
@@ -576,7 +628,7 @@
             for b in range(3):
                 for c in range(3):
                     row = b * 4 + c
-                    first[a * 9 + b * 3 + c, d : d + 1, :] = v[row : row + 1, :16]
+                    first[a * 27 + b * 9 + c * 3 + d] = v[row : row + 1, :16]
     for b in range(3):
         for c in range(3):
             if b < 2:
@@ -595,25 +647,66 @@
     loss[...] = pltpu.roll(row, 126, 1)[:, :1]
 
 
-def run_unpack(scale, place, mine, theirs):
-    shapes = ((1, 1), (27, 3, 16), (1, 16), (81, 16, 16), (1, 16), (81, 2, 16), (1, 2))
+def run_unpack(scale, mine, theirs):
+    shapes = ((1, 1), (81, 1, 16), (1, 16), (81, 16, 16), (1, 16), (81, 2, 16), (1, 2))
     return pl.pallas_call(
         functools.partial(unpack_kernel, scale),
         out_shape=tuple(jax.ShapeDtypeStruct(s, F32) for s in shapes),
-        in_specs=[pl.BlockSpec(memory_space=pltpu.SMEM), vmem(), vmem()],
+        in_specs=[vmem(), vmem()],
         out_specs=(vmem(),) * len(shapes),
         scratch_shapes=[pltpu.VMEM((PACK_ROWS, 128), F32)],
         compiler_params=pltpu.CompilerParams(vmem_limit_bytes=16 * 1024 * 1024),
-    )(place, mine, theirs)
+    )(mine, theirs)
 
 
 def pad_taps(v):
     return jnp.pad(v, [(0, 0)] * (v.ndim - 2) + [(0, 1), (0, 0)])
 
 
+def taps_kernel(kernel_ref, taps_ref, flipped_ref, spread):
+    shape = (16, 128)
+    lane = iota(shape, 1)
+    group = (lane // 16) % 4
+    repeat = jnp.where(iota(shape, 0) == lane % 16, 1.0, 0.0).astype(BF16)
+    spread[...] = jnp.dot(kernel_ref[...], repeat, preferred_element_type=F32)
+    unit = jnp.where(iota((16, 16), 0) == iota((16, 16), 1), 1.0, 0.0).astype(BF16)
+    starts = [128 * k for k in range(10)] + [1168]
+    turned = [
+        lax.dot_general(
+            unit, kernel_ref[k : k + 128, :], (((1,), (1,)), ((), ())), preferred_element_type=F32
+        )
+        for k in starts
+    ]
+    zero = jnp.zeros(shape, F32)
+    for d in range(3):
+        for a in range(3):
+            for b in range(3):
+                plain = zero
+                flipped = zero
+                for c in range(3):
+                    tap = a * 27 + b * 9 + c * 3 + d
+                    plain = jnp.where(group == c, spread[tap * 16 : tap * 16 + 16, :], plain)
+                    tap = 80 - tap
+                    chunk = tap // 8
+                    offset = tap * 16 - starts[chunk]
+                    shift = (c * 16 - offset) % 128
+                    v = turned[chunk]
+                    v = pltpu.roll(v, shift, 1) if shift else v
+                    flipped = jnp.where(lane // 16 == c, v, flipped)
+                flipped = flipped + pltpu.roll(flipped, 64, 1)
+                taps_ref[d * 9 + a * 3 + b] = plain.astype(BF16)
+                flipped_ref[d * 9 + a * 3 + b] = flipped.astype(BF16)
+
+
 def hidden_taps(kernel):
-    v = pad_taps(jnp.transpose(kernel, (5, 2, 3, 0, 4, 1))).reshape(27, 16, 64)
-    return jnp.concatenate([v, v], axis=2)
+    return pl.pallas_call(
+        taps_kernel,
+        out_shape=(jax.ShapeDtypeStruct((27, 16, 128), BF16),) * 2,
+        in_specs=[vmem()],
+        out_specs=(vmem(),) * 2,
+        scratch_shapes=[pltpu.VMEM((1296, 128), F32)],
+        compiler_params=pltpu.CompilerParams(vmem_limit_bytes=16 * 1024 * 1024),
+    )(jnp.transpose(kernel, (2, 3, 4, 5, 0, 1)).reshape(1296, 16))
 
 
 def banded_taps(v):
@@ -627,9 +720,8 @@
     return lax.ppermute(v, "gy", [(i, partner(i)) for i in range(axis_size)])
 
 
-def gather_noise(noise):
+def gather_y(noise, weights):
     size_y = lax.axis_size("gy")
-    size_x = lax.axis_size("gx")
     even = lax.axis_index("gy") % 2 == 0
     chips = size_y // 2
 
@@ -639,29 +731,23 @@
     def chip_after(i):
         return ((((i >> 1) + 1) ^ 1) - 1) % chips * 2 + (i & 1)
 
+    distant = swapped(noise, size_y, far)
     beside = swapped(noise, size_y, lambda i: i ^ 1)
-    near, beside = lax.optimization_barrier((noise, beside))
-    distant = swapped(near, size_y, far)
     block = jnp.concatenate(
         [jnp.where(even, noise, beside), jnp.where(even, beside, noise)], axis=1
     )
+    block, *weights = lax.optimization_barrier((block, *weights))
     paired = swapped(block, size_y, lambda i: i ^ 2)
     across = swapped(block, size_y, chip_after)
-    even_chip = (lax.axis_index("gy") // 2) % 2 == 0
-    before = jnp.where(even_chip, across, paired)
-    after = jnp.where(even_chip, paired, across)
-    middle = jnp.concatenate([before, block, after], axis=1)
-    window = jnp.where(
-        even,
-        jnp.concatenate([distant, middle], axis=1),
-        jnp.concatenate([middle, distant], axis=1),
-    )
-    window = window.reshape(2, 4 * ROWS, 128)
-    sent = jnp.broadcast_to(window[None], (size_x,) + window.shape)
-    return lax.all_to_all(sent, "gx", 0, 0, tiled=True).reshape(16, 4 * ROWS, 128)
-
-
-def sum_over_y(mine, theirs):
+    return run_window(
+        distant.reshape(2, 8, 128),
+        block.reshape(2, 16, 128),
+        paired.reshape(2, 16, 128),
+        across.reshape(2, 16, 128),
+    ), weights
+
+
+def sum_over_y(mine, theirs, *before_last):
     size_y = lax.axis_size("gy")
 
     def along_z(partner):
@@ -676,15 +762,18 @@
         lambda i: i ^ 16,
         along_z(lambda z: z ^ 1),
         along_z(lambda z: (((z + 1) ^ 1) - 1) % 8),
-        along_z(lambda z: crossing[z]),
     ):
         v = v + swapped(v, size_y, partner)
-    return v, swapped(v, size_y, lambda i: i ^ 1)
+    v, *before_last = lax.optimization_barrier((v, *before_last))
+    v = v + swapped(v, size_y, along_z(lambda z: crossing[z]))
+    return v, before_last
 
 
 def local(noise, w_first, b_first, w_middle, b_middle, w_last, b_last):
     size_y = lax.axis_size("gy")
     sites = float(noise.size * lax.axis_size("gx") * size_y)
+    sent, (w_first, w_middle, w_last) = gather_y(noise, (w_first, w_middle, w_last))
+    gathered = lax.all_to_all(sent, "gx", 0, 0, tiled=True).reshape(16, 4 * ROWS, 128)
     flip = (slice(None), slice(None)) + (slice(None, None, -1),) * 4
     small = jnp.concatenate(
         [
@@ -694,37 +783,34 @@
         axis=0,
     )
     small = jnp.pad(small, ((0, 0), (0, 5)))
-    taps2 = hidden_taps(w_middle)
-    taps2t = hidden_taps(jnp.transpose(w_middle[flip], (1, 0, 2, 3, 4, 5)))
+    taps2, taps2t = hidden_taps(w_middle)
     taps3 = banded_taps(jnp.transpose(w_last, (5, 2, 3, 0, 4, 1)).reshape(27, 2, 3, 16))
     tapsd = banded_taps(jnp.transpose(w_first[flip], (5, 2, 3, 1, 4, 0)).reshape(27, 1, 3, 16))
     tapsd = jnp.concatenate([tapsd, tapsd], axis=1)
 
-    gathered = gather_noise(noise)
-    place = jnp.stack([lax.axis_index("gx"), lax.axis_index("gy") % 2]).astype(jnp.int32)
-    field, rest, window, to_partner, to_beyond, mine, theirs = run_main(
-        place,
+    parts, window, to_partner, to_beyond, mine, theirs = run_main(
         gathered,
         small,
         jnp.asarray(tap_selector(), BF16),
         taps2,
         taps2t,
         taps3,
-        b_first.reshape(16, 1),
-        b_middle.reshape(16, 1),
-        jnp.repeat(b_last, 4).reshape(8, 1),
+        b_first.reshape(1, 16),
+        b_middle.reshape(1, 16),
+        b_last.reshape(1, 2),
     )
     partner = swapped(to_partner, size_y, lambda i: i ^ 1)
     beyond = swapped(to_beyond, size_y, lambda i: (((i + 1) ^ 1) - 1) % size_y)
-    noise_grad = run_input(place, partner, beyond, window, tapsd, rest)
-
-    mine, theirs = sum_over_y(mine, theirs)
-    loss, first, b1, middle, b2, last, b3 = run_unpack(1.0 / sites, place, mine, theirs)
+    mine, (partner, beyond) = sum_over_y(mine, theirs, partner, beyond)
+    field, noise_grad = run_input(partner, beyond, window, tapsd, parts, noise.reshape(2, 8, 128))
+    mine, field, noise_grad = lax.optimization_barrier((mine, field, noise_grad))
+    theirs = swapped(mine, size_y, lambda i: i ^ 1)
+    loss, first, b1, middle, b2, last, b3 = run_unpack(1.0 / sites, mine, theirs)
     return (
         field.reshape(noise.shape),
         noise_grad.reshape(noise.shape),
         loss.reshape(()),
-        jnp.transpose(first.reshape(3, 3, 3, 3, 16), (4, 0, 1, 2, 3))[:, None],
+        jnp.transpose(first.reshape(3, 3, 3, 3, 1, 16), (5, 4, 0, 1, 2, 3)),
         b1.reshape(16),
         jnp.transpose(middle.reshape(3, 3, 3, 3, 16, 16), (4, 5, 0, 1, 2, 3)),
         b2.reshape(16),

time: 83.1 us -> 77.5 us (0.933)
  local copies, waits for them, and re-layouts: 13 us -> 5.53 us
  waiting for transfers between devices: 12.3 us -> 16.8 us
  other arithmetic: 3.36 us -> 1.94 us
  starting transfers between devices: 31.9 us -> 30.5 us
    all_to_all x1, waiting for transfers between devices: 0.01 us -> 7.19 us  [local(): lax.all_to_all(sent, 'gx', 0, 0, tiled=True).reshape(16, 4 * ROWS, 128)]
    ppermute x12, waiting for transfers between devices: 12.3 us -> 9.61 us  [swapped(): return lax.ppermute(v, 'gy', [(i, partner(i)) for i in range(axis_size)])]
    unnamed x36 -> x27, local copies, waits for them, and re-layouts: 5.25 us -> 3.13 us
    reshape x4 -> x0, local copies, waits for them, and re-layouts: 1.84 us -> none  [the longest x1 0.68 us: local(): b_first.reshape(16, 1)]
    broadcast_in_dim x3 -> x0, local copies, waits for them, and re-layouts: 1.51 us -> none  [the longest x1 0.8 us: gather_noise(): sent = jnp.broadcast_to(window[None], (size_x,) + window.shape)]
    ppermute x12, starting transfers between devices: 25.6 us -> 24.2 us  [swapped(): return lax.ppermute(v, 'gy', [(i, partner(i)) for i in range(axis_size)])]
    pallas_call x2 -> x4, Pallas kernels: 19.4 us -> 20.4 us  [the longest x1 18.2 us: run_main(): pl.pallas_call(main_kernel, out_shape=(jax.ShapeDtypeStruct((3, 2, 8, 128...]
  transfers between devices with their start and end apart: 13 -> 13, of which waited for: 7 -> 6; matrix products, arithmetic and copies ran while one was open for 12% -> 6% of each run, Pallas kernels for 2% -> 2%
where the time goes in v3:
time: 77.5 us; the launch traced here: 77.1 us
  starting transfers between devices  30.5 us (39%)
  Pallas kernels  21.5 us (28%)
  waiting for transfers between devices  16.8 us (22%)
  local copies, waits for them, and re-layouts  5.53 us (7%)
  other arithmetic  1.94 us (3%)
  between operations  0.9 us (1%)
    ppermute x12, starting transfers between devices, swapped(): return lax.ppermute(v, 'gy', [(i, partner(i)) for i in range(axis_size)])  24.2 us
    pallas_call x1, Pallas kernels, run_main(): pl.pallas_call(main_kernel, out_shape=(jax.ShapeDtypeStruct((3, 2, 8, 128...  18.2 us
    ppermute x12, waiting for transfers between devices, swapped(): return lax.ppermute(v, 'gy', [(i, partner(i)) for i in range(axis_size)])  9.61 us
    all_to_all x1, waiting for transfers between devices, local(): lax.all_to_all(sent, 'gx', 0, 0, tiled=True).reshape(16, 4 * ROWS, 128)  7.19 us
    all_to_all x1, starting transfers between devices, local(): lax.all_to_all(sent, 'gx', 0, 0, tiled=True).reshape(16, 4 * ROWS, 128)  6.36 us
    unnamed x27, local copies, waits for them, and re-layouts  3.13 us
  transfers between devices with their start and end apart: 13, of which 6 were waited for; matrix products, arithmetic and copies ran while one was open for 6% of the time, Pallas kernels for 2%

profile of v3, /device:TPU:1, one launch (start us, length us, event | category | flops | bytes accessed | tf_op | source)
XLA Modules:
  0.0 77.1 jit_solution(16347866718455584355)
XLA Ops:
  0.6 3.3 %collective-permute-start.1 = (f32[2,2,4,128]{3,2,1,0:T(4,128)}, f32[2,2,4,128]{3,2,1,0:T(4,128)S(1)}, u32[]{:S(2)}, u32[]{:S(2)}) collective-permute-start(f32[2,2,4,128]{3,2,1,0:T(4,128)} %param.8), channel_id=1, source_target_pairs={{0,1},{1,0},{2,3},{3,2},{4,5},{5,4},{6,7},{7,6},{8,9},{9,8},{10,11... | collective-permute-start | bytes 24584 | tf_op jit(solution)/shard_map/ppermute | solution.py:720
  4.0 1.2 %collective-permute-start = (f32[2,2,4,128]{3,2,1,0:T(4,128)}, f32[2,2,4,128]{3,2,1,0:T(4,128)S(1)}, u32[]{:S(2)}, u32[]{:S(2)}) collective-permute-start(f32[2,2,4,128]{3,2,1,0:T(4,128)} %param.8), channel_id=1, source_target_pairs={{0,29},{1,4},{2,31},{3,6},{4,1},{5,8},{6,3},{7,10},{8,5},{9,12},{1... | collective-permute-start | bytes 24584 | tf_op jit(solution)/shard_map/ppermute | solution.py:720
  5.2 0.7 copy-done.4
  6.2 0.1 pad_bitcast_fusion.1
  6.2 1.7 %collective-permute-start.2 = (f32[2,4,4,128]{3,2,1,0:T(4,128)S(1)}, f32[2,4,4,128]{3,2,1,0:T(4,128)S(1)}, u32[]{:S(2)}, u32[]{:S(2)}) collective-permute-start(f32[2,4,4,128]{3,2,1,0:T(4,128)S(1)} %pad_maximum_fusion.4), channel_id=1, source_target_pairs={{0,2},{1,3},{2,0},{3,1},{4,6},{5,7},{6,4},{7,5},{8,10},{9,11},{10,... | collective-permute-start | bytes 49160 | tf_op jit(solution)/shard_map/ppermute | solution.py:720
  8.0 3.0 %collective-permute-start.3 = (f32[2,4,4,128]{3,2,1,0:T(4,128)S(1)}, f32[2,4,4,128]{3,2,1,0:T(4,128)S(1)}, u32[]{:S(2)}, u32[]{:S(2)}) collective-permute-start(f32[2,4,4,128]{3,2,1,0:T(4,128)S(1)} %pad_maximum_fusion.4), channel_id=1, source_target_pairs={{0,30},{1,31},{2,4},{3,5},{4,2},{5,3},{6,8},{7,9},{8,6},{9,7},{10,... | collective-permute-start | bytes 49160 | tf_op jit(solution)/shard_map/ppermute | solution.py:720
  11.0 0.2 maximum_bitcast_fusion
  11.2 0.5 pad_maximum_fusion
  11.6 0.3 copy.39
  11.9 0.1 copy.40
  12.1 0.7 pad_maximum_fusion.1.taps3_ref
  12.8 0.1 reshape.105
  12.9 0.1 reshape.104
  13.0 0.1 pad_maximum_fusion.5
  13.2 0.1 copy.51
  13.3 0.1 copy.37
  13.4 0.6 shard_map.152
  14.1 0.6 copy-done.2
  14.7 0.6 copy-done.3
  15.3 0.6 pad.14.small_ref
  16.0 0.7 shard_map.151
  16.7 6.4 %all-to-all-start = ((bf16[8,2,56,128]{3,2,1,0:T(8,128)(2,1)}), bf16[8,2,56,128]{3,2,1,0:T(8,128)(2,1)S(1)}, u32[]{:S(2)}, u32[]{:S(2)}) async-start(bf16[8,2,56,128]{3,2,1,0:T(8,128)(2,1)} %shard_map.151), calls=%async_computation | async-start | bytes 458752 | tf_op jit(solution)/shard_map/all_to_all | solution.py:776
  23.1 7.2 %all-to-all-done = bf16[8,2,56,128]{3,2,1,0:T(8,128)(2,1)S(1)} async-done(((bf16[8,2,56,128]{3,2,1,0:T(8,128)(2,1)}), bf16[8,2,56,128]{3,2,1,0:T(8,128)(2,1)S(1)}, u32[]{:S(2)}, u32[]{:S(2)}) %all-to-all-start) | async-done | bytes 229408 | tf_op jit(solution)/shard_map/all_to_all | solution.py:776
  30.3 0.7 copy-done.6
  30.9 18.2 %shard_map.153 = (f32[3,2,8,128]{3,2,1,0:T(8,128)}, bf16[4,128,128]{2,1,0:T(8,128)(2,1)}, bf16[4,64,128]{2,1,0:T(8,128)(2,1)}, bf16[4,64,128]{2,1,0:T(8,128)(2,1...) custom-call(bf16[16,56,128]{2,1,0:T(8,128)(2,1)} %bitcast.69, bf16[144,32]{1,0:T(8,128)(2,1)} %pad.14.small_ref, ...), custom_call_target="tpu_custom_call" | custom-call | tf_op jit(solution)/shard_map/pallas_call | solution.py:543
  49.1 3.3 %collective-permute-start.4 = (f32[144,128]{1,0:T(8,128)}, f32[144,128]{1,0:T(8,128)S(1)}, u32[]{:S(2)}, u32[]{:S(2)}) collective-permute-start(f32[144,128]{1,0:T(8,128)} %get-tuple-element.43), channel_id=1, source_target_pairs={{0,1},{1,0},{2,3},{3,2},{4,5},{5,4},{6,7},{7,6},{8,9},{9,8},{10,11... | collective-permute-start | bytes 221192 | tf_op jit(solution)/shard_map/ppermute | solution.py:720
  52.5 0.1 copy.46
  52.6 0.1 copy.50
  52.7 0.9 %collective-permute-done.4 = f32[144,128]{1,0:T(8,128)S(1)} collective-permute-done((f32[144,128]{1,0:T(8,128)}, f32[144,128]{1,0:T(8,128)S(1)}, u32[]{:S(2)}, u32[]{:S(2)}) %collective-permute-start.4) | collective-permute-done | bytes 73760 | tf_op jit(solution)/shard_map/ppermute | solution.py:720
  53.6 0.1 collective-permute-start.5
  53.7 3.2 %collective-permute-done.5 = f32[144,128]{1,0:T(8,128)S(1)} collective-permute-done((f32[144,128]{1,0:T(8,128)S(1)}, f32[144,128]{1,0:T(8,128)S(1)}, u32[]{:S(2)}, u32[]{:S(2)}) %collective-permute-start.5) | collective-permute-done | bytes 73760 | tf_op jit(solution)/shard_map/ppermute | solution.py:720
  56.9 0.3 collective-permute-start.6
  57.3 0.1 copy.43
  57.4 0.1 copy.47
  57.5 0.3 copy-done.12
  57.7 1.5 %collective-permute-start.8 = (bf16[4,64,128]{2,1,0:T(8,128)(2,1)S(1)}, bf16[4,64,128]{2,1,0:T(8,128)(2,1)S(1)}, u32[]{:S(2)}, u32[]{:S(2)}) collective-permute-start(bf16[4,64,128]{2,1,0:T(8,128)(2,1)S(1)} %copy-done.12), channel_id=1, source_target_pairs={{0,1},{1,0},{2,3},{3,2},{4,5},{5,4},{6,7},{7,6},{8,9},{9,8},{10,11... | collective-permute-start | bytes 196616 | tf_op jit(solution)/shard_map/ppermute | solution.py:720
  59.2 1.6 %collective-permute-start.9 = (bf16[4,64,128]{2,1,0:T(8,128)(2,1)S(1)}, bf16[4,64,128]{2,1,0:T(8,128)(2,1)S(1)}, u32[]{:S(2)}, u32[]{:S(2)}) collective-permute-start(bf16[4,64,128]{2,1,0:T(8,128)(2,1)S(1)} %copy-done.11), channel_id=1, source_target_pairs={{0,31},{1,2},{2,1},{3,4},{4,3},{5,6},{6,5},{7,8},{8,7},{9,10},{10,... | collective-permute-start | bytes 196616 | tf_op jit(solution)/shard_map/ppermute | solution.py:720
  60.8 1.8 %collective-permute-start.7 = (f32[144,128]{1,0:T(8,128)S(1)}, f32[144,128]{1,0:T(8,128)S(1)}, u32[]{:S(2)}, u32[]{:S(2)}) collective-permute-start(f32[144,128]{1,0:T(8,128)S(1)} %add.32), channel_id=1, source_target_pairs={{0,14},{1,15},{2,4},{3,5},{4,2},{5,3},{6,8},{7,9},{8,6},{9,7},{10,... | collective-permute-start | bytes 221192 | tf_op jit(solution)/shard_map/ppermute | solution.py:720
  62.7 0.1 copy.48
  62.8 0.1 copy.49
  62.9 2.4 %collective-permute-done.7 = f32[144,128]{1,0:T(8,128)S(1)} collective-permute-done((f32[144,128]{1,0:T(8,128)S(1)}, f32[144,128]{1,0:T(8,128)S(1)}, u32[]{:S(2)}, u32[]{:S(2)}) %collective-permute-start.7) | collective-permute-done | bytes 73760 | tf_op jit(solution)/shard_map/ppermute | solution.py:720
  65.4 1.6 %collective-permute-start.10 = (f32[144,128]{1,0:T(8,128)S(1)}, f32[144,128]{1,0:T(8,128)S(1)}, u32[]{:S(2)}, u32[]{:S(2)}) collective-permute-start(f32[144,128]{1,0:T(8,128)S(1)} %add.33), channel_id=1, source_target_pairs={{0,6},{1,7},{2,12},{3,13},{4,10},{5,11},{6,0},{7,1},{8,14},{9,15},... | collective-permute-start | bytes 221192 | tf_op jit(solution)/shard_map/ppermute | solution.py:720
  66.9 0.4 maximum_maximum_fusion.taps_ref
  67.4 0.9 %shard_map.154 = (f32[2,8,128]{2,1,0:T(8,128)}, f32[2,8,128]{2,1,0:T(8,128)}) custom-call(bf16[4,64,128]{2,1,0:T(8,128)(2,1)S(1)} %collective-permute-done.8.partner_ref, bf16[4,64,128]{2,1,0:T(8,128)(2,1)S(1)} %collective-permute-done.9.beyond_ref, bf16[4,128,128]{2,1,0:T(8,128)(2,1)S(1)} %copy-done.1, ...), custom_call_target="tpu_custom_call" | custom-call | tf_op jit(solution)/shard_map/pallas_call | solution.py:589
  68.2 2.2 %collective-permute-done.10 = f32[144,128]{1,0:T(8,128)S(1)} collective-permute-done((f32[144,128]{1,0:T(8,128)S(1)}, f32[144,128]{1,0:T(8,128)S(1)}, u32[]{:S(2)}, u32[]{:S(2)}) %collective-permute-start.10) | collective-permute-done | bytes 73760 | tf_op jit(solution)/shard_map/ppermute | solution.py:720
  70.5 4.7 %collective-permute-start.11 = (f32[144,128]{1,0:T(8,128)S(1)}, f32[144,128]{1,0:T(8,128)S(1)}, u32[]{:S(2)}, u32[]{:S(2)}) collective-permute-start(f32[144,128]{1,0:T(8,128)S(1)} %add.34.mine_ref), channel_id=1, source_target_pairs={{0,1},{1,0},{2,3},{3,2},{4,5},{5,4},{6,7},{7,6},{8,9},{9,8},{10,11... | collective-permute-start | bytes 221192 | tf_op jit(solution)/shard_map/ppermute | solution.py:720
  75.1 0.9 %collective-permute-done.11.theirs_ref = f32[144,128]{1,0:T(8,128)S(1)} collective-permute-done((f32[144,128]{1,0:T(8,128)S(1)}, f32[144,128]{1,0:T(8,128)S(1)}, u32[]{:S(2)}, u32[]{:S(2)}) %collective-permute-start.11) | collective-permute-done | bytes 73760 | tf_op jit(solution)/shard_map/ppermute | solution.py:720
  76.0 1.1 %shard_map.155 = (f32[1,1]{1,0:T(1,128)}, f32[81,1,16]{2,1,0:T(1,128)}, f32[1,16]{1,0:T(1,128)}, f32[81,16,16]{2,1,0:T(8,128)}, f32[1,16]{1,0:T(1,128)}, /*index=5*/f32[81,2,16]{2,1,0:T(2,128)}, f32[1,2]{1,0:T(1,128)}) custom-call(f32[144,128]{1,0:T(8,128)S(1)} %add.34.mine_ref, f32[144,128]{1,0:T(8,128)S(1)} %collective-permute-done.11.theirs_ref), custom_call_target="tpu_custom_call" | custom-call | tf_op jit(solution)/shard_map/pallas_call | solution.py:652
  (50 shorter events, 0.5 us)
Async XLA Ops:
  0.6 4.6 %collective-permute-start.1 = (f32[2,2,4,128]{3,2,1,0:T(4,128)}, f32[2,2,4,128]{3,2,1,0:T(4,128)S(1)}, u32[]{:S(2)}, u32[]{:S(2)}) collective-permute-start(f32[2,2,4,128]{3,2,1,0:T(4,128)} %param.8), channel_id=1, source_target_pairs={{0,1},{1,0},{2,3},{3,2},{4,5},{5,4},{6,7},{7,6},{8,9},{9,8},{10,11... | collective-permute-start | bytes 24584 | tf_op jit(solution)/shard_map/ppermute | solution.py:720
  4.0 12.0 %collective-permute-start = (f32[2,2,4,128]{3,2,1,0:T(4,128)}, f32[2,2,4,128]{3,2,1,0:T(4,128)S(1)}, u32[]{:S(2)}, u32[]{:S(2)}) collective-permute-start(f32[2,2,4,128]{3,2,1,0:T(4,128)} %param.8), channel_id=1, source_target_pairs={{0,29},{1,4},{2,31},{3,6},{4,1},{5,8},{6,3},{7,10},{8,5},{9,12},{1... | collective-permute-start | bytes 24584 | tf_op jit(solution)/shard_map/ppermute | solution.py:720
  5.2 0.7 copy-start.4
  5.2 0.8 %copy-start.8 = (bf16[2,16,3,3,3,3]{1,0,5,4,3,2:T(2,128)(2,1)S(1)}, bf16[2,16,3,3,3,3]{1,0,5,4,3,2:T(2,128)(2,1)}, u32[]{:S(2)}) copy-start(bf16[2,16,3,3,3,3]{1,0,5,4,3,2:T(2,128)(2,1)} %param.13) | copy-start | bytes 15556
  6.2 9.7 %collective-permute-start.2 = (f32[2,4,4,128]{3,2,1,0:T(4,128)S(1)}, f32[2,4,4,128]{3,2,1,0:T(4,128)S(1)}, u32[]{:S(2)}, u32[]{:S(2)}) collective-permute-start(f32[2,4,4,128]{3,2,1,0:T(4,128)S(1)} %pad_maximum_fusion.4), channel_id=1, source_target_pairs={{0,2},{1,3},{2,0},{3,1},{4,6},{5,7},{6,4},{7,5},{8,10},{9,11},{10,... | collective-permute-start | bytes 49160 | tf_op jit(solution)/shard_map/ppermute | solution.py:720
  8.0 8.0 %collective-permute-start.3 = (f32[2,4,4,128]{3,2,1,0:T(4,128)S(1)}, f32[2,4,4,128]{3,2,1,0:T(4,128)S(1)}, u32[]{:S(2)}, u32[]{:S(2)}) collective-permute-start(f32[2,4,4,128]{3,2,1,0:T(4,128)S(1)} %pad_maximum_fusion.4), channel_id=1, source_target_pairs={{0,30},{1,31},{2,4},{3,5},{4,2},{5,3},{6,8},{7,9},{8,6},{9,7},{10,... | collective-permute-start | bytes 49160 | tf_op jit(solution)/shard_map/ppermute | solution.py:720
  11.6 1.3 %copy-start.9 = (bf16[16,1,3,3,3,3]{0,5,4,3,2,1:T(4,128)(2,1)S(1)}, bf16[16,1,3,3,3,3]{0,5,4,3,2,1:T(4,128)(2,1)}, u32[]{:S(2)}) copy-start(bf16[16,1,3,3,3,3]{0,5,4,3,2,1:T(4,128)(2,1)} %param.9) | copy-start | bytes 7780
  11.9 1.5 %copy-start = (bf16[16,16,3,3,3,3]{1,0,5,4,3,2:T(8,128)(2,1)S(1)}, bf16[16,16,3,3,3,3]{1,0,5,4,3,2:T(8,128)(2,1)}, u32[]{:S(2)}) copy-start(bf16[16,16,3,3,3,3]{1,0,5,4,3,2:T(8,128)(2,1)} %param.11) | copy-start | bytes 124420
  13.2 40.5 %copy-start.7 = (bf16[27,1,3,16]{3,0,2,1:T(8,128)(2,1)}, bf16[27,1,3,16]{3,0,2,1:T(8,128)(2,1)S(1)}, u32[]{:S(2)}) copy-start(bf16[27,1,3,16]{3,0,2,1:T(8,128)(2,1)S(1)} %reshape.112) | copy-start | bytes 7780
  14.1 0.6 copy-start.2
  14.7 0.6 copy-start.3
  16.7 13.6 %all-to-all-start = ((bf16[8,2,56,128]{3,2,1,0:T(8,128)(2,1)}), bf16[8,2,56,128]{3,2,1,0:T(8,128)(2,1)S(1)}, u32[]{:S(2)}, u32[]{:S(2)}) async-start(bf16[8,2,56,128]{3,2,1,0:T(8,128)(2,1)} %shard_map.151), calls=%async_computation | async-start | bytes 458752 | tf_op jit(solution)/shard_map/all_to_all | solution.py:776
  30.3 0.7 copy-start.6
  49.1 4.4 %collective-permute-start.4 = (f32[144,128]{1,0:T(8,128)}, f32[144,128]{1,0:T(8,128)S(1)}, u32[]{:S(2)}, u32[]{:S(2)}) collective-permute-start(f32[144,128]{1,0:T(8,128)} %get-tuple-element.43), channel_id=1, source_target_pairs={{0,1},{1,0},{2,3},{3,2},{4,5},{5,4},{6,7},{7,6},{8,9},{9,8},{10,11... | collective-permute-start | bytes 221192 | tf_op jit(solution)/shard_map/ppermute | solution.py:720
  52.4 1.1 %copy-start.10 = (f32[144,128]{1,0:T(8,128)S(1)}, f32[144,128]{1,0:T(8,128)}, u32[]{:S(2)}) copy-start(f32[144,128]{1,0:T(8,128)} %get-tuple-element.42) | copy-start | bytes 221188
  53.6 3.3 %collective-permute-start.5 = (f32[144,128]{1,0:T(8,128)S(1)}, f32[144,128]{1,0:T(8,128)S(1)}, u32[]{:S(2)}, u32[]{:S(2)}) collective-permute-start(f32[144,128]{1,0:T(8,128)S(1)} %add.30), channel_id=1, source_target_pairs={{0,16},{1,17},{2,18},{3,19},{4,20},{5,21},{6,22},{7,23},{8,24},{9,... | collective-permute-start | bytes 221192 | tf_op jit(solution)/shard_map/ppermute | solution.py:720
  53.7 3.5 %slice-start = ((bf16[27,1,3,16]{3,0,2,1:T(8,128)(2,1)}), bf16[27,1,1,16]{3,0,2,1:T(8,128)(2,1)S(1)}, s32[]{:S(2)}) async-start(bf16[27,1,3,16]{3,0,2,1:T(8,128)(2,1)} %copy-done.7), calls=%async_computation.1 | async-start | bytes 16384 | tf_op jit(solution)/shard_map/jit(_roll_static)/slice | solution.py:714
  56.9 0.8 %copy-start.12 = (bf16[4,64,128]{2,1,0:T(8,128)(2,1)S(1)}, bf16[4,64,128]{2,1,0:T(8,128)(2,1)}, u32[]{:S(2)}) copy-start(bf16[4,64,128]{2,1,0:T(8,128)(2,1)} %get-tuple-element.44) | copy-start | bytes 196612
  56.9 2.3 %copy-start.11 = (bf16[4,64,128]{2,1,0:T(8,128)(2,1)S(1)}, bf16[4,64,128]{2,1,0:T(8,128)(2,1)}, u32[]{:S(2)}) copy-start(bf16[4,64,128]{2,1,0:T(8,128)(2,1)} %get-tuple-element.45) | copy-start | bytes 196612
  56.9 3.9 %collective-permute-start.6 = (f32[144,128]{1,0:T(8,128)S(1)}, f32[144,128]{1,0:T(8,128)S(1)}, u32[]{:S(2)}, u32[]{:S(2)}) collective-permute-start(f32[144,128]{1,0:T(8,128)S(1)} %add.31), channel_id=1, source_target_pairs={{0,2},{1,3},{2,0},{3,1},{4,6},{5,7},{6,4},{7,5},{8,10},{9,11},{10,... | collective-permute-start | bytes 221192 | tf_op jit(solution)/shard_map/ppermute | solution.py:720
  57.7 7.6 %collective-permute-start.8 = (bf16[4,64,128]{2,1,0:T(8,128)(2,1)S(1)}, bf16[4,64,128]{2,1,0:T(8,128)(2,1)S(1)}, u32[]{:S(2)}, u32[]{:S(2)}) collective-permute-start(bf16[4,64,128]{2,1,0:T(8,128)(2,1)S(1)} %copy-done.12), channel_id=1, source_target_pairs={{0,1},{1,0},{2,3},{3,2},{4,5},{5,4},{6,7},{7,6},{8,9},{9,8},{10,11... | collective-permute-start | bytes 196616 | tf_op jit(solution)/shard_map/ppermute | solution.py:720
  59.2 6.1 %collective-permute-start.9 = (bf16[4,64,128]{2,1,0:T(8,128)(2,1)S(1)}, bf16[4,64,128]{2,1,0:T(8,128)(2,1)S(1)}, u32[]{:S(2)}, u32[]{:S(2)}) collective-permute-start(bf16[4,64,128]{2,1,0:T(8,128)(2,1)S(1)} %copy-done.11), channel_id=1, source_target_pairs={{0,31},{1,2},{2,1},{3,4},{4,3},{5,6},{6,5},{7,8},{8,7},{9,10},{10,... | collective-permute-start | bytes 196616 | tf_op jit(solution)/shard_map/ppermute | solution.py:720
  60.8 4.5 %collective-permute-start.7 = (f32[144,128]{1,0:T(8,128)S(1)}, f32[144,128]{1,0:T(8,128)S(1)}, u32[]{:S(2)}, u32[]{:S(2)}) collective-permute-start(f32[144,128]{1,0:T(8,128)S(1)} %add.32), channel_id=1, source_target_pairs={{0,14},{1,15},{2,4},{3,5},{4,2},{5,3},{6,8},{7,9},{8,6},{9,7},{10,... | collective-permute-start | bytes 221192 | tf_op jit(solution)/shard_map/ppermute | solution.py:720
  62.9 4.5 %copy-start.1 = (bf16[4,128,128]{2,1,0:T(8,128)(2,1)S(1)}, bf16[4,128,128]{2,1,0:T(8,128)(2,1)}, u32[]{:S(2)}) copy-start(bf16[4,128,128]{2,1,0:T(8,128)(2,1)} %get-tuple-element.49.own_ref) | copy-start | bytes 393220
  65.3 2.0 %copy-start.5 = (f32[3,2,8,128]{3,2,1,0:T(8,128)S(1)}, f32[3,2,8,128]{3,2,1,0:T(8,128)}, u32[]{:S(2)}) copy-start(f32[3,2,8,128]{3,2,1,0:T(8,128)} %get-tuple-element.50.parts_ref) | copy-start | bytes 73732
  65.4 5.1 %collective-permute-start.10 = (f32[144,128]{1,0:T(8,128)S(1)}, f32[144,128]{1,0:T(8,128)S(1)}, u32[]{:S(2)}, u32[]{:S(2)}) collective-permute-start(f32[144,128]{1,0:T(8,128)S(1)} %add.33), channel_id=1, source_target_pairs={{0,6},{1,7},{2,12},{3,13},{4,10},{5,11},{6,0},{7,1},{8,14},{9,15},... | collective-permute-start | bytes 221192 | tf_op jit(solution)/shard_map/ppermute | solution.py:720
  70.5 5.6 %collective-permute-start.11 = (f32[144,128]{1,0:T(8,128)S(1)}, f32[144,128]{1,0:T(8,128)S(1)}, u32[]{:S(2)}, u32[]{:S(2)}) collective-permute-start(f32[144,128]{1,0:T(8,128)S(1)} %add.34.mine_ref), channel_id=1, source_target_pairs={{0,1},{1,0},{2,3},{3,2},{4,5},{5,4},{6,7},{7,6},{8,9},{9,8},{10,11... | collective-permute-start | bytes 221192 | tf_op jit(solution)/shard_map/ppermute | solution.py:720

commit v4 on v3

--- a/solution.py
+++ b/solution.py
@@ -17,6 +17,7 @@
 ROWS = 2 + 2 * HALO
 XP = 10
 PACK_ROWS = 288
+SMALL_ROWS = (112, 120)
 GROUP = 8
 
 
@@ -215,7 +216,7 @@
         h1[2 * xp + 2, row, :] = out[128:]
         return 0
 
-    lax.fori_loop(0, 24, first_body, 0, unroll=12)
+    lax.fori_loop(0, 24, first_body, 0, unroll=24)
     wrap(h1)
 
     def second_body(step, _):
@@ -228,7 +229,7 @@
         h2[xl + 1, pl.ds(pl.multiple_of(yp * 128, 128), 128), :] = out.astype(BF16)
         return 0
 
-    lax.fori_loop(0, 40, second_body, 0, unroll=20)
+    lax.fori_loop(0, 40, second_body, 0, unroll=40)
     wrap(h2)
 
     top = iota((8, 256), 0) < 4
@@ -747,6 +748,18 @@
     ), weights
 
 
+def add_rounded(v, partner):
+    size_y = lax.axis_size("gy")
+    first, last = SMALL_ROWS
+    high = lax.reduce_precision(v, 8, 7)
+    low = lax.reduce_precision(v[first:last] - high[first:last], 8, 7)
+    got = swapped(jnp.concatenate([high, low], axis=0).astype(BF16), size_y, partner).astype(F32)
+    rows = v.shape[0]
+    total = high + got[:rows]
+    small = total[first:last] + (low + got[rows:])
+    return jnp.concatenate([total[:first], small, total[last:]], axis=0)
+
+
 def sum_over_y(mine, theirs, *before_last):
     size_y = lax.axis_size("gy")
 
@@ -758,14 +771,11 @@
 
     crossing = (3, 6, 5, 0, 7, 2, 1, 4)
     v = mine + swapped(theirs, size_y, lambda i: i ^ 1)
-    for partner in (
-        lambda i: i ^ 16,
-        along_z(lambda z: z ^ 1),
-        along_z(lambda z: (((z + 1) ^ 1) - 1) % 8),
-    ):
-        v = v + swapped(v, size_y, partner)
+    v = add_rounded(v, lambda i: i ^ 16)
+    v = add_rounded(v, along_z(lambda z: z ^ 1))
     v, *before_last = lax.optimization_barrier((v, *before_last))
-    v = v + swapped(v, size_y, along_z(lambda z: crossing[z]))
+    v = add_rounded(v, along_z(lambda z: (((z + 1) ^ 1) - 1) % 8))
+    v = add_rounded(v, along_z(lambda z: crossing[z]))
     return v, before_last
 
 

time: 77.5 us -> 79 us (1.019)
  other arithmetic: 1.94 us -> 3 us
    another operation x0 -> x8, other arithmetic: none -> 0.96 us
    unnamed x27 -> x25, local copies, waits for them, and re-layouts: 3.13 us -> 3.58 us
  transfers between devices with their start and end apart: 13 -> 13, of which waited for: 6 -> 7; matrix products, arithmetic and copies ran while one was open for 6% -> 6% of each run, Pallas kernels for 2% -> 2%
where the time goes in v4:
time: 79 us; the launch traced here: 78.6 us
  starting transfers between devices  30.7 us (39%)
  Pallas kernels  20.8 us (26%)
  waiting for transfers between devices  16.9 us (21%)
  local copies, waits for them, and re-layouts  6.03 us (8%)
  other arithmetic  3 us (4%)
  between operations  1.1 us (1%)
    ppermute x12, starting transfers between devices, swapped(): return lax.ppermute(v, 'gy', [(i, partner(i)) for i in range(axis_size)])  24.4 us
    pallas_call x1, Pallas kernels, run_main(): pl.pallas_call(main_kernel, out_shape=(jax.ShapeDtypeStruct((3, 2, 8, 128...  17.5 us
    ppermute x12, waiting for transfers between devices, swapped(): return lax.ppermute(v, 'gy', [(i, partner(i)) for i in range(axis_size)])  9.72 us
    all_to_all x1, waiting for transfers between devices, local(): lax.all_to_all(sent, 'gx', 0, 0, tiled=True).reshape(16, 4 * ROWS, 128)  7.19 us
    all_to_all x1, starting transfers between devices, local(): lax.all_to_all(sent, 'gx', 0, 0, tiled=True).reshape(16, 4 * ROWS, 128)  6.36 us
    unnamed x25, local copies, waits for them, and re-layouts  3.58 us
  transfers between devices with their start and end apart: 13, of which 7 were waited for; matrix products, arithmetic and copies ran while one was open for 6% of the time, Pallas kernels for 2%

profile of v4, /device:TPU:1, one launch (start us, length us, event | category | flops | bytes accessed | tf_op | source)
XLA Modules:
  0.0 78.6 jit_solution(5054012680276806543)
XLA Ops:
  0.6 3.3 %collective-permute-start.1 = (f32[2,2,4,128]{3,2,1,0:T(4,128)}, f32[2,2,4,128]{3,2,1,0:T(4,128)S(1)}, u32[]{:S(2)}, u32[]{:S(2)}) collective-permute-start(f32[2,2,4,128]{3,2,1,0:T(4,128)} %param.8), channel_id=1, source_target_pairs={{0,1},{1,0},{2,3},{3,2},{4,5},{5,4},{6,7},{7,6},{8,9},{9,8},{10,11... | collective-permute-start | bytes 24584 | tf_op jit(solution)/shard_map/ppermute | solution.py:721
  4.0 1.2 %collective-permute-start = (f32[2,2,4,128]{3,2,1,0:T(4,128)}, f32[2,2,4,128]{3,2,1,0:T(4,128)S(1)}, u32[]{:S(2)}, u32[]{:S(2)}) collective-permute-start(f32[2,2,4,128]{3,2,1,0:T(4,128)} %param.8), channel_id=1, source_target_pairs={{0,29},{1,4},{2,31},{3,6},{4,1},{5,8},{6,3},{7,10},{8,5},{9,12},{1... | collective-permute-start | bytes 24584 | tf_op jit(solution)/shard_map/ppermute | solution.py:721
  5.2 0.7 copy-done.4
  6.2 1.7 %collective-permute-start.2 = (f32[2,4,4,128]{3,2,1,0:T(4,128)S(1)}, f32[2,4,4,128]{3,2,1,0:T(4,128)S(1)}, u32[]{:S(2)}, u32[]{:S(2)}) collective-permute-start(f32[2,4,4,128]{3,2,1,0:T(4,128)S(1)} %pad_maximum_fusion.10), channel_id=1, source_target_pairs={{0,2},{1,3},{2,0},{3,1},{4,6},{5,7},{6,4},{7,5},{8,10},{9,11},{10,... | collective-permute-start | bytes 49160 | tf_op jit(solution)/shard_map/ppermute | solution.py:721
  8.0 3.0 %collective-permute-start.3 = (f32[2,4,4,128]{3,2,1,0:T(4,128)S(1)}, f32[2,4,4,128]{3,2,1,0:T(4,128)S(1)}, u32[]{:S(2)}, u32[]{:S(2)}) collective-permute-start(f32[2,4,4,128]{3,2,1,0:T(4,128)S(1)} %pad_maximum_fusion.10), channel_id=1, source_target_pairs={{0,30},{1,31},{2,4},{3,5},{4,2},{5,3},{6,8},{7,9},{8,6},{9,7},{10,... | collective-permute-start | bytes 49160 | tf_op jit(solution)/shard_map/ppermute | solution.py:721
  11.0 0.2 maximum_bitcast_fusion
  11.2 0.5 pad_maximum_fusion
  11.6 0.3 copy.39
  11.9 0.1 copy.40
  12.1 0.7 pad_maximum_fusion.3.taps3_ref
  12.8 0.1 reshape.105
  12.9 0.1 reshape.104
  13.2 0.1 copy.37
  13.3 0.6 shard_map.152
  13.9 0.6 copy-done.2
  14.6 0.7 copy-done.3
  15.3 0.1 copy.51
  15.4 0.6 pad.14.small_ref
  16.0 0.7 shard_map.151
  16.7 6.4 %all-to-all-start = ((bf16[8,2,56,128]{3,2,1,0:T(8,128)(2,1)}), bf16[8,2,56,128]{3,2,1,0:T(8,128)(2,1)S(1)}, u32[]{:S(2)}, u32[]{:S(2)}) async-start(bf16[8,2,56,128]{3,2,1,0:T(8,128)(2,1)} %shard_map.151), calls=%async_computation | async-start | bytes 458752 | tf_op jit(solution)/shard_map/all_to_all | solution.py:786
  23.1 7.2 %all-to-all-done = bf16[8,2,56,128]{3,2,1,0:T(8,128)(2,1)S(1)} async-done(((bf16[8,2,56,128]{3,2,1,0:T(8,128)(2,1)}), bf16[8,2,56,128]{3,2,1,0:T(8,128)(2,1)S(1)}, u32[]{:S(2)}, u32[]{:S(2)}) %all-to-all-start) | async-done | bytes 229408 | tf_op jit(solution)/shard_map/all_to_all | solution.py:786
  30.3 0.7 copy-done.6
  31.0 17.5 %shard_map.153 = (f32[3,2,8,128]{3,2,1,0:T(8,128)}, bf16[4,128,128]{2,1,0:T(8,128)(2,1)}, bf16[4,64,128]{2,1,0:T(8,128)(2,1)}, bf16[4,64,128]{2,1,0:T(8,128)(2,1...) custom-call(bf16[16,56,128]{2,1,0:T(8,128)(2,1)} %bitcast.69, bf16[144,32]{1,0:T(8,128)(2,1)} %pad.14.small_ref, ...), custom_call_target="tpu_custom_call" | custom-call | tf_op jit(solution)/shard_map/pallas_call | solution.py:544
  48.5 3.3 %collective-permute-start.4 = (f32[144,128]{1,0:T(8,128)}, f32[144,128]{1,0:T(8,128)S(1)}, u32[]{:S(2)}, u32[]{:S(2)}) collective-permute-start(f32[144,128]{1,0:T(8,128)} %get-tuple-element.43), channel_id=1, source_target_pairs={{0,1},{1,0},{2,3},{3,2},{4,5},{5,4},{6,7},{7,6},{8,9},{9,8},{10,11... | collective-permute-start | bytes 221192 | tf_op jit(solution)/shard_map/ppermute | solution.py:721
  51.8 1.1 %collective-permute-done.4 = f32[144,128]{1,0:T(8,128)S(1)} collective-permute-done((f32[144,128]{1,0:T(8,128)}, f32[144,128]{1,0:T(8,128)S(1)}, u32[]{:S(2)}, u32[]{:S(2)}) %collective-permute-start.4) | collective-permute-done | bytes 73760 | tf_op jit(solution)/shard_map/ppermute | solution.py:721
  52.9 0.9 %reduce-precision_convert_fusion.1 = (bf16[144,128]{1,0:T(8,128)(2,1)S(1)}, f32[144,128]{1,0:T(8,128)S(1)}) fusion(f32[144,128]{1,0:T(8,128)} %get-tuple-element.42, f32[144,128]{1,0:T(8,128)S(1)} %collective-permute-done.4), kind=kLoop, calls=%fused_computation.51 | loop fusion | flops 55296 | bytes 258048 | tf_op jit(solution)/shard_map/convert.6
  53.8 0.1 collective-permute-start.5
  54.0 2.8 %collective-permute-done.5 = bf16[152,128]{1,0:T(8,128)(2,1)S(1)} collective-permute-done((bf16[152,128]{1,0:T(8,128)(2,1)S(1)}, bf16[152,128]{1,0:T(8,128)(2,1)S(1)}, u32[]{:S(2)}, u32[]{:S(2)}) %collective-permute-start.5) | collective-permute-done | bytes 38944 | tf_op jit(solution)/shard_map/ppermute | solution.py:721
  56.9 0.1 collective-permute-start.6
  57.0 0.7 copy-done.11
  57.7 1.5 %collective-permute-start.7 = (bf16[4,64,128]{2,1,0:T(8,128)(2,1)S(1)}, bf16[4,64,128]{2,1,0:T(8,128)(2,1)S(1)}, u32[]{:S(2)}, u32[]{:S(2)}) collective-permute-start(bf16[4,64,128]{2,1,0:T(8,128)(2,1)S(1)} %copy-done.11), channel_id=1, source_target_pairs={{0,1},{1,0},{2,3},{3,2},{4,5},{5,4},{6,7},{7,6},{8,9},{9,8},{10,11... | collective-permute-start | bytes 196616 | tf_op jit(solution)/shard_map/ppermute | solution.py:721
  59.2 1.1 %collective-permute-start.8 = (bf16[4,64,128]{2,1,0:T(8,128)(2,1)S(1)}, bf16[4,64,128]{2,1,0:T(8,128)(2,1)S(1)}, u32[]{:S(2)}, u32[]{:S(2)}) collective-permute-start(bf16[4,64,128]{2,1,0:T(8,128)(2,1)S(1)} %copy-done.10), channel_id=1, source_target_pairs={{0,31},{1,2},{2,1},{3,4},{4,3},{5,6},{6,5},{7,8},{8,7},{9,10},{10,... | collective-permute-start | bytes 196616 | tf_op jit(solution)/shard_map/ppermute | solution.py:721
  60.5 2.5 %collective-permute-done.8.beyond_ref = bf16[4,64,128]{2,1,0:T(8,128)(2,1)S(1)} collective-permute-done((bf16[4,64,128]{2,1,0:T(8,128)(2,1)S(1)}, bf16[4,64,128]{2,1,0:T(8,128)(2,1)S(1)}, u32[]{:S(2)}, u32[]{:S(2)}) %collective-permute-start.8) | collective-permute-done | bytes 65568 | tf_op jit(solution)/shard_map/ppermute | solution.py:721
  63.0 4.3 %collective-permute-start.9 = (bf16[152,128]{1,0:T(8,128)(2,1)S(1)}, bf16[152,128]{1,0:T(8,128)(2,1)S(1)}, u32[]{:S(2)}, u32[]{:S(2)}) collective-permute-start(bf16[152,128]{1,0:T(8,128)(2,1)S(1)} %pad_maximum_fusion.6), channel_id=1, source_target_pairs={{0,14},{1,15},{2,4},{3,5},{4,2},{5,3},{6,8},{7,9},{8,6},{9,7},{10,... | collective-permute-start | bytes 116744 | tf_op jit(solution)/shard_map/ppermute | solution.py:721
  67.3 0.1 copy.46
  67.4 0.1 copy.50
  67.5 0.1 copy.43
  67.6 0.1 copy.47
  67.8 0.1 copy.48
  67.9 0.1 copy.49
  68.0 0.7 collective-permute-done.9
  68.8 1.8 %collective-permute-start.10 = (bf16[152,128]{1,0:T(8,128)(2,1)S(1)}, bf16[152,128]{1,0:T(8,128)(2,1)S(1)}, u32[]{:S(2)}, u32[]{:S(2)}) collective-permute-start(bf16[152,128]{1,0:T(8,128)(2,1)S(1)} %pad_maximum_fusion.7), channel_id=1, source_target_pairs={{0,6},{1,7},{2,12},{3,13},{4,10},{5,11},{6,0},{7,1},{8,14},{9,15},... | collective-permute-start | bytes 116744 | tf_op jit(solution)/shard_map/ppermute | solution.py:721
  70.6 0.4 maximum_maximum_fusion.taps_ref
  71.0 0.9 %shard_map.154 = (f32[2,8,128]{2,1,0:T(8,128)}, f32[2,8,128]{2,1,0:T(8,128)}) custom-call(bf16[4,64,128]{2,1,0:T(8,128)(2,1)S(1)} %collective-permute-done.7.partner_ref, bf16[4,64,128]{2,1,0:T(8,128)(2,1)S(1)} %collective-permute-done.8.beyond_ref, bf16[4,128,128]{2,1,0:T(8,128)(2,1)S(1)} %copy-done.1, ...), custom_call_target="tpu_custom_call" | custom-call | tf_op jit(solution)/shard_map/pallas_call | solution.py:590
  71.9 1.7 %collective-permute-done.10 = bf16[152,128]{1,0:T(8,128)(2,1)S(1)} collective-permute-done((bf16[152,128]{1,0:T(8,128)(2,1)S(1)}, bf16[152,128]{1,0:T(8,128)(2,1)S(1)}, u32[]{:S(2)}, u32[]{:S(2)}) %collective-permute-start.10) | collective-permute-done | bytes 38944 | tf_op jit(solution)/shard_map/ppermute | solution.py:721
  73.7 2.8 %collective-permute-start.11 = (f32[144,128]{1,0:T(8,128)S(1)}, f32[144,128]{1,0:T(8,128)S(1)}, u32[]{:S(2)}, u32[]{:S(2)}) collective-permute-start(f32[144,128]{1,0:T(8,128)S(1)} %pad_maximum_fusion.2.mine_ref), channel_id=1, source_target_pairs={{0,1},{1,0},{2,3},{3,2},{4,5},{5,4},{6,7},{7,6},{8,9},{9,8},{10,11... | collective-permute-start | bytes 221192 | tf_op jit(solution)/shard_map/ppermute | solution.py:721
  76.6 0.9 %collective-permute-done.11.theirs_ref = f32[144,128]{1,0:T(8,128)S(1)} collective-permute-done((f32[144,128]{1,0:T(8,128)S(1)}, f32[144,128]{1,0:T(8,128)S(1)}, u32[]{:S(2)}, u32[]{:S(2)}) %collective-permute-start.11) | collective-permute-done | bytes 73760 | tf_op jit(solution)/shard_map/ppermute | solution.py:721
  77.5 1.1 %shard_map.155 = (f32[1,1]{1,0:T(1,128)}, f32[81,1,16]{2,1,0:T(1,128)}, f32[1,16]{1,0:T(1,128)}, f32[81,16,16]{2,1,0:T(8,128)}, f32[1,16]{1,0:T(1,128)}, /*index=5*/f32[81,2,16]{2,1,0:T(2,128)}, f32[1,2]{1,0:T(1,128)}) custom-call(f32[144,128]{1,0:T(8,128)S(1)} %pad_maximum_fusion.2.mine_ref, f32[144,128]{1,0:T(8,128)S(1)} %collective-permute-done.11.theirs_ref), custom_call_target="tpu_custom_call" | custom-call | tf_op jit(solution)/shard_map/pallas_call | solution.py:653
  (78 shorter events, 0.8 us)
Async XLA Ops:
  0.6 4.6 %collective-permute-start.1 = (f32[2,2,4,128]{3,2,1,0:T(4,128)}, f32[2,2,4,128]{3,2,1,0:T(4,128)S(1)}, u32[]{:S(2)}, u32[]{:S(2)}) collective-permute-start(f32[2,2,4,128]{3,2,1,0:T(4,128)} %param.8), channel_id=1, source_target_pairs={{0,1},{1,0},{2,3},{3,2},{4,5},{5,4},{6,7},{7,6},{8,9},{9,8},{10,11... | collective-permute-start | bytes 24584 | tf_op jit(solution)/shard_map/ppermute | solution.py:721
  4.0 12.0 %collective-permute-start = (f32[2,2,4,128]{3,2,1,0:T(4,128)}, f32[2,2,4,128]{3,2,1,0:T(4,128)S(1)}, u32[]{:S(2)}, u32[]{:S(2)}) collective-permute-start(f32[2,2,4,128]{3,2,1,0:T(4,128)} %param.8), channel_id=1, source_target_pairs={{0,29},{1,4},{2,31},{3,6},{4,1},{5,8},{6,3},{7,10},{8,5},{9,12},{1... | collective-permute-start | bytes 24584 | tf_op jit(solution)/shard_map/ppermute | solution.py:721
  5.2 0.7 copy-start.4
  5.2 0.8 %copy-start.8 = (bf16[2,16,3,3,3,3]{1,0,5,4,3,2:T(2,128)(2,1)S(1)}, bf16[2,16,3,3,3,3]{1,0,5,4,3,2:T(2,128)(2,1)}, u32[]{:S(2)}) copy-start(bf16[2,16,3,3,3,3]{1,0,5,4,3,2:T(2,128)(2,1)} %param.13) | copy-start | bytes 15556
  6.2 9.8 %collective-permute-start.2 = (f32[2,4,4,128]{3,2,1,0:T(4,128)S(1)}, f32[2,4,4,128]{3,2,1,0:T(4,128)S(1)}, u32[]{:S(2)}, u32[]{:S(2)}) collective-permute-start(f32[2,4,4,128]{3,2,1,0:T(4,128)S(1)} %pad_maximum_fusion.10), channel_id=1, source_target_pairs={{0,2},{1,3},{2,0},{3,1},{4,6},{5,7},{6,4},{7,5},{8,10},{9,11},{10,... | collective-permute-start | bytes 49160 | tf_op jit(solution)/shard_map/ppermute | solution.py:721
  8.0 8.0 %collective-permute-start.3 = (f32[2,4,4,128]{3,2,1,0:T(4,128)S(1)}, f32[2,4,4,128]{3,2,1,0:T(4,128)S(1)}, u32[]{:S(2)}, u32[]{:S(2)}) collective-permute-start(f32[2,4,4,128]{3,2,1,0:T(4,128)S(1)} %pad_maximum_fusion.10), channel_id=1, source_target_pairs={{0,30},{1,31},{2,4},{3,5},{4,2},{5,3},{6,8},{7,9},{8,6},{9,7},{10,... | collective-permute-start | bytes 49160 | tf_op jit(solution)/shard_map/ppermute | solution.py:721
  11.6 1.3 %copy-start.9 = (bf16[16,1,3,3,3,3]{0,5,4,3,2,1:T(4,128)(2,1)S(1)}, bf16[16,1,3,3,3,3]{0,5,4,3,2,1:T(4,128)(2,1)}, u32[]{:S(2)}) copy-start(bf16[16,1,3,3,3,3]{0,5,4,3,2,1:T(4,128)(2,1)} %param.9) | copy-start | bytes 7780
  11.9 1.4 %copy-start = (bf16[16,16,3,3,3,3]{1,0,5,4,3,2:T(8,128)(2,1)S(1)}, bf16[16,16,3,3,3,3]{1,0,5,4,3,2:T(8,128)(2,1)}, u32[]{:S(2)}) copy-start(bf16[16,16,3,3,3,3]{1,0,5,4,3,2:T(8,128)(2,1)} %param.11) | copy-start | bytes 124420
  13.9 0.7 copy-start.2
  14.5 0.7 copy-start.3
  15.2 41.8 %copy-start.7 = (bf16[27,1,3,16]{3,0,2,1:T(8,128)(2,1)}, bf16[27,1,3,16]{3,0,2,1:T(8,128)(2,1)S(1)}, u32[]{:S(2)}) copy-start(bf16[27,1,3,16]{3,0,2,1:T(8,128)(2,1)S(1)} %reshape.112) | copy-start | bytes 7780
  16.7 13.6 %all-to-all-start = ((bf16[8,2,56,128]{3,2,1,0:T(8,128)(2,1)}), bf16[8,2,56,128]{3,2,1,0:T(8,128)(2,1)S(1)}, u32[]{:S(2)}, u32[]{:S(2)}) async-start(bf16[8,2,56,128]{3,2,1,0:T(8,128)(2,1)} %shard_map.151), calls=%async_computation | async-start | bytes 458752 | tf_op jit(solution)/shard_map/all_to_all | solution.py:786
  30.3 0.7 copy-start.6
  48.5 4.4 %collective-permute-start.4 = (f32[144,128]{1,0:T(8,128)}, f32[144,128]{1,0:T(8,128)S(1)}, u32[]{:S(2)}, u32[]{:S(2)}) collective-permute-start(f32[144,128]{1,0:T(8,128)} %get-tuple-element.43), channel_id=1, source_target_pairs={{0,1},{1,0},{2,3},{3,2},{4,5},{5,4},{6,7},{7,6},{8,9},{9,8},{10,11... | collective-permute-start | bytes 221192 | tf_op jit(solution)/shard_map/ppermute | solution.py:721
  53.8 2.9 %collective-permute-start.5 = (bf16[152,128]{1,0:T(8,128)(2,1)S(1)}, bf16[152,128]{1,0:T(8,128)(2,1)S(1)}, u32[]{:S(2)}, u32[]{:S(2)}) collective-permute-start(bf16[152,128]{1,0:T(8,128)(2,1)S(1)} %pad_maximum_fusion.4), channel_id=1, source_target_pairs={{0,16},{1,17},{2,18},{3,19},{4,20},{5,21},{6,22},{7,23},{8,24},{9,... | collective-permute-start | bytes 116744 | tf_op jit(solution)/shard_map/ppermute | solution.py:721
  56.9 0.8 %copy-start.11 = (bf16[4,64,128]{2,1,0:T(8,128)(2,1)S(1)}, bf16[4,64,128]{2,1,0:T(8,128)(2,1)}, u32[]{:S(2)}) copy-start(bf16[4,64,128]{2,1,0:T(8,128)(2,1)} %get-tuple-element.44) | copy-start | bytes 196612
  56.9 2.3 %copy-start.10 = (bf16[4,64,128]{2,1,0:T(8,128)(2,1)S(1)}, bf16[4,64,128]{2,1,0:T(8,128)(2,1)}, u32[]{:S(2)}) copy-start(bf16[4,64,128]{2,1,0:T(8,128)(2,1)} %get-tuple-element.45) | copy-start | bytes 196612
  56.9 3.5 %collective-permute-start.6 = (bf16[152,128]{1,0:T(8,128)(2,1)S(1)}, bf16[152,128]{1,0:T(8,128)(2,1)S(1)}, u32[]{:S(2)}, u32[]{:S(2)}) collective-permute-start(bf16[152,128]{1,0:T(8,128)(2,1)S(1)} %pad_maximum_fusion.5), channel_id=1, source_target_pairs={{0,2},{1,3},{2,0},{3,1},{4,6},{5,7},{6,4},{7,5},{8,10},{9,11},{10,... | collective-permute-start | bytes 116744 | tf_op jit(solution)/shard_map/ppermute | solution.py:721
  57.7 2.7 %collective-permute-start.7 = (bf16[4,64,128]{2,1,0:T(8,128)(2,1)S(1)}, bf16[4,64,128]{2,1,0:T(8,128)(2,1)S(1)}, u32[]{:S(2)}, u32[]{:S(2)}) collective-permute-start(bf16[4,64,128]{2,1,0:T(8,128)(2,1)S(1)} %copy-done.11), channel_id=1, source_target_pairs={{0,1},{1,0},{2,3},{3,2},{4,5},{5,4},{6,7},{7,6},{8,9},{9,8},{10,11... | collective-permute-start | bytes 196616 | tf_op jit(solution)/shard_map/ppermute | solution.py:721
  59.2 3.7 %collective-permute-start.8 = (bf16[4,64,128]{2,1,0:T(8,128)(2,1)S(1)}, bf16[4,64,128]{2,1,0:T(8,128)(2,1)S(1)}, u32[]{:S(2)}, u32[]{:S(2)}) collective-permute-start(bf16[4,64,128]{2,1,0:T(8,128)(2,1)S(1)} %copy-done.10), channel_id=1, source_target_pairs={{0,31},{1,2},{2,1},{3,4},{4,3},{5,6},{6,5},{7,8},{8,7},{9,10},{10,... | collective-permute-start | bytes 196616 | tf_op jit(solution)/shard_map/ppermute | solution.py:721
  62.9 4.4 %slice-start = ((bf16[27,1,3,16]{3,0,2,1:T(8,128)(2,1)}), bf16[27,1,1,16]{3,0,2,1:T(8,128)(2,1)S(1)}, s32[]{:S(2)}) async-start(bf16[27,1,3,16]{3,0,2,1:T(8,128)(2,1)} %copy-done.7), calls=%async_computation.1 | async-start | bytes 16384 | tf_op jit(solution)/shard_map/jit(_roll_static)/slice | solution.py:715
  63.0 5.7 %collective-permute-start.9 = (bf16[152,128]{1,0:T(8,128)(2,1)S(1)}, bf16[152,128]{1,0:T(8,128)(2,1)S(1)}, u32[]{:S(2)}, u32[]{:S(2)}) collective-permute-start(bf16[152,128]{1,0:T(8,128)(2,1)S(1)} %pad_maximum_fusion.6), channel_id=1, source_target_pairs={{0,14},{1,15},{2,4},{3,5},{4,2},{5,3},{6,8},{7,9},{8,6},{9,7},{10,... | collective-permute-start | bytes 116744 | tf_op jit(solution)/shard_map/ppermute | solution.py:721
  68.8 2.2 %copy-start.1 = (bf16[4,128,128]{2,1,0:T(8,128)(2,1)S(1)}, bf16[4,128,128]{2,1,0:T(8,128)(2,1)}, u32[]{:S(2)}) copy-start(bf16[4,128,128]{2,1,0:T(8,128)(2,1)} %get-tuple-element.49.own_ref) | copy-start | bytes 393220
  68.8 2.2 %copy-start.5 = (f32[3,2,8,128]{3,2,1,0:T(8,128)S(1)}, f32[3,2,8,128]{3,2,1,0:T(8,128)}, u32[]{:S(2)}) copy-start(f32[3,2,8,128]{3,2,1,0:T(8,128)} %get-tuple-element.50.parts_ref) | copy-start | bytes 73732
  68.8 4.8 %collective-permute-start.10 = (bf16[152,128]{1,0:T(8,128)(2,1)S(1)}, bf16[152,128]{1,0:T(8,128)(2,1)S(1)}, u32[]{:S(2)}, u32[]{:S(2)}) collective-permute-start(bf16[152,128]{1,0:T(8,128)(2,1)S(1)} %pad_maximum_fusion.7), channel_id=1, source_target_pairs={{0,6},{1,7},{2,12},{3,13},{4,10},{5,11},{6,0},{7,1},{8,14},{9,15},... | collective-permute-start | bytes 116744 | tf_op jit(solution)/shard_map/ppermute | solution.py:721
  73.7 3.8 %collective-permute-start.11 = (f32[144,128]{1,0:T(8,128)S(1)}, f32[144,128]{1,0:T(8,128)S(1)}, u32[]{:S(2)}, u32[]{:S(2)}) collective-permute-start(f32[144,128]{1,0:T(8,128)S(1)} %pad_maximum_fusion.2.mine_ref), channel_id=1, source_target_pairs={{0,1},{1,0},{2,3},{3,2},{4,5},{5,4},{6,7},{7,6},{8,9},{9,8},{10,11... | collective-permute-start | bytes 221192 | tf_op jit(solution)/shard_map/ppermute | solution.py:721

commit v5 on v3

--- a/solution.py
+++ b/solution.py
@@ -215,7 +215,7 @@
         h1[2 * xp + 2, row, :] = out[128:]
         return 0
 
-    lax.fori_loop(0, 24, first_body, 0, unroll=12)
+    lax.fori_loop(0, 24, first_body, 0, unroll=24)
     wrap(h1)
 
     def second_body(step, _):
@@ -228,7 +228,7 @@
         h2[xl + 1, pl.ds(pl.multiple_of(yp * 128, 128), 128), :] = out.astype(BF16)
         return 0
 
-    lax.fori_loop(0, 40, second_body, 0, unroll=20)
+    lax.fori_loop(0, 40, second_body, 0, unroll=40)
     wrap(h2)
 
     top = iota((8, 256), 0) < 4

time: 77.5 us -> 76.6 us (0.988)
  no operation moved by 1% of the time
where the time goes in v5:
time: 76.6 us; the launch traced here: 76.2 us
  starting transfers between devices  30.1 us (39%)
  Pallas kernels  20.8 us (27%)
  waiting for transfers between devices  16.8 us (22%)
  local copies, waits for them, and re-layouts  5.75 us (8%)
  other arithmetic  1.94 us (3%)
  between operations  0.9 us (1%)
    ppermute x12, starting transfers between devices, swapped(): return lax.ppermute(v, 'gy', [(i, partner(i)) for i in range(axis_size)])  23.7 us
    pallas_call x1, Pallas kernels, run_main(): pl.pallas_call(main_kernel, out_shape=(jax.ShapeDtypeStruct((3, 2, 8, 128...  17.5 us
    ppermute x12, waiting for transfers between devices, swapped(): return lax.ppermute(v, 'gy', [(i, partner(i)) for i in range(axis_size)])  9.62 us
    all_to_all x1, waiting for transfers between devices, local(): lax.all_to_all(sent, 'gx', 0, 0, tiled=True).reshape(16, 4 * ROWS, 128)  7.19 us
    all_to_all x1, starting transfers between devices, local(): lax.all_to_all(sent, 'gx', 0, 0, tiled=True).reshape(16, 4 * ROWS, 128)  6.36 us
    unnamed x27, local copies, waits for them, and re-layouts  3.35 us
  transfers between devices with their start and end apart: 13, of which 6 were waited for; matrix products, arithmetic and copies ran while one was open for 6% of the time, Pallas kernels for 2%

profile of v5, /device:TPU:1, one launch (start us, length us, event | category | flops | bytes accessed | tf_op | source)
XLA Modules:
  0.0 76.2 jit_solution(4443781325567222141)
XLA Ops:
  0.6 3.3 %collective-permute-start.1 = (f32[2,2,4,128]{3,2,1,0:T(4,128)}, f32[2,2,4,128]{3,2,1,0:T(4,128)S(1)}, u32[]{:S(2)}, u32[]{:S(2)}) collective-permute-start(f32[2,2,4,128]{3,2,1,0:T(4,128)} %param.8), channel_id=1, source_target_pairs={{0,1},{1,0},{2,3},{3,2},{4,5},{5,4},{6,7},{7,6},{8,9},{9,8},{10,11... | collective-permute-start | bytes 24584 | tf_op jit(solution)/shard_map/ppermute | solution.py:720
  4.0 1.2 %collective-permute-start = (f32[2,2,4,128]{3,2,1,0:T(4,128)}, f32[2,2,4,128]{3,2,1,0:T(4,128)S(1)}, u32[]{:S(2)}, u32[]{:S(2)}) collective-permute-start(f32[2,2,4,128]{3,2,1,0:T(4,128)} %param.8), channel_id=1, source_target_pairs={{0,29},{1,4},{2,31},{3,6},{4,1},{5,8},{6,3},{7,10},{8,5},{9,12},{1... | collective-permute-start | bytes 24584 | tf_op jit(solution)/shard_map/ppermute | solution.py:720
  5.2 0.7 copy-done.4
  6.2 0.1 pad_bitcast_fusion.1
  6.2 1.7 %collective-permute-start.2 = (f32[2,4,4,128]{3,2,1,0:T(4,128)S(1)}, f32[2,4,4,128]{3,2,1,0:T(4,128)S(1)}, u32[]{:S(2)}, u32[]{:S(2)}) collective-permute-start(f32[2,4,4,128]{3,2,1,0:T(4,128)S(1)} %pad_maximum_fusion.4), channel_id=1, source_target_pairs={{0,2},{1,3},{2,0},{3,1},{4,6},{5,7},{6,4},{7,5},{8,10},{9,11},{10,... | collective-permute-start | bytes 49160 | tf_op jit(solution)/shard_map/ppermute | solution.py:720
  8.0 3.0 %collective-permute-start.3 = (f32[2,4,4,128]{3,2,1,0:T(4,128)S(1)}, f32[2,4,4,128]{3,2,1,0:T(4,128)S(1)}, u32[]{:S(2)}, u32[]{:S(2)}) collective-permute-start(f32[2,4,4,128]{3,2,1,0:T(4,128)S(1)} %pad_maximum_fusion.4), channel_id=1, source_target_pairs={{0,30},{1,31},{2,4},{3,5},{4,2},{5,3},{6,8},{7,9},{8,6},{9,7},{10,... | collective-permute-start | bytes 49160 | tf_op jit(solution)/shard_map/ppermute | solution.py:720
  11.0 0.2 maximum_bitcast_fusion
  11.2 0.5 pad_maximum_fusion
  11.6 0.3 copy.39
  11.9 0.1 copy.40
  12.1 0.7 pad_maximum_fusion.1.taps3_ref
  12.8 0.1 reshape.105
  12.9 0.1 reshape.104
  13.0 0.1 pad_maximum_fusion.5
  13.2 0.1 copy.51
  13.3 0.1 copy.37
  13.4 0.6 shard_map.152
  14.1 0.6 copy-done.2
  14.7 0.6 copy-done.3
  15.3 0.6 pad.14.small_ref
  16.0 0.7 shard_map.151
  16.7 6.4 %all-to-all-start = ((bf16[8,2,56,128]{3,2,1,0:T(8,128)(2,1)}), bf16[8,2,56,128]{3,2,1,0:T(8,128)(2,1)S(1)}, u32[]{:S(2)}, u32[]{:S(2)}) async-start(bf16[8,2,56,128]{3,2,1,0:T(8,128)(2,1)} %shard_map.151), calls=%async_computation | async-start | bytes 458752 | tf_op jit(solution)/shard_map/all_to_all | solution.py:776
  23.1 7.2 %all-to-all-done = bf16[8,2,56,128]{3,2,1,0:T(8,128)(2,1)S(1)} async-done(((bf16[8,2,56,128]{3,2,1,0:T(8,128)(2,1)}), bf16[8,2,56,128]{3,2,1,0:T(8,128)(2,1)S(1)}, u32[]{:S(2)}, u32[]{:S(2)}) %all-to-all-start) | async-done | bytes 229408 | tf_op jit(solution)/shard_map/all_to_all | solution.py:776
  30.3 0.7 copy-done.6
  30.9 17.5 %shard_map.153 = (f32[3,2,8,128]{3,2,1,0:T(8,128)}, bf16[4,128,128]{2,1,0:T(8,128)(2,1)}, bf16[4,64,128]{2,1,0:T(8,128)(2,1)}, bf16[4,64,128]{2,1,0:T(8,128)(2,1...) custom-call(bf16[16,56,128]{2,1,0:T(8,128)(2,1)} %bitcast.69, bf16[144,32]{1,0:T(8,128)(2,1)} %pad.14.small_ref, ...), custom_call_target="tpu_custom_call" | custom-call | tf_op jit(solution)/shard_map/pallas_call | solution.py:543
  48.4 3.3 %collective-permute-start.4 = (f32[144,128]{1,0:T(8,128)}, f32[144,128]{1,0:T(8,128)S(1)}, u32[]{:S(2)}, u32[]{:S(2)}) collective-permute-start(f32[144,128]{1,0:T(8,128)} %get-tuple-element.43), channel_id=1, source_target_pairs={{0,1},{1,0},{2,3},{3,2},{4,5},{5,4},{6,7},{7,6},{8,9},{9,8},{10,11... | collective-permute-start | bytes 221192 | tf_op jit(solution)/shard_map/ppermute | solution.py:720
  51.8 0.1 copy.46
  51.9 0.1 copy.50
  52.0 0.9 %collective-permute-done.4 = f32[144,128]{1,0:T(8,128)S(1)} collective-permute-done((f32[144,128]{1,0:T(8,128)}, f32[144,128]{1,0:T(8,128)S(1)}, u32[]{:S(2)}, u32[]{:S(2)}) %collective-permute-start.4) | collective-permute-done | bytes 73760 | tf_op jit(solution)/shard_map/ppermute | solution.py:720
  52.9 0.1 collective-permute-start.5
  53.0 3.2 %collective-permute-done.5 = f32[144,128]{1,0:T(8,128)S(1)} collective-permute-done((f32[144,128]{1,0:T(8,128)S(1)}, f32[144,128]{1,0:T(8,128)S(1)}, u32[]{:S(2)}, u32[]{:S(2)}) %collective-permute-start.5) | collective-permute-done | bytes 73760 | tf_op jit(solution)/shard_map/ppermute | solution.py:720
  56.2 0.1 collective-permute-start.6
  56.4 0.1 copy.43
  56.5 0.1 copy.47
  56.6 0.5 copy-done.12
  57.0 1.5 %collective-permute-start.8 = (bf16[4,64,128]{2,1,0:T(8,128)(2,1)S(1)}, bf16[4,64,128]{2,1,0:T(8,128)(2,1)S(1)}, u32[]{:S(2)}, u32[]{:S(2)}) collective-permute-start(bf16[4,64,128]{2,1,0:T(8,128)(2,1)S(1)} %copy-done.12), channel_id=1, source_target_pairs={{0,1},{1,0},{2,3},{3,2},{4,5},{5,4},{6,7},{7,6},{8,9},{9,8},{10,11... | collective-permute-start | bytes 196616 | tf_op jit(solution)/shard_map/ppermute | solution.py:720
  58.5 1.3 %collective-permute-start.9 = (bf16[4,64,128]{2,1,0:T(8,128)(2,1)S(1)}, bf16[4,64,128]{2,1,0:T(8,128)(2,1)S(1)}, u32[]{:S(2)}, u32[]{:S(2)}) collective-permute-start(bf16[4,64,128]{2,1,0:T(8,128)(2,1)S(1)} %copy-done.11), channel_id=1, source_target_pairs={{0,31},{1,2},{2,1},{3,4},{4,3},{5,6},{6,5},{7,8},{8,7},{9,10},{10,... | collective-permute-start | bytes 196616 | tf_op jit(solution)/shard_map/ppermute | solution.py:720
  59.9 1.9 %collective-permute-start.7 = (f32[144,128]{1,0:T(8,128)S(1)}, f32[144,128]{1,0:T(8,128)S(1)}, u32[]{:S(2)}, u32[]{:S(2)}) collective-permute-start(f32[144,128]{1,0:T(8,128)S(1)} %add.32), channel_id=1, source_target_pairs={{0,14},{1,15},{2,4},{3,5},{4,2},{5,3},{6,8},{7,9},{8,6},{9,7},{10,... | collective-permute-start | bytes 221192 | tf_op jit(solution)/shard_map/ppermute | solution.py:720
  61.8 0.1 copy.48
  61.9 0.1 copy.49
  62.0 2.4 %collective-permute-done.7 = f32[144,128]{1,0:T(8,128)S(1)} collective-permute-done((f32[144,128]{1,0:T(8,128)S(1)}, f32[144,128]{1,0:T(8,128)S(1)}, u32[]{:S(2)}, u32[]{:S(2)}) %collective-permute-start.7) | collective-permute-done | bytes 73760 | tf_op jit(solution)/shard_map/ppermute | solution.py:720
  64.4 1.6 %collective-permute-start.10 = (f32[144,128]{1,0:T(8,128)S(1)}, f32[144,128]{1,0:T(8,128)S(1)}, u32[]{:S(2)}, u32[]{:S(2)}) collective-permute-start(f32[144,128]{1,0:T(8,128)S(1)} %add.33), channel_id=1, source_target_pairs={{0,6},{1,7},{2,12},{3,13},{4,10},{5,11},{6,0},{7,1},{8,14},{9,15},... | collective-permute-start | bytes 221192 | tf_op jit(solution)/shard_map/ppermute | solution.py:720
  66.0 0.4 maximum_maximum_fusion.taps_ref
  66.4 0.9 %shard_map.154 = (f32[2,8,128]{2,1,0:T(8,128)}, f32[2,8,128]{2,1,0:T(8,128)}) custom-call(bf16[4,64,128]{2,1,0:T(8,128)(2,1)S(1)} %collective-permute-done.8.partner_ref, bf16[4,64,128]{2,1,0:T(8,128)(2,1)S(1)} %collective-permute-done.9.beyond_ref, bf16[4,128,128]{2,1,0:T(8,128)(2,1)S(1)} %copy-done.1, ...), custom_call_target="tpu_custom_call" | custom-call | tf_op jit(solution)/shard_map/pallas_call | solution.py:589
  67.3 2.2 %collective-permute-done.10 = f32[144,128]{1,0:T(8,128)S(1)} collective-permute-done((f32[144,128]{1,0:T(8,128)S(1)}, f32[144,128]{1,0:T(8,128)S(1)}, u32[]{:S(2)}, u32[]{:S(2)}) %collective-permute-start.10) | collective-permute-done | bytes 73760 | tf_op jit(solution)/shard_map/ppermute | solution.py:720
  69.5 4.7 %collective-permute-start.11 = (f32[144,128]{1,0:T(8,128)S(1)}, f32[144,128]{1,0:T(8,128)S(1)}, u32[]{:S(2)}, u32[]{:S(2)}) collective-permute-start(f32[144,128]{1,0:T(8,128)S(1)} %add.34.mine_ref), channel_id=1, source_target_pairs={{0,1},{1,0},{2,3},{3,2},{4,5},{5,4},{6,7},{7,6},{8,9},{9,8},{10,11... | collective-permute-start | bytes 221192 | tf_op jit(solution)/shard_map/ppermute | solution.py:720
  74.2 0.9 %collective-permute-done.11.theirs_ref = f32[144,128]{1,0:T(8,128)S(1)} collective-permute-done((f32[144,128]{1,0:T(8,128)S(1)}, f32[144,128]{1,0:T(8,128)S(1)}, u32[]{:S(2)}, u32[]{:S(2)}) %collective-permute-start.11) | collective-permute-done | bytes 73760 | tf_op jit(solution)/shard_map/ppermute | solution.py:720
  75.1 1.1 %shard_map.155 = (f32[1,1]{1,0:T(1,128)}, f32[81,1,16]{2,1,0:T(1,128)}, f32[1,16]{1,0:T(1,128)}, f32[81,16,16]{2,1,0:T(8,128)}, f32[1,16]{1,0:T(1,128)}, /*index=5*/f32[81,2,16]{2,1,0:T(2,128)}, f32[1,2]{1,0:T(1,128)}) custom-call(f32[144,128]{1,0:T(8,128)S(1)} %add.34.mine_ref, f32[144,128]{1,0:T(8,128)S(1)} %collective-permute-done.11.theirs_ref), custom_call_target="tpu_custom_call" | custom-call | tf_op jit(solution)/shard_map/pallas_call | solution.py:652
  (50 shorter events, 0.5 us)
Async XLA Ops:
  0.6 4.6 %collective-permute-start.1 = (f32[2,2,4,128]{3,2,1,0:T(4,128)}, f32[2,2,4,128]{3,2,1,0:T(4,128)S(1)}, u32[]{:S(2)}, u32[]{:S(2)}) collective-permute-start(f32[2,2,4,128]{3,2,1,0:T(4,128)} %param.8), channel_id=1, source_target_pairs={{0,1},{1,0},{2,3},{3,2},{4,5},{5,4},{6,7},{7,6},{8,9},{9,8},{10,11... | collective-permute-start | bytes 24584 | tf_op jit(solution)/shard_map/ppermute | solution.py:720
  4.0 12.0 %collective-permute-start = (f32[2,2,4,128]{3,2,1,0:T(4,128)}, f32[2,2,4,128]{3,2,1,0:T(4,128)S(1)}, u32[]{:S(2)}, u32[]{:S(2)}) collective-permute-start(f32[2,2,4,128]{3,2,1,0:T(4,128)} %param.8), channel_id=1, source_target_pairs={{0,29},{1,4},{2,31},{3,6},{4,1},{5,8},{6,3},{7,10},{8,5},{9,12},{1... | collective-permute-start | bytes 24584 | tf_op jit(solution)/shard_map/ppermute | solution.py:720
  5.2 0.7 copy-start.4
  5.2 0.8 %copy-start.8 = (bf16[2,16,3,3,3,3]{1,0,5,4,3,2:T(2,128)(2,1)S(1)}, bf16[2,16,3,3,3,3]{1,0,5,4,3,2:T(2,128)(2,1)}, u32[]{:S(2)}) copy-start(bf16[2,16,3,3,3,3]{1,0,5,4,3,2:T(2,128)(2,1)} %param.13) | copy-start | bytes 15556
  6.2 9.7 %collective-permute-start.2 = (f32[2,4,4,128]{3,2,1,0:T(4,128)S(1)}, f32[2,4,4,128]{3,2,1,0:T(4,128)S(1)}, u32[]{:S(2)}, u32[]{:S(2)}) collective-permute-start(f32[2,4,4,128]{3,2,1,0:T(4,128)S(1)} %pad_maximum_fusion.4), channel_id=1, source_target_pairs={{0,2},{1,3},{2,0},{3,1},{4,6},{5,7},{6,4},{7,5},{8,10},{9,11},{10,... | collective-permute-start | bytes 49160 | tf_op jit(solution)/shard_map/ppermute | solution.py:720
  8.0 8.0 %collective-permute-start.3 = (f32[2,4,4,128]{3,2,1,0:T(4,128)S(1)}, f32[2,4,4,128]{3,2,1,0:T(4,128)S(1)}, u32[]{:S(2)}, u32[]{:S(2)}) collective-permute-start(f32[2,4,4,128]{3,2,1,0:T(4,128)S(1)} %pad_maximum_fusion.4), channel_id=1, source_target_pairs={{0,30},{1,31},{2,4},{3,5},{4,2},{5,3},{6,8},{7,9},{8,6},{9,7},{10,... | collective-permute-start | bytes 49160 | tf_op jit(solution)/shard_map/ppermute | solution.py:720
  11.6 1.3 %copy-start.9 = (bf16[16,1,3,3,3,3]{0,5,4,3,2,1:T(4,128)(2,1)S(1)}, bf16[16,1,3,3,3,3]{0,5,4,3,2,1:T(4,128)(2,1)}, u32[]{:S(2)}) copy-start(bf16[16,1,3,3,3,3]{0,5,4,3,2,1:T(4,128)(2,1)} %param.9) | copy-start | bytes 7780
  11.9 1.5 %copy-start = (bf16[16,16,3,3,3,3]{1,0,5,4,3,2:T(8,128)(2,1)S(1)}, bf16[16,16,3,3,3,3]{1,0,5,4,3,2:T(8,128)(2,1)}, u32[]{:S(2)}) copy-start(bf16[16,16,3,3,3,3]{1,0,5,4,3,2:T(8,128)(2,1)} %param.11) | copy-start | bytes 124420
  13.2 39.8 %copy-start.7 = (bf16[27,1,3,16]{3,0,2,1:T(8,128)(2,1)}, bf16[27,1,3,16]{3,0,2,1:T(8,128)(2,1)S(1)}, u32[]{:S(2)}) copy-start(bf16[27,1,3,16]{3,0,2,1:T(8,128)(2,1)S(1)} %reshape.112) | copy-start | bytes 7780
  14.1 0.6 copy-start.2
  14.7 0.6 copy-start.3
  16.7 13.6 %all-to-all-start = ((bf16[8,2,56,128]{3,2,1,0:T(8,128)(2,1)}), bf16[8,2,56,128]{3,2,1,0:T(8,128)(2,1)S(1)}, u32[]{:S(2)}, u32[]{:S(2)}) async-start(bf16[8,2,56,128]{3,2,1,0:T(8,128)(2,1)} %shard_map.151), calls=%async_computation | async-start | bytes 458752 | tf_op jit(solution)/shard_map/all_to_all | solution.py:776
  30.3 0.7 copy-start.6
  48.4 4.5 %collective-permute-start.4 = (f32[144,128]{1,0:T(8,128)}, f32[144,128]{1,0:T(8,128)S(1)}, u32[]{:S(2)}, u32[]{:S(2)}) collective-permute-start(f32[144,128]{1,0:T(8,128)} %get-tuple-element.43), channel_id=1, source_target_pairs={{0,1},{1,0},{2,3},{3,2},{4,5},{5,4},{6,7},{7,6},{8,9},{9,8},{10,11... | collective-permute-start | bytes 221192 | tf_op jit(solution)/shard_map/ppermute | solution.py:720
  51.8 1.1 %copy-start.10 = (f32[144,128]{1,0:T(8,128)S(1)}, f32[144,128]{1,0:T(8,128)}, u32[]{:S(2)}) copy-start(f32[144,128]{1,0:T(8,128)} %get-tuple-element.42) | copy-start | bytes 221188
  52.9 3.3 %collective-permute-start.5 = (f32[144,128]{1,0:T(8,128)S(1)}, f32[144,128]{1,0:T(8,128)S(1)}, u32[]{:S(2)}, u32[]{:S(2)}) collective-permute-start(f32[144,128]{1,0:T(8,128)S(1)} %add.30), channel_id=1, source_target_pairs={{0,16},{1,17},{2,18},{3,19},{4,20},{5,21},{6,22},{7,23},{8,24},{9,... | collective-permute-start | bytes 221192 | tf_op jit(solution)/shard_map/ppermute | solution.py:720
  53.0 3.3 %slice-start = ((bf16[27,1,3,16]{3,0,2,1:T(8,128)(2,1)}), bf16[27,1,1,16]{3,0,2,1:T(8,128)(2,1)S(1)}, s32[]{:S(2)}) async-start(bf16[27,1,3,16]{3,0,2,1:T(8,128)(2,1)} %copy-done.7), calls=%async_computation.1 | async-start | bytes 16384 | tf_op jit(solution)/shard_map/jit(_roll_static)/slice | solution.py:714
  56.2 0.8 %copy-start.12 = (bf16[4,64,128]{2,1,0:T(8,128)(2,1)S(1)}, bf16[4,64,128]{2,1,0:T(8,128)(2,1)}, u32[]{:S(2)}) copy-start(bf16[4,64,128]{2,1,0:T(8,128)(2,1)} %get-tuple-element.44) | copy-start | bytes 196612
  56.2 2.3 %copy-start.11 = (bf16[4,64,128]{2,1,0:T(8,128)(2,1)S(1)}, bf16[4,64,128]{2,1,0:T(8,128)(2,1)}, u32[]{:S(2)}) copy-start(bf16[4,64,128]{2,1,0:T(8,128)(2,1)} %get-tuple-element.45) | copy-start | bytes 196612
  56.2 3.7 %collective-permute-start.6 = (f32[144,128]{1,0:T(8,128)S(1)}, f32[144,128]{1,0:T(8,128)S(1)}, u32[]{:S(2)}, u32[]{:S(2)}) collective-permute-start(f32[144,128]{1,0:T(8,128)S(1)} %add.31), channel_id=1, source_target_pairs={{0,2},{1,3},{2,0},{3,1},{4,6},{5,7},{6,4},{7,5},{8,10},{9,11},{10,... | collective-permute-start | bytes 221192 | tf_op jit(solution)/shard_map/ppermute | solution.py:720
  57.0 7.4 %collective-permute-start.8 = (bf16[4,64,128]{2,1,0:T(8,128)(2,1)S(1)}, bf16[4,64,128]{2,1,0:T(8,128)(2,1)S(1)}, u32[]{:S(2)}, u32[]{:S(2)}) collective-permute-start(bf16[4,64,128]{2,1,0:T(8,128)(2,1)S(1)} %copy-done.12), channel_id=1, source_target_pairs={{0,1},{1,0},{2,3},{3,2},{4,5},{5,4},{6,7},{7,6},{8,9},{9,8},{10,11... | collective-permute-start | bytes 196616 | tf_op jit(solution)/shard_map/ppermute | solution.py:720
  58.5 5.9 %collective-permute-start.9 = (bf16[4,64,128]{2,1,0:T(8,128)(2,1)S(1)}, bf16[4,64,128]{2,1,0:T(8,128)(2,1)S(1)}, u32[]{:S(2)}, u32[]{:S(2)}) collective-permute-start(bf16[4,64,128]{2,1,0:T(8,128)(2,1)S(1)} %copy-done.11), channel_id=1, source_target_pairs={{0,31},{1,2},{2,1},{3,4},{4,3},{5,6},{6,5},{7,8},{8,7},{9,10},{10,... | collective-permute-start | bytes 196616 | tf_op jit(solution)/shard_map/ppermute | solution.py:720
  59.9 4.5 %collective-permute-start.7 = (f32[144,128]{1,0:T(8,128)S(1)}, f32[144,128]{1,0:T(8,128)S(1)}, u32[]{:S(2)}, u32[]{:S(2)}) collective-permute-start(f32[144,128]{1,0:T(8,128)S(1)} %add.32), channel_id=1, source_target_pairs={{0,14},{1,15},{2,4},{3,5},{4,2},{5,3},{6,8},{7,9},{8,6},{9,7},{10,... | collective-permute-start | bytes 221192 | tf_op jit(solution)/shard_map/ppermute | solution.py:720
  62.0 4.5 %copy-start.1 = (bf16[4,128,128]{2,1,0:T(8,128)(2,1)S(1)}, bf16[4,128,128]{2,1,0:T(8,128)(2,1)}, u32[]{:S(2)}) copy-start(bf16[4,128,128]{2,1,0:T(8,128)(2,1)} %get-tuple-element.49.own_ref) | copy-start | bytes 393220
  64.4 2.0 %copy-start.5 = (f32[3,2,8,128]{3,2,1,0:T(8,128)S(1)}, f32[3,2,8,128]{3,2,1,0:T(8,128)}, u32[]{:S(2)}) copy-start(f32[3,2,8,128]{3,2,1,0:T(8,128)} %get-tuple-element.50.parts_ref) | copy-start | bytes 73732
  64.4 5.1 %collective-permute-start.10 = (f32[144,128]{1,0:T(8,128)S(1)}, f32[144,128]{1,0:T(8,128)S(1)}, u32[]{:S(2)}, u32[]{:S(2)}) collective-permute-start(f32[144,128]{1,0:T(8,128)S(1)} %add.33), channel_id=1, source_target_pairs={{0,6},{1,7},{2,12},{3,13},{4,10},{5,11},{6,0},{7,1},{8,14},{9,15},... | collective-permute-start | bytes 221192 | tf_op jit(solution)/shard_map/ppermute | solution.py:720
  69.5 5.6 %collective-permute-start.11 = (f32[144,128]{1,0:T(8,128)S(1)}, f32[144,128]{1,0:T(8,128)S(1)}, u32[]{:S(2)}, u32[]{:S(2)}) collective-permute-start(f32[144,128]{1,0:T(8,128)S(1)} %add.34.mine_ref), channel_id=1, source_target_pairs={{0,1},{1,0},{2,3},{3,2},{4,5},{5,4},{6,7},{7,6},{8,9},{9,8},{10,11... | collective-permute-start | bytes 221192 | tf_op jit(solution)/shard_map/ppermute | solution.py:720
